TPU v7x, 512 devices: a whole 4x4x16 slice. The times are simulated.
512 devices in a mesh: vec: 4 (over y_lo, core), row: 8 (over x, y_hi), col: 16 (over z).
Axes of the slice: x: 4, y: 4 (y_hi: 2, y_lo: 2; y = y_hi * 2 + y_lo), z: 16, core: 2. Of those that a mesh axis runs over, the one named last changes fastest.
Arguments:
- checkpoints: float32 [2, 2, 16, 256, 2048], P(None, None, 'vec', 'row', 'col'), may hold values from -6 to 6
- adjoints_in: float32 [2, 16, 256, 2048], P(None, 'vec', 'row', 'col'), may hold values from -4 to 4
- vector_bits: int32 [16, 256, 2048], P('vec', 'row', 'col'), may hold values 0 or 1
- potential_int: int32 [256, 2048], P('row', 'col'), may hold values from -32767 to 32767
- pot_scale: float32 [1], replicated, may hold values from 1.5e-05 to 9e-05
- energies: float32 [16], replicated, may hold values from -0.9 to 0.9
- residual: float32 [16, 256, 2048], P(None, 'row', 'col'), may hold values from -6 to 6
- first_segment: int32 [1], replicated, may hold values from 0 to 62
Outputs:
- potential_grad: float32 [256, 2048], P('row', 'col')
- adjoint_out: float32 [2, 16, 256, 2048], P(None, 'vec', 'row', 'col')
All inputs are finite; a program needn't handle non-finite values. No bound on the sum of `vector_bits` on one device may be relied on, other than what follows from the above.
Results may differ from a plain program's by a relative error of at most 0.0003.
Values sent between devices are 32-bit elements; how exact they have to be, the bound alone decides.
No kernel may reach another device: no remote copies, remote signals or barrier semaphores. Data moves between devices by JAX's collectives and lax.ppermute only.
A program may use at most 64 MiB of HBM per device.

v0:
```python
import math

import jax
import jax.numpy as jnp
from jax import lax
from jax.sharding import PartitionSpec as P

SEG = 16
MOMENTS = 1024
QMAX = 32767


def extended_2(value, sides, width):
    for axis, dim in sides:
        devices, length = (lax.axis_size(axis), value.shape[dim])
        up = [(i, (i + 1) % devices) for i in range(devices)]
        down = [(j, i) for i, j in up]
        last = lax.slice_in_dim(value, length - width, length, axis=dim)
        initial = lax.slice_in_dim(value, 0, width, axis=dim)
        before = lax.ppermute(last, axis, up)
        after = lax.ppermute(initial, axis, down)
        value = jnp.concatenate([before, value, after], axis=dim)
    return value


def window_coefs(first_segment, energies):
    moment_order = first_segment[0] * SEG + jnp.arange(2 * SEG, dtype=jnp.int32)
    degree = moment_order.astype(jnp.float32)
    kernel_norm = float(MOMENTS + 1)
    angle_step = math.pi / kernel_norm
    jackson = (
        (kernel_norm - degree) * jnp.cos(angle_step * degree)
        + jnp.sin(angle_step * degree) * (math.cos(angle_step) / math.sin(angle_step))
    ) / kernel_norm
    factor = jnp.where(moment_order == 0, 1.0, 2.0).astype(jnp.float32)
    angles = jnp.arccos(energies)
    cosines = jnp.cos(degree[:, None] * angles[None, :])
    return (jackson * factor)[:, None] * cosines / (math.pi * jnp.sin(angles))[None, :]


def stencil(extended, onsite, inv_span):
    middle = extended[..., 1:-1, 1:-1]
    beside = (
        extended[..., 2:, 1:-1]
        + extended[..., :-2, 1:-1]
        + extended[..., 1:-1, 2:]
        + extended[..., 1:-1, :-2]
    )
    return inv_span * (onsite * middle - beside)


def per_device(
    checkpoints,
    adjoints_in,
    vector_bits,
    potential_int,
    pot_scale,
    energies,
    residual,
    first_segment,
):
    pot_factor = pot_scale[0]
    inv_span = 1.0 / (4.5 + QMAX * pot_factor)
    onsite = potential_int.astype(jnp.float32) * pot_factor
    coefficients = window_coefs(first_segment, energies)
    vector_count = lax.axis_size("vec") * vector_bits.shape[0]
    inv_count = 1.0 / vector_count
    sign_weights = (2 * vector_bits - 1).astype(jnp.float32) * inv_count
    earlier = checkpoints[:, 0]
    current = checkpoints[:, 1]
    zero_grad = jnp.zeros(onsite.shape, jnp.float32)
    carried = (adjoints_in[0], adjoints_in[1], zero_grad)
    weights = jnp.einsum("ne,eij->nij", coefficients, residual, precision=lax.Precision.HIGHEST)

    def forward_step(pair_state, unused):
        before, now = pair_state
        padded = extended_2(now, (("row", 2), ("col", 3)), 1)
        advanced = 2.0 * stencil(padded, onsite, inv_span) - before
        return ((now, advanced), advanced)

    _, generated = lax.scan(forward_step, (earlier, current), None, length=SEG - 2)
    states = jnp.concatenate([earlier[None], current[None], generated], axis=0)

    def adjoint_step(step_carry, inputs):
        after_one, after_two, accum_grad = step_carry
        state_now, weight_now = inputs
        padded = extended_2(after_one, (("row", 1), ("col", 2)), 1)
        accum_grad = accum_grad + jnp.sum(after_one * state_now, axis=0)
        advanced = weight_now * sign_weights + 2.0 * stencil(padded, onsite, inv_span) - after_two
        return ((advanced, after_one, accum_grad), None)

    for segment in (1, 0):
        carried, _ = lax.scan(
            adjoint_step,
            carried,
            (states[:, segment], weights[segment * SEG : (segment + 1) * SEG]),
            reverse=True,
        )
    adjoint_zero, adjoint_first, accum_grad = carried
    gradient = lax.psum(accum_grad, "vec") * (2.0 * inv_span)
    return (gradient, jnp.stack([adjoint_zero, adjoint_first]))


def solution(mesh):
    return jax.shard_map(
        per_device,
        mesh=mesh,
        in_specs=(
            P(None, None, "vec", "row", "col"),
            P(None, "vec", "row", "col"),
            P("vec", "row", "col"),
            P("row", "col"),
            P(),
            P(),
            P(None, "row", "col"),
            P(),
        ),
        out_specs=(P("row", "col"), P(None, "vec", "row", "col")),
        check_vma=False,
    )
```

profile of v0, /device:TPU:1, one launch (start us, length us, event | category | flops | bytes accessed | tf_op | source)
XLA Modules:
  0.0 1037.0 jit_solution(17202050149933971582)
XLA Ops:
  3.1 292.1 %while.51 = (s32[]{:T(128)}, f32[2,4,32,128]{3,2,1,0:T(8,128)S(1)}, f32[2,4,32,128]{3,2,1,0:T(8,128)S(1)}, f32[14,2,4,32,128]{4,3,2,0,1:T(8,128)S(1)}, f32[]{:T(128)}, /*index=5*/f32[32,128]{1,0:T(8,128)S(1)}, s32[]{:T(128)}) while((s32[]{:T(128)}, f32[2,4,32,128]{3,2,1,0:T(8,128)S(1)}, f32[2,4,32,128]{3,2,1,0:T(8,128)S(1)}, ...), condition=%wide.region_1.2_spmd, body=%wide.region_0.1_spmd.sunk | while | flops 593922 | bytes 1741821 | solution.py:81
  3.1 7.8 collective-permute-start
  12.9 6.0 collective-permute-done.1
  22.7 9.5 collective-permute-start.3
  36.6 4.9 collective-permute-start.1
  46.6 5.0 collective-permute-start.3
  66.1 5.0 collective-permute-start.3
  75.6 4.9 collective-permute-start.1
  85.6 5.0 collective-permute-start.3
  95.1 4.9 collective-permute-start.1
  115.3 4.9 collective-permute-start.1
  219.0 4.9 collective-permute-start.1
  238.8 4.9 collective-permute-start.1
  257.9 4.9 collective-permute-start.1
  277.5 4.9 collective-permute-start.1
  297.4 303.5 %while.53 = (s32[]{:T(128)}, f32[4,32,128]{2,1,0:T(8,128)S(1)}, f32[4,32,128]{2,1,0:T(8,128)S(1)}, f32[32,128]{1,0:T(8,128)S(1)}, f32[16,32,128]{2,0,1:T(8,128)S...) while((s32[]{:T(128)}, f32[4,32,128]{2,1,0:T(8,128)S(1)}, ...), condition=%wide.region_4.5_spmd.clone, body=%wide.region_2.4_spmd.clone.sunk | while | flops 366596 | bytes 962295 | solution.py:93
  357.6 4.9 collective-permute-start.9
  376.4 4.9 collective-permute-start.9
  395.0 4.9 collective-permute-start.9
  432.4 4.9 collective-permute-start.9
  451.2 4.9 collective-permute-start.9
  509.5 4.9 collective-permute-start.9
  546.4 4.9 collective-permute-start.9
  565.4 4.9 collective-permute-start.9
  601.0 303.3 %while.52 = (s32[]{:T(128)}, f32[4,32,128]{2,1,0:T(8,128)S(1)}, f32[4,32,128]{2,1,0:T(8,128)S(1)}, f32[32,128]{1,0:T(8,128)S(1)}, f32[16,32,128]{2,0,1:T(8,128)S...) while((s32[]{:T(128)}, f32[4,32,128]{2,1,0:T(8,128)S(1)}, ...), condition=%wide.region_7.8_spmd, body=%wide.region_5.7_spmd.sunk | while | flops 362499 | bytes 962277 | solution.py:93
  680.5 4.9 collective-permute-start.5
  698.6 4.9 collective-permute-start.5
  717.3 4.9 collective-permute-start.5
  735.7 4.9 collective-permute-start.5
  812.5 4.9 collective-permute-start.5
  850.3 4.9 collective-permute-start.5
  905.0 131.4 %psum.7 = f32[32,128]{1,0:T(8,128)S(1)} all-reduce(f32[32,128]{1,0:T(8,128)S(1)} %get-tuple-element.400), channel_id=1, replica_groups=mesh['vec'=4,'row'=8,'col'=16] {'vec'}, use_global_device_ids=true, to_apply=%region_8.9 | all-reduce | flops 4096 | bytes 32768 | tf_op jit(solution)/shard_map/psum | solution.py:100
  (735 shorter events, 752.6 us)
Async XLA Ops:
  3.1 9.8 collective-permute-start
  11.0 8.0 collective-permute-start.1
  19.1 13.8 %collective-permute-start.2 = (f32[2,4,34,1]{3,2,1,0:T(8,128)S(1)}, f32[2,4,34,1]{3,2,1,0:T(8,128)S(1)}, u32[]{:S(2)}, u32[]{:S(2)}) collective-permute-start(f32[2,4,34,1]{3,2,1,0:T(8,128)S(1)} %get-tuple-element.670), channel_id=1, source_target_pairs={{0,1},{1,2},{2,3},{3,4},{4,5},{5,6},{6,7},{7,8},{8,9},{9,10},{10,1... | collective-permute-start | bytes 3272 | tf_op jit(solution)/shard_map/while/body/eval_jaxpr/ppermute | solution.py:20
  22.7 11.7 %collective-permute-start.3 = (f32[2,4,34,1]{3,2,1,0:T(8,128)S(1)}, f32[2,4,34,1]{3,2,1,0:T(8,128)S(1)}, u32[]{:S(2)}, u32[]{:S(2)}) collective-permute-start(f32[2,4,34,1]{3,2,1,0:T(8,128)S(1)} %get-tuple-element.671), channel_id=1, source_target_pairs={{1,0},{2,1},{3,2},{4,3},{5,4},{6,5},{7,6},{8,7},{9,8},{10,9},{11,1... | collective-permute-start | bytes 3272 | tf_op jit(solution)/shard_map/while/body/eval_jaxpr/ppermute | solution.py:21
  36.6 8.0 collective-permute-start.1
  56.1 8.0 collective-permute-start.1
  75.6 8.0 collective-permute-start.1
  83.7 8.0 collective-permute-start.2
  95.1 8.0 collective-permute-start.1
  115.3 8.0 collective-permute-start.1
  136.3 8.0 collective-permute-start.1
  156.5 8.0 collective-permute-start.1
  178.1 8.0 collective-permute-start.1
  186.2 9.3 collective-permute-start.2
  199.2 8.0 collective-permute-start.1
  219.0 8.0 collective-permute-start.1
  238.8 8.0 collective-permute-start.1
  257.9 8.0 collective-permute-start.1
  277.5 8.0 collective-permute-start.1
  318.7 7.9 collective-permute-start.9
  338.5 7.9 collective-permute-start.9
  357.6 7.9 collective-permute-start.9
  376.4 8.0 collective-permute-start.9
  395.0 7.9 collective-permute-start.9
  413.8 7.9 collective-permute-start.9
  432.4 7.9 collective-permute-start.9
  451.2 7.9 collective-permute-start.9
  470.1 7.9 collective-permute-start.9
  489.7 7.9 collective-permute-start.9
  509.5 7.9 collective-permute-start.9
  527.8 7.9 collective-permute-start.9
  546.4 7.9 collective-permute-start.9
  (156 other events, 1316.7 us)
where the time goes:
time: 1040 us
  starting transfers between devices  629 us (60%)
  waiting for transfers between devices  250 us (24%)
  blocking collectives  131 us (13%)
  other arithmetic  10.7 us (1%)
    ppermute x92, starting transfers between devices, extended_2(): before = lax.ppermute(last, axis, up)  351 us
    ppermute x92, starting transfers between devices, extended_2(): after = lax.ppermute(initial, axis, down)  278 us
    ppermute x92, waiting for transfers between devices, extended_2(): before = lax.ppermute(last, axis, up)  169 us
    psum x1, blocking collectives, per_device(): gradient = lax.psum(accum_grad, 'vec') * (2.0 * inv_span)  131 us
    ppermute x92, waiting for transfers between devices, extended_2(): after = lax.ppermute(initial, axis, down)  81.1 us
  transfers between devices with their start and end apart: 184, of which 112 were waited for; matrix products, arithmetic and copies ran while one was open for 0% of the time, Pallas kernels for 0%

commit v1 on v0

v1 whole, which is shorter than its diff:
```python
import functools
import math

import jax
import jax.numpy as jnp
from jax import lax
from jax.experimental import pallas as pl
from jax.experimental.pallas import tpu as pltpu
from jax.sharding import PartitionSpec as P

SEG = 16
MOMENTS = 1024
QMAX = 32767
TERMS = 2 * SEG

ADJ, SGN, RES, ONS = 0, 8, 12, 28
PLANES = 29
ROWS = 32
HALO = 32
EXT = ROWS + 2 * HALO
FHALO = 16
FEXT = ROWS + 2 * FHALO
LANES = 128
FPLANES = 16
MAIN = PLANES * ROWS
G_ADJ = 7 * EXT
G_ONS = EXT // 4
G_ROWS = G_ADJ + G_ONS + 2 * FEXT


def window_coefs(first_segment, energies):
    moment_order = first_segment[0] * SEG + jnp.arange(TERMS, dtype=jnp.int32)
    degree = moment_order.astype(jnp.float32)
    kernel_norm = float(MOMENTS + 1)
    angle_step = math.pi / kernel_norm
    jackson = (
        (kernel_norm - degree) * jnp.cos(angle_step * degree)
        + jnp.sin(angle_step * degree) * (math.cos(angle_step) / math.sin(angle_step))
    ) / kernel_norm
    factor = jnp.where(moment_order == 0, 1.0, 2.0).astype(jnp.float32)
    angles = jnp.arccos(energies)
    cosines = jnp.cos(degree[:, None] * angles[None, :])
    return (jackson * factor)[:, None] * cosines / (math.pi * jnp.sin(angles))[None, :]


def lane_iota():
    return lax.broadcasted_iota(jnp.int32, (8, LANES), 1)


def sub_iota():
    return lax.broadcasted_iota(jnp.int32, (8, LANES), 0)


def tile(ref, row):
    return ref[pl.ds(row, 8), :]


def main_tile(own, above, below, plane, t):
    section = (above, own, below)[t // 4]
    return tile(section, plane * ROWS + (t % 4) * 8)


def fwd_tile(chk, above, below, plane, t):
    if t < 2:
        return tile(above, MAIN + plane * FHALO + t * 8)
    if t < 6:
        return tile(chk, plane * ROWS + (t - 2) * 8)
    return tile(below, MAIN + plane * FHALO + (t - 6) * 8)


def pack_kernel(own, chk, above, below, to_left, to_right):
    lane = lane_iota()

    def pack(tiles, row):
        count = len(tiles)
        width = LANES // count
        group = lane // width
        left = right = None
        for j, value in enumerate(tiles):
            rolled = pltpu.roll(value, width * j, 1) if j else value
            left = rolled if j == 0 else jnp.where(group == j, rolled, left)
            right = rolled if j == 0 else jnp.where(group == (j + count - 1) % count, rolled, right)
        to_left[pl.ds(row, 8), :] = left
        to_right[pl.ds(row, 8), :] = right

    for g in range(7):
        for t in range(EXT // 8):
            pack([main_tile(own, above, below, 4 * g + j, t) for j in range(4)], g * EXT + t * 8)
    for m in range(3):
        pack([main_tile(own, above, below, ONS, 3 * j + m) for j in range(4)], G_ADJ + m * 8)
    for g in range(2):
        for t in range(FEXT // 8):
            pack(
                [fwd_tile(chk, above, below, 8 * g + j, t) for j in range(8)],
                G_ADJ + G_ONS + g * FEXT + t * 8,
            )


def main_kernel(
    coef, scale, own, chk, above, below, from_right, from_left,
    adj_out, grad_out,
    xc, xh, sgc, sgh, rsc, rsh, onc, onh, fc, fh, vs,
):
    lane = lane_iota()
    sub = sub_iota()
    first_lane, last_lane = lane == 0, lane == LANES - 1
    first_sub, last_sub = sub == 0, sub == 7
    s = scale[0]

    def strip(row, j, count):
        width = LANES // count
        mixed = jnp.where(lane // width == j, tile(from_right, row), tile(from_left, row))
        return pltpu.roll(mixed, (LANES - width * j) % LANES, 1) if j else mixed

    for t in range(EXT // 8):
        for plane in range(8):
            xc[plane, pl.ds(t * 8, 8), :] = main_tile(own, above, below, plane, t)
            xh[plane, pl.ds(t * 8, 8), :] = strip((plane // 4) * EXT + t * 8, plane % 4, 4)
        for v in range(4):
            sgc[v, pl.ds(t * 8, 8), :] = main_tile(own, above, below, SGN + v, t)
            sgh[v, pl.ds(t * 8, 8), :] = strip(2 * EXT + t * 8, v, 4)
        for e in range(16):
            rsc[e, pl.ds(t * 8, 8), :] = main_tile(own, above, below, RES + e, t)
            rsh[e, pl.ds(t * 8, 8), :] = strip((3 + e // 4) * EXT + t * 8, e % 4, 4)
        onc[pl.ds(t * 8, 8), :] = main_tile(own, above, below, ONS, t) * s
        onh[pl.ds(t * 8, 8), :] = strip(G_ADJ + (t % 3) * 8, t // 3, 4) * s
    for t in range(FEXT // 8):
        for plane in range(FPLANES):
            fc[plane, pl.ds(t * 8, 8), :] = fwd_tile(chk, above, below, plane, t)
            fh[plane, pl.ds(t * 8, 8), :] = strip(
                G_ADJ + G_ONS + (plane // 8) * FEXT + t * 8, plane % 8, 8
            )
    for segment in range(2):
        for which in range(2):
            for v in range(4):
                for i in range(4):
                    vs[segment * SEG + which, v, pl.ds(i * 8, 8), :] = tile(
                        chk, (segment * 8 + which * 4 + v) * ROWS + i * 8
                    )

    def neighbours(cref, href, plane, lo, hi, count):
        def load(t):
            c, h = cref[plane, pl.ds(t * 8, 8), :], href[plane, pl.ds(t * 8, 8), :]
            return c, h

        def rolled(pair, shift):
            return tuple(pltpu.roll(p, shift, 0) for p in pair)

        here = load(lo)
        prev_up = rolled(load(lo - 1) if lo > 0 else here, 1)
        here_up = rolled(here, 1)
        here_down = rolled(here, 7)
        for t in range(lo, hi):
            after = load(t + 1) if t + 1 < count else here
            after_up, after_down = rolled(after, 1), rolled(after, 7)
            c, h = here
            cl, cr = pltpu.roll(c, 1, 1), pltpu.roll(c, LANES - 1, 1)
            hl, hr = pltpu.roll(h, 1, 1), pltpu.roll(h, LANES - 1, 1)
            side_c = jnp.where(first_lane, hl, cl) + jnp.where(last_lane, hr, cr)
            side_h = jnp.where(first_lane, cl, hl) + jnp.where(last_lane, cr, hr)
            vert = [
                jnp.where(first_sub, prev_up[k], here_up[k])
                + jnp.where(last_sub, after_down[k], here_down[k])
                for k in range(2)
            ]
            yield t, c, h, side_c + vert[0], side_h + vert[1]
            here, prev_up, here_up, here_down = after, here_up, after_up, after_down

    def forward(k, new, old, lo, hi):
        for segment in range(2):
            for v in range(4):
                p_new = segment * 8 + new * 4 + v
                p_old = segment * 8 + old * 4 + v
                for t, c, h, nc, nh in neighbours(fc, fh, p_new, lo, hi, FEXT // 8):
                    row = pl.ds(t * 8, 8)
                    on = pl.ds(t * 8 + HALO - FHALO, 8)
                    out_c = onc[on, :] * c - s * nc - fc[p_old, row, :]
                    out_h = onh[on, :] * h - s * nh - fh[p_old, row, :]
                    fc[p_old, row, :] = out_c
                    fh[p_old, row, :] = out_h
                    if 2 <= t < 6:
                        vs[segment * SEG + k, v, pl.ds((t - 2) * 8, 8), :] = out_c

    for start, stop, lo, hi in ((1, 4, 0, 8), (4, 8, 1, 7)):
        def body(i, carry, lo=lo, hi=hi):
            forward(2 * i, 1, 0, lo, hi)
            forward(2 * i + 1, 0, 1, lo, hi)
            return carry
        lax.fori_loop(start, stop, body, 0)

    def adjoint(t_term, new, old, lo, hi, grads):
        grads = list(grads)
        weights = {}
        for t in range(lo, hi):
            wc = wh = None
            row = pl.ds(t * 8, 8)
            for e in range(16):
                q = coef[t_term, e]
                pc, phh = rsc[e, row, :] * q, rsh[e, row, :] * q
                wc, wh = (pc, phh) if wc is None else (wc + pc, wh + phh)
            wcr[row, :] = wc
            whr[row, :] = wh
        for v in range(4):
            p_new, p_old = new * 4 + v, old * 4 + v
            for t, c, h, nc, nh in neighbours(xc, xh, p_new, lo, hi, EXT // 8):
                row = pl.ds(t * 8, 8)
                if 4 <= t < 8:
                    grads[t - 4] = grads[t - 4] + c * vs[t_term, v, pl.ds((t - 4) * 8, 8), :]
                xc[p_old, row, :] = wcr[row, :] * sgc[v, row, :] + (onc[row, :] * c - s * nc) - xc[p_old, row, :]
                xh[p_old, row, :] = whr[row, :] * sgh[v, row, :] + (onh[row, :] * h - s * nh) - xh[p_old, row, :]
        return tuple(grads)

    def run(wc_ref, wh_ref):
        nonlocal wcr, whr
        wcr, whr = wc_ref, wh_ref
        grads = tuple(jnp.zeros((8, LANES), jnp.float32) for _ in range(4))
        for phase in range(4):
            def body(i, carry, phase=phase):
                t_term = TERMS - 1 - 8 * phase - 2 * i
                carry = adjoint(t_term, 0, 1, phase, EXT // 8 - phase, carry)
                return adjoint(t_term - 1, 1, 0, phase, EXT // 8 - phase, carry)
            grads = lax.fori_loop(0, 4, body, grads)
        for i in range(4):
            grad_out[pl.ds(i * 8, 8), :] = grads[i] * s

    wcr = whr = None
    pl.run_scoped(run, pltpu.VMEM((EXT, LANES), jnp.float32), pltpu.VMEM((EXT, LANES), jnp.float32))
    for which in range(2):
        for v in range(4):
            for i in range(4):
                adj_out[which, v, pl.ds(i * 8, 8), :] = xc[which * 4 + v, pl.ds(HALO + i * 8, 8), :]


VMEM_SPEC = pl.BlockSpec(memory_space=pltpu.VMEM)
SMEM_SPEC = pl.BlockSpec(memory_space=pltpu.SMEM)
F32 = jnp.float32


def per_device(
    checkpoints,
    adjoints_in,
    vector_bits,
    potential_int,
    pot_scale,
    energies,
    residual,
    first_segment,
):
    pot_factor = pot_scale[0]
    inv_span = 1.0 / (4.5 + QMAX * pot_factor)
    onsite = potential_int.astype(F32) * pot_factor
    coefs = window_coefs(first_segment, energies)
    vector_count = lax.axis_size("vec") * vector_bits.shape[0]
    signs = (2 * vector_bits - 1).astype(F32) * (1.0 / vector_count)

    own = jnp.concatenate(
        [adjoints_in.reshape(8, ROWS, LANES), signs, residual, onsite[None]], axis=0
    ).reshape(MAIN, LANES)
    chk = checkpoints.reshape(FPLANES, ROWS, LANES)
    to_below = jnp.concatenate([own, chk[:, ROWS - FHALO :].reshape(-1, LANES)], axis=0)
    to_above = jnp.concatenate([own, chk[:, :FHALO].reshape(-1, LANES)], axis=0)
    chk = chk.reshape(FPLANES * ROWS, LANES)

    def shift(value, axis, step):
        n = lax.axis_size(axis)
        return lax.ppermute(value, axis, [(i, (i + step) % n) for i in range(n)])

    above = shift(to_below, "row", 1)
    below = shift(to_above, "row", -1)

    strips = jax.ShapeDtypeStruct((G_ROWS, LANES), F32)
    to_left, to_right = pl.pallas_call(
        pack_kernel,
        out_shape=(strips, strips),
        in_specs=[VMEM_SPEC] * 4,
        out_specs=(VMEM_SPEC, VMEM_SPEC),
        name="pack_columns",
    )(own, chk, above, below)
    from_left = shift(to_right, "col", 1)
    from_right = shift(to_left, "col", -1)

    ext = (EXT, LANES)
    adjoint_out, grad = pl.pallas_call(
        main_kernel,
        out_shape=(
            jax.ShapeDtypeStruct((2, 4, ROWS, LANES), F32),
            jax.ShapeDtypeStruct((ROWS, LANES), F32),
        ),
        in_specs=[SMEM_SPEC, SMEM_SPEC] + [VMEM_SPEC] * 6,
        out_specs=(VMEM_SPEC, VMEM_SPEC),
        scratch_shapes=[
            pltpu.VMEM((8, *ext), F32), pltpu.VMEM((8, *ext), F32),
            pltpu.VMEM((4, *ext), F32), pltpu.VMEM((4, *ext), F32),
            pltpu.VMEM((16, *ext), F32), pltpu.VMEM((16, *ext), F32),
            pltpu.VMEM(ext, F32), pltpu.VMEM(ext, F32),
            pltpu.VMEM((FPLANES, FEXT, LANES), F32), pltpu.VMEM((FPLANES, FEXT, LANES), F32),
            pltpu.VMEM((TERMS, 4, ROWS, LANES), F32),
        ],
        compiler_params=pltpu.CompilerParams(vmem_limit_bytes=40 * 1024 * 1024),
        name="window",
    )(coefs, (2.0 * inv_span)[None], own, chk, above, below, from_right, from_left)

    grad = grad + lax.ppermute(grad, "vec", [(0, 1), (1, 0), (2, 3), (3, 2)])
    grad = grad + lax.ppermute(grad, "vec", [(0, 2), (2, 0), (1, 3), (3, 1)])
    return grad, adjoint_out


def solution(mesh):
    return jax.shard_map(
        per_device,
        mesh=mesh,
        in_specs=(
            P(None, None, "vec", "row", "col"),
            P(None, "vec", "row", "col"),
            P("vec", "row", "col"),
            P("row", "col"),
            P(),
            P(),
            P(None, "row", "col"),
            P(),
        ),
        out_specs=(P("row", "col"), P(None, "vec", "row", "col")),
        check_vma=False,
    )
```

time: 1040 us -> 94.5 us (0.09)
  starting transfers between devices: 629 us -> 29.6 us
  waiting for transfers between devices: 250 us -> 38.2 us
  blocking collectives: 131 us -> 0 us
  Pallas kernels: 0 us -> 17.5 us
    ppermute x184 -> x6, starting transfers between devices: 629 us -> 29.6 us  [the longest x4 22.9 us: shift(): return lax.ppermute(value, axis, [(i, (i + step) % n) for i in range(n)])]
    ppermute x184 -> x6, waiting for transfers between devices: 250 us -> 38.2 us  [the longest x4 36.1 us: shift(): return lax.ppermute(value, axis, [(i, (i + step) % n) for i in range(n)])]
    psum x1 -> x0, blocking collectives: 131 us -> none  [per_device(): gradient = lax.psum(accum_grad, 'vec') * (2.0 * inv_span)]
    pallas_call x0 -> x2, Pallas kernels: none -> 17.5 us  [the longest x1 14.5 us: per_device(): pl.pallas_call(main_kernel, out_shape=(jax.ShapeDtypeStruct((2, 4, ROWS,...]
  transfers between devices with their start and end apart: 184 -> 6, of which waited for: 112 -> 6; matrix products, arithmetic and copies ran while one was open for 0% -> 0% of each run, Pallas kernels for 0% -> 0%
where the time goes in v1:
time: 94.5 us; the launch traced here: 94 us
  waiting for transfers between devices  38.2 us (40%)
  starting transfers between devices  29.6 us (31%)
  Pallas kernels  17.5 us (19%)
  local copies, waits for them, and re-layouts  4.76 us (5%)
  between operations  2.13 us (2%)
  other arithmetic  1.86 us (2%)
    ppermute x4, waiting for transfers between devices, shift(): return lax.ppermute(value, axis, [(i, (i + step) % n) for i in range(n)])  36.1 us
    ppermute x4, starting transfers between devices, shift(): return lax.ppermute(value, axis, [(i, (i + step) % n) for i in range(n)])  22.9 us
    pallas_call x1, Pallas kernels, per_device(): pl.pallas_call(main_kernel, out_shape=(jax.ShapeDtypeStruct((2, 4, ROWS,...  14.5 us
    unnamed x22, local copies, waits for them, and re-layouts  3.72 us
    ppermute x1, starting transfers between devices, per_device(): grad = grad + lax.ppermute(grad, 'vec', [(0, 1), (1, 0), (2, 3), (3, 2)])  3.56 us
    ppermute x1, starting transfers between devices, per_device(): grad = grad + lax.ppermute(grad, 'vec', [(0, 2), (2, 0), (1, 3), (3, 1)])  3.15 us
    pallas_call x1, Pallas kernels, per_device(): pl.pallas_call(pack_kernel, out_shape=(strips, strips), in_specs=[VMEM_SP...  2.95 us
  transfers between devices with their start and end apart: 6, of which 6 were waited for; matrix products, arithmetic and copies ran while one was open for 0% of the time, Pallas kernels for 0%

profile of v1, /device:TPU:1, one launch (start us, length us, event | category | flops | bytes accessed | tf_op | source)
XLA Modules:
  0.0 94.0 jit_solution(8296854259682188863)
XLA Ops:
  1.3 0.9 convert_multiply_fusion
  2.1 0.0 copy-start.9
  2.1 0.0 copy-start.7
  2.2 0.0 copy-start.8
  2.2 1.0 %fusion.2 = (f32[16,16,128]{2,1,0:T(8,128)S(1)}, f32[16,16,128]{2,1,0:T(8,128)S(1)}) fusion(f32[16,32,128]{2,1,0:T(8,128)} %bitcast.16), kind=kLoop, calls=%fused_computation.12 | loop fusion | bytes 524288 | tf_op jit(solution)/shard_map/slice | solution.py:261
  3.2 0.0 copy-done.9
  3.2 0.0 copy-done.7
  3.2 0.0 copy-done.8
  3.3 0.1 pad_maximum_fusion
  3.4 0.7 copy-done
  4.1 5.6 %collective-permute-start = (f32[1184,128]{1,0:T(8,128)S(1)}, f32[1184,128]{1,0:T(8,128)S(1)}, u32[]{:S(2)}, u32[]{:S(2)}) collective-permute-start(f32[1184,128]{1,0:T(8,128)S(1)} %get-tuple-element.13), channel_id=1, source_target_pairs={{0,16},{16,32},{32,48},{48,64},{64,80},{80,96},{96,112},{112,0},{1... | collective-permute-start | bytes 1818632 | tf_op jit(solution)/shard_map/ppermute | solution.py:266
  9.7 4.1 %collective-permute-start.1 = (f32[1184,128]{1,0:T(8,128)S(1)}, f32[1184,128]{1,0:T(8,128)S(1)}, u32[]{:S(2)}, u32[]{:S(2)}) collective-permute-start(f32[1184,128]{1,0:T(8,128)S(1)} %get-tuple-element.12), channel_id=1, source_target_pairs={{0,112},{16,0},{32,16},{48,32},{64,48},{80,64},{96,80},{112,96},{1... | collective-permute-start | bytes 1818632 | tf_op jit(solution)/shard_map/ppermute | solution.py:266
  14.5 0.1 fusion
  14.6 18.2 %collective-permute-done.above = f32[1184,128]{1,0:T(8,128)S(1)} collective-permute-done((f32[1184,128]{1,0:T(8,128)S(1)}, f32[1184,128]{1,0:T(8,128)S(1)}, u32[]{:S(2)}, u32[]{:S(2)}) %collective-permute-start) | collective-permute-done | bytes 606240 | tf_op jit(solution)/shard_map/ppermute | solution.py:266
  32.8 6.2 %collective-permute-done.1.below = f32[1184,128]{1,0:T(8,128)S(1)} collective-permute-done((f32[1184,128]{1,0:T(8,128)S(1)}, f32[1184,128]{1,0:T(8,128)S(1)}, u32[]{:S(2)}, u32[]{:S(2)}) %collective-permute-start.1) | collective-permute-done | bytes 606240 | tf_op jit(solution)/shard_map/ppermute | solution.py:266
  39.0 0.8 copy-done.4
  39.9 3.0 %pack_columns.1 = (f32[824,128]{1,0:T(8,128)}, f32[824,128]{1,0:T(8,128)}) custom-call(f32[928,128]{1,0:T(8,128)} %bitcast.14, f32[512,128]{1,0:T(8,128)} %bitcast.17, f32[1184,128]{1,0:T(8,128)} %copy-done.2, f32[1184,128]{1,0:T(8,128)} %copy-done.4), custom_call_target="tpu_custom_call" | custom-call | tf_op jit(solution)/shard_map/pack_columns/pallas_call | solution.py:272
  42.8 11.2 %collective-permute-start.2 = (f32[824,128]{1,0:T(8,128)}, f32[824,128]{1,0:T(8,128)S(1)}, u32[]{:S(2)}, u32[]{:S(2)}) collective-permute-start(f32[824,128]{1,0:T(8,128)} %get-tuple-element.6), channel_id=1, source_target_pairs={{0,15},{1,0},{2,1},{3,2},{4,3},{5,4},{6,5},{7,6},{8,7},{9,8},{10,9... | collective-permute-start | bytes 1265672 | tf_op jit(solution)/shard_map/ppermute | solution.py:266
  54.1 1.9 %collective-permute-start.3 = (f32[824,128]{1,0:T(8,128)}, f32[824,128]{1,0:T(8,128)S(1)}, u32[]{:S(2)}, u32[]{:S(2)}) collective-permute-start(f32[824,128]{1,0:T(8,128)} %get-tuple-element.7), channel_id=1, source_target_pairs={{0,1},{1,2},{2,3},{3,4},{4,5},{5,6},{6,7},{7,8},{8,9},{9,10},{10,1... | collective-permute-start | bytes 1265672 | tf_op jit(solution)/shard_map/ppermute | solution.py:266
  56.0 0.1 sine_multiply_fusion
  56.1 0.1 multiply_divide_fusion.coef
  56.3 6.7 %collective-permute-done.2.from_right = f32[824,128]{1,0:T(8,128)S(1)} collective-permute-done((f32[824,128]{1,0:T(8,128)}, f32[824,128]{1,0:T(8,128)S(1)}, u32[]{:S(2)}, u32[]{:S(2)}) %collective-permute-start.2) | collective-permute-done | bytes 421920 | tf_op jit(solution)/shard_map/ppermute | solution.py:266
  63.0 4.9 %collective-permute-done.3.from_left = f32[824,128]{1,0:T(8,128)S(1)} collective-permute-done((f32[824,128]{1,0:T(8,128)}, f32[824,128]{1,0:T(8,128)S(1)}, u32[]{:S(2)}, u32[]{:S(2)}) %collective-permute-start.3) | collective-permute-done | bytes 421920 | tf_op jit(solution)/shard_map/ppermute | solution.py:266
  67.9 0.0 copy-done.6
  67.9 1.1 %copy-done.3 = f32[1184,128]{1,0:T(8,128)S(1)} copy-done((f32[1184,128]{1,0:T(8,128)S(1)}, f32[1184,128]{1,0:T(8,128)}, u32[]{:S(2)}) %copy-start.3) | copy-done | bytes 606232
  69.0 1.1 %copy-done.5 = f32[1184,128]{1,0:T(8,128)S(1)} copy-done((f32[1184,128]{1,0:T(8,128)S(1)}, f32[1184,128]{1,0:T(8,128)}, u32[]{:S(2)}) %copy-start.5) | copy-done | bytes 606232
  70.0 14.5 %window.1 = (f32[2,4,32,128]{3,2,1,0:T(8,128)}, f32[32,128]{1,0:T(8,128)S(1)}) custom-call(f32[32,16]{1,0:T(8,128)S(1)} %multiply_divide_fusion.coef, f32[1]{0:T(128)} %bitcast.2.scale, f32[928,128]{1,0:T(8,128)S(1)} %bitcast.15, f32[512,128]{1,0:T(8,128)S(1)} %bitcast.18, f32[1184,128]{1,0:T(8,128)S(1)} %copy-done.3, f32[1184,128]{1,0:T(8,128)S(1)} %copy-done.5, ...), custom_call_target="tpu_custom_call" | custom-call | tf_op jit(solution)/shard_map/window/pallas_call | solution.py:283
  84.6 3.6 %collective-permute-start.4 = (f32[32,128]{1,0:T(8,128)S(1)}, f32[32,128]{1,0:T(8,128)S(1)}, u32[]{:S(2)}, u32[]{:S(2)}) collective-permute-start(f32[32,128]{1,0:T(8,128)S(1)} %get-tuple-element.8), channel_id=1, source_target_pairs={{0,128},{128,0},{256,384},{384,256},{1,129},{129,1},{257,385},{385... | collective-permute-start | bytes 49160 | tf_op jit(solution)/shard_map/ppermute | solution.py:303
  88.1 0.8 collective-permute-done.4
  89.0 3.2 %collective-permute-start.5 = (f32[32,128]{1,0:T(8,128)S(1)}, f32[32,128]{1,0:T(8,128)S(1)}, u32[]{:S(2)}, u32[]{:S(2)}) collective-permute-start(f32[32,128]{1,0:T(8,128)S(1)} %add.30), channel_id=1, source_target_pairs={{0,256},{256,0},{128,384},{384,128},{1,257},{257,1},{129,385},{385... | collective-permute-start | bytes 49160 | tf_op jit(solution)/shard_map/ppermute | solution.py:304
  92.1 1.3 %collective-permute-done.5 = f32[32,128]{1,0:T(8,128)S(1)} collective-permute-done((f32[32,128]{1,0:T(8,128)S(1)}, f32[32,128]{1,0:T(8,128)S(1)}, u32[]{:S(2)}, u32[]{:S(2)}) %collective-permute-start.5) | collective-permute-done | bytes 16416 | tf_op jit(solution)/shard_map/ppermute | solution.py:304
  93.4 0.6 add.31
  (15 shorter events, 0.1 us)
Async XLA Ops:
  2.1 1.1 %copy-start.9 = (s32[32,128]{1,0:T(8,128)S(1)}, s32[32,128]{1,0:T(8,128)}, u32[]{:S(2)}) copy-start(s32[32,128]{1,0:T(8,128)} %param.11) | copy-start | bytes 49156
  2.1 1.1 %copy-start.7 = (f32[16,32,128]{2,1,0:T(8,128)S(1)}, f32[16,32,128]{2,1,0:T(8,128)}, u32[]{:S(2)}) copy-start(f32[16,32,128]{2,1,0:T(8,128)} %param.14) | copy-start | bytes 786436
  2.2 1.1 %copy-start.8 = (f32[2,4,32,128]{3,2,1,0:T(8,128)S(1)}, f32[2,4,32,128]{3,2,1,0:T(8,128)}, u32[]{:S(2)}) copy-start(f32[2,4,32,128]{3,2,1,0:T(8,128)} %param.9) | copy-start | bytes 393220
  3.3 0.8 copy-start
  4.1 28.7 %collective-permute-start = (f32[1184,128]{1,0:T(8,128)S(1)}, f32[1184,128]{1,0:T(8,128)S(1)}, u32[]{:S(2)}, u32[]{:S(2)}) collective-permute-start(f32[1184,128]{1,0:T(8,128)S(1)} %get-tuple-element.13), channel_id=1, source_target_pairs={{0,16},{16,32},{32,48},{48,64},{64,80},{80,96},{96,112},{112,0},{1... | collective-permute-start | bytes 1818632 | tf_op jit(solution)/shard_map/ppermute | solution.py:266
  9.7 29.3 %collective-permute-start.1 = (f32[1184,128]{1,0:T(8,128)S(1)}, f32[1184,128]{1,0:T(8,128)S(1)}, u32[]{:S(2)}, u32[]{:S(2)}) collective-permute-start(f32[1184,128]{1,0:T(8,128)S(1)} %get-tuple-element.12), channel_id=1, source_target_pairs={{0,112},{16,0},{32,16},{48,32},{64,48},{80,64},{96,80},{112,96},{1... | collective-permute-start | bytes 1818632 | tf_op jit(solution)/shard_map/ppermute | solution.py:266
  32.8 6.2 %copy-start.2 = (f32[1184,128]{1,0:T(8,128)}, f32[1184,128]{1,0:T(8,128)S(1)}, u32[]{:S(2)}) copy-start(f32[1184,128]{1,0:T(8,128)S(1)} %collective-permute-done.above) | copy-start | bytes 1818628
  39.0 0.9 copy-start.4
  39.9 28.0 %copy-start.1 = (f32[29,32,128]{2,1,0:T(8,128)S(1)}, f32[29,32,128]{2,1,0:T(8,128)}, u32[]{:S(2)}) copy-start(f32[29,32,128]{2,1,0:T(8,128)} %copy-done) | copy-start | bytes 1425412
  39.9 28.0 %copy-start.6 = (f32[2,2,4,32,128]{4,3,2,1,0:T(8,128)S(1)}, f32[2,2,4,32,128]{4,3,2,1,0:T(8,128)}, u32[]{:S(2)}) copy-start(f32[2,2,4,32,128]{4,3,2,1,0:T(8,128)} %param.8) | copy-start | bytes 786436
  42.8 13.2 %copy-start.10 = (f32[16]{0:T(128)S(1)}, f32[16]{0:T(128)}, u32[]{:S(2)}) copy-start(f32[16]{0:T(128)} %param.13) | copy-start | bytes 196
  42.8 20.1 %collective-permute-start.2 = (f32[824,128]{1,0:T(8,128)}, f32[824,128]{1,0:T(8,128)S(1)}, u32[]{:S(2)}, u32[]{:S(2)}) collective-permute-start(f32[824,128]{1,0:T(8,128)} %get-tuple-element.6), channel_id=1, source_target_pairs={{0,15},{1,0},{2,1},{3,2},{4,3},{5,4},{6,5},{7,6},{8,7},{9,8},{10,9... | collective-permute-start | bytes 1265672 | tf_op jit(solution)/shard_map/ppermute | solution.py:266
  54.1 13.8 %collective-permute-start.3 = (f32[824,128]{1,0:T(8,128)}, f32[824,128]{1,0:T(8,128)S(1)}, u32[]{:S(2)}, u32[]{:S(2)}) collective-permute-start(f32[824,128]{1,0:T(8,128)} %get-tuple-element.7), channel_id=1, source_target_pairs={{0,1},{1,2},{2,3},{3,4},{4,5},{5,6},{6,7},{7,8},{8,9},{9,10},{10,1... | collective-permute-start | bytes 1265672 | tf_op jit(solution)/shard_map/ppermute | solution.py:266
  67.9 1.1 %copy-start.3 = (f32[1184,128]{1,0:T(8,128)S(1)}, f32[1184,128]{1,0:T(8,128)}, u32[]{:S(2)}) copy-start(f32[1184,128]{1,0:T(8,128)} %copy-done.2) | copy-start | bytes 1818628
  69.0 1.1 %copy-start.5 = (f32[1184,128]{1,0:T(8,128)S(1)}, f32[1184,128]{1,0:T(8,128)}, u32[]{:S(2)}) copy-start(f32[1184,128]{1,0:T(8,128)} %copy-done.4) | copy-start | bytes 1818628
  84.6 4.4 %collective-permute-start.4 = (f32[32,128]{1,0:T(8,128)S(1)}, f32[32,128]{1,0:T(8,128)S(1)}, u32[]{:S(2)}, u32[]{:S(2)}) collective-permute-start(f32[32,128]{1,0:T(8,128)S(1)} %get-tuple-element.8), channel_id=1, source_target_pairs={{0,128},{128,0},{256,384},{384,256},{1,129},{129,1},{257,385},{385... | collective-permute-start | bytes 49160 | tf_op jit(solution)/shard_map/ppermute | solution.py:303
  89.0 4.5 %collective-permute-start.5 = (f32[32,128]{1,0:T(8,128)S(1)}, f32[32,128]{1,0:T(8,128)S(1)}, u32[]{:S(2)}, u32[]{:S(2)}) collective-permute-start(f32[32,128]{1,0:T(8,128)S(1)} %add.30), channel_id=1, source_target_pairs={{0,256},{256,0},{128,384},{384,128},{1,257},{257,1},{129,385},{385... | collective-permute-start | bytes 49160 | tf_op jit(solution)/shard_map/ppermute | solution.py:304

commit v2 on v1

--- a/solution.py
+++ b/solution.py
@@ -12,6 +12,8 @@
 MOMENTS = 1024
 QMAX = 32767
 TERMS = 2 * SEG
+NVEC = 16
+F32 = jnp.float32
 
 ADJ, SGN, RES, ONS = 0, 8, 12, 28
 PLANES = 29
@@ -68,6 +70,35 @@
     return tile(below, MAIN + plane * FHALO + (t - 6) * 8)
 
 
+def prepare_kernel(factor, adj, bits, pot, res, chk, to_below, to_above, bits_v, pot_v, sems):
+    copies = []
+
+    def start(src, dst):
+        copy = pltpu.make_async_copy(src, dst, sems.at[len(copies)])
+        copy.start()
+        copies.append(copy)
+
+    start(bits, bits_v)
+    start(pot, pot_v)
+    for out, first in ((to_below, ROWS - FHALO), (to_above, 0)):
+        start(adj, out.at[pl.ds(ADJ * ROWS, 8 * ROWS)])
+        start(res, out.at[pl.ds(RES * ROWS, 16 * ROWS)])
+        for plane in range(FPLANES):
+            start(
+                chk.at[pl.ds(plane * ROWS + first, FHALO)],
+                out.at[pl.ds(MAIN + plane * FHALO, FHALO)],
+            )
+    copies[0].wait()
+    signs = (2 * bits_v[...] - 1).astype(F32) * (1.0 / NVEC)
+    copies[1].wait()
+    onsite = pot_v[...].astype(F32) * factor[0]
+    for out in (to_below, to_above):
+        out[pl.ds(SGN * ROWS, 4 * ROWS), :] = signs
+        out[pl.ds(ONS * ROWS, ROWS), :] = onsite
+    for copy in copies[2:]:
+        copy.wait()
+
+
 def pack_kernel(own, chk, above, below, to_left, to_right):
     lane = lane_iota()
 
@@ -122,8 +153,8 @@
         for e in range(16):
             rsc[e, pl.ds(t * 8, 8), :] = main_tile(own, above, below, RES + e, t)
             rsh[e, pl.ds(t * 8, 8), :] = strip((3 + e // 4) * EXT + t * 8, e % 4, 4)
-        onc[pl.ds(t * 8, 8), :] = main_tile(own, above, below, ONS, t) * s
-        onh[pl.ds(t * 8, 8), :] = strip(G_ADJ + (t % 3) * 8, t // 3, 4) * s
+        onc[pl.ds(t * 8, 8), :] = main_tile(own, above, below, ONS, t)
+        onh[pl.ds(t * 8, 8), :] = strip(G_ADJ + (t % 3) * 8, t // 3, 4)
     for t in range(FEXT // 8):
         for plane in range(FPLANES):
             fc[plane, pl.ds(t * 8, 8), :] = fwd_tile(chk, above, below, plane, t)
@@ -233,7 +264,7 @@
 
 VMEM_SPEC = pl.BlockSpec(memory_space=pltpu.VMEM)
 SMEM_SPEC = pl.BlockSpec(memory_space=pltpu.SMEM)
-F32 = jnp.float32
+HBM_SPEC = pl.BlockSpec(memory_space=pltpu.HBM)
 
 
 def per_device(
@@ -248,24 +279,40 @@
 ):
     pot_factor = pot_scale[0]
     inv_span = 1.0 / (4.5 + QMAX * pot_factor)
-    onsite = potential_int.astype(F32) * pot_factor
     coefs = window_coefs(first_segment, energies)
-    vector_count = lax.axis_size("vec") * vector_bits.shape[0]
-    signs = (2 * vector_bits - 1).astype(F32) * (1.0 / vector_count)
-
-    own = jnp.concatenate(
-        [adjoints_in.reshape(8, ROWS, LANES), signs, residual, onsite[None]], axis=0
-    ).reshape(MAIN, LANES)
-    chk = checkpoints.reshape(FPLANES, ROWS, LANES)
-    to_below = jnp.concatenate([own, chk[:, ROWS - FHALO :].reshape(-1, LANES)], axis=0)
-    to_above = jnp.concatenate([own, chk[:, :FHALO].reshape(-1, LANES)], axis=0)
-    chk = chk.reshape(FPLANES * ROWS, LANES)
+    chk = checkpoints.reshape(FPLANES * ROWS, LANES)
+    send = jax.ShapeDtypeStruct((MAIN + FPLANES * FHALO, LANES), F32)
+    own, to_above = pl.pallas_call(
+        prepare_kernel,
+        out_shape=(send, send),
+        in_specs=[SMEM_SPEC] + [HBM_SPEC] * 5,
+        out_specs=(VMEM_SPEC, VMEM_SPEC),
+        scratch_shapes=[
+            pltpu.VMEM((4 * ROWS, LANES), jnp.int32),
+            pltpu.VMEM((ROWS, LANES), jnp.int32),
+            pltpu.SemaphoreType.DMA((2 + 2 * (2 + FPLANES),)),
+        ],
+        compiler_params=pltpu.CompilerParams(vmem_limit_bytes=4 * 1024 * 1024),
+        name="prepare",
+    )(
+        (pot_factor * 2.0 * inv_span)[None],
+        *(
+            pltpu.with_memory_space_constraint(value, pltpu.HBM)
+            for value in (
+                adjoints_in.reshape(8 * ROWS, LANES),
+                vector_bits.reshape(4 * ROWS, LANES),
+                potential_int,
+                residual.reshape(16 * ROWS, LANES),
+                chk,
+            )
+        ),
+    )
 
     def shift(value, axis, step):
         n = lax.axis_size(axis)
         return lax.ppermute(value, axis, [(i, (i + step) % n) for i in range(n)])
 
-    above = shift(to_below, "row", 1)
+    above = shift(own, "row", 1)
     below = shift(to_above, "row", -1)
 
     strips = jax.ShapeDtypeStruct((G_ROWS, LANES), F32)
@@ -274,6 +321,7 @@
         out_shape=(strips, strips),
         in_specs=[VMEM_SPEC] * 4,
         out_specs=(VMEM_SPEC, VMEM_SPEC),
+        compiler_params=pltpu.CompilerParams(vmem_limit_bytes=6 * 1024 * 1024),
         name="pack_columns",
     )(own, chk, above, below)
     from_left = shift(to_right, "col", 1)
@@ -296,12 +344,11 @@
             pltpu.VMEM((FPLANES, FEXT, LANES), F32), pltpu.VMEM((FPLANES, FEXT, LANES), F32),
             pltpu.VMEM((TERMS, 4, ROWS, LANES), F32),
         ],
-        compiler_params=pltpu.CompilerParams(vmem_limit_bytes=40 * 1024 * 1024),
+        compiler_params=pltpu.CompilerParams(vmem_limit_bytes=14 * 1024 * 1024),
         name="window",
     )(coefs, (2.0 * inv_span)[None], own, chk, above, below, from_right, from_left)
 
-    grad = grad + lax.ppermute(grad, "vec", [(0, 1), (1, 0), (2, 3), (3, 2)])
-    grad = grad + lax.ppermute(grad, "vec", [(0, 2), (2, 0), (1, 3), (3, 1)])
+    grad = jnp.sum(lax.all_gather(grad, "vec"), axis=0)
     return grad, adjoint_out
 
 

time: 94.5 us -> 85.3 us (0.903)
  starting transfers between devices: 29.6 us -> 22.8 us
  blocking collectives: 0 us -> 6.72 us
  local copies, waits for them, and re-layouts: 4.76 us -> 0.01 us
  waiting for transfers between devices: 38.2 us -> 35.9 us
  other arithmetic: 1.86 us -> 0.88 us
    all_gather x0 -> x1, blocking collectives: none -> 6.72 us  [per_device(): grad = jnp.sum(lax.all_gather(grad, 'vec'), axis=0)]
    ppermute x2 -> x0, starting transfers between devices: 6.71 us -> none  [the longest x1 3.56 us: per_device(): grad = grad + lax.ppermute(grad, 'vec', [(0, 1), (1, 0), (2, 3), (3, 2)])]
    unnamed x22 -> x4, local copies, waits for them, and re-layouts: 3.72 us -> 0.01 us
    pallas_call x1, Pallas kernels: 2.95 us -> 0.47 us  [per_device(): pl.pallas_call(pack_kernel, out_shape=(strips, strips), in_specs=[VMEM_SP...]
    ppermute x2 -> x0, waiting for transfers between devices: 2.13 us -> none  [the longest x1 1.31 us: per_device(): grad = grad + lax.ppermute(grad, 'vec', [(0, 2), (2, 0), (1, 3), (3, 1)])]
    pallas_call x0 -> x1, Pallas kernels: none -> 1.69 us  [per_device(): pl.pallas_call(prepare_kernel, out_shape=(send, send), in_specs=[SMEM_SPE...]
    slice x1 -> x0, local copies, waits for them, and re-layouts: 1.04 us -> none  [per_device(): to_above = jnp.concatenate([own, chk[:, :FHALO].reshape(-1, LANES)], axis=0)]
  transfers between devices with their start and end apart: 6 -> 4, of which waited for: 6 -> 4; matrix products, arithmetic and copies ran while one was open for 0% -> 0% of each run, Pallas kernels for 0% -> 0%
where the time goes in v2:
time: 85.3 us; the launch traced here: 85.1 us
  waiting for transfers between devices  35.9 us (42%)
  starting transfers between devices  22.8 us (27%)
  Pallas kernels  16.7 us (20%)
  blocking collectives  6.72 us (8%)
  between operations  2.06 us (2%)
  other arithmetic  0.88 us (1%)
    ppermute x4, waiting for transfers between devices, shift(): return lax.ppermute(value, axis, [(i, (i + step) % n) for i in range(n)])  35.9 us
    ppermute x4, starting transfers between devices, shift(): return lax.ppermute(value, axis, [(i, (i + step) % n) for i in range(n)])  22.8 us
    pallas_call x1, Pallas kernels, per_device(): pl.pallas_call(main_kernel, out_shape=(jax.ShapeDtypeStruct((2, 4, ROWS,...  14.5 us
    all_gather x1, blocking collectives, per_device(): grad = jnp.sum(lax.all_gather(grad, 'vec'), axis=0)  6.72 us
  transfers between devices with their start and end apart: 4, of which 4 were waited for; matrix products, arithmetic and copies ran while one was open for 0% of the time, Pallas kernels for 0%

profile of v2, /device:TPU:1, one launch (start us, length us, event | category | flops | bytes accessed | tf_op | source)
XLA Modules:
  0.0 85.1 jit_solution(18153993055822207399)
XLA Ops:
  1.3 0.0 copy-start
  1.3 1.7 %prepare.1 = (f32[1184,128]{1,0:T(8,128)S(1)}, f32[1184,128]{1,0:T(8,128)S(1)}) custom-call(f32[1]{0:T(128)S(6)} %mul.89.factor, f32[256,128]{1,0:T(8,128)} %bitcast.11, s32[128,128]{1,0:T(8,128)} %bitcast.12, s32[32,128]{1,0:T(8,128)} %pot.1, f32[512,128]{1,0:T(8,128)} %bitcast.10, f32[512,128]{1,0:T(8,128)} %bitcast.6), custom_call_target="tpu_custom_call" | custom-call | tf_op jit(solution)/shard_map/prepare/pallas_call | solution.py:285
  3.0 5.7 %collective-permute-start = (f32[1184,128]{1,0:T(8,128)S(1)}, f32[1184,128]{1,0:T(8,128)S(1)}, u32[]{:S(2)}, u32[]{:S(2)}) collective-permute-start(f32[1184,128]{1,0:T(8,128)S(1)} %get-tuple-element.8.own), channel_id=1, source_target_pairs={{0,16},{16,32},{32,48},{48,64},{64,80},{80,96},{96,112},{112,0},{1... | collective-permute-start | bytes 1818632 | tf_op jit(solution)/shard_map/ppermute | solution.py:313
  8.7 4.1 %collective-permute-start.1 = (f32[1184,128]{1,0:T(8,128)S(1)}, f32[1184,128]{1,0:T(8,128)S(1)}, u32[]{:S(2)}, u32[]{:S(2)}) collective-permute-start(f32[1184,128]{1,0:T(8,128)S(1)} %get-tuple-element.9), channel_id=1, source_target_pairs={{0,112},{16,0},{32,16},{48,32},{64,48},{80,64},{96,80},{112,96},{1... | collective-permute-start | bytes 1818632 | tf_op jit(solution)/shard_map/ppermute | solution.py:313
  13.5 18.2 %collective-permute-done.above = f32[1184,128]{1,0:T(8,128)S(1)} collective-permute-done((f32[1184,128]{1,0:T(8,128)S(1)}, f32[1184,128]{1,0:T(8,128)S(1)}, u32[]{:S(2)}, u32[]{:S(2)}) %collective-permute-start) | collective-permute-done | bytes 606240 | tf_op jit(solution)/shard_map/ppermute | solution.py:313
  31.8 6.2 %collective-permute-done.1.below = f32[1184,128]{1,0:T(8,128)S(1)} collective-permute-done((f32[1184,128]{1,0:T(8,128)S(1)}, f32[1184,128]{1,0:T(8,128)S(1)}, u32[]{:S(2)}, u32[]{:S(2)}) %collective-permute-start.1) | collective-permute-done | bytes 606240 | tf_op jit(solution)/shard_map/ppermute | solution.py:313
  38.0 0.0 copy-done
  38.0 0.5 pack_columns.1
  38.5 0.0 copy-start.1
  38.5 11.1 %collective-permute-start.2 = (f32[824,128]{1,0:T(8,128)S(1)}, f32[824,128]{1,0:T(8,128)S(1)}, u32[]{:S(2)}, u32[]{:S(2)}) collective-permute-start(f32[824,128]{1,0:T(8,128)S(1)} %get-tuple-element.10), channel_id=1, source_target_pairs={{0,15},{1,0},{2,1},{3,2},{4,3},{5,4},{6,5},{7,6},{8,7},{9,8},{10,9... | collective-permute-start | bytes 1265672 | tf_op jit(solution)/shard_map/ppermute | solution.py:313
  49.6 1.9 %collective-permute-start.3 = (f32[824,128]{1,0:T(8,128)S(1)}, f32[824,128]{1,0:T(8,128)S(1)}, u32[]{:S(2)}, u32[]{:S(2)}) collective-permute-start(f32[824,128]{1,0:T(8,128)S(1)} %get-tuple-element.11), channel_id=1, source_target_pairs={{0,1},{1,2},{2,3},{3,4},{4,5},{5,6},{6,7},{7,8},{8,9},{9,10},{10,1... | collective-permute-start | bytes 1265672 | tf_op jit(solution)/shard_map/ppermute | solution.py:313
  51.5 0.0 copy-done.1
  51.6 0.1 sine_multiply_fusion
  51.6 0.1 multiply_divide_fusion.coef
  51.8 6.4 %collective-permute-done.2.from_right = f32[824,128]{1,0:T(8,128)S(1)} collective-permute-done((f32[824,128]{1,0:T(8,128)S(1)}, f32[824,128]{1,0:T(8,128)S(1)}, u32[]{:S(2)}, u32[]{:S(2)}) %collective-permute-start.2) | collective-permute-done | bytes 421920 | tf_op jit(solution)/shard_map/ppermute | solution.py:313
  58.2 5.0 %collective-permute-done.3.from_left = f32[824,128]{1,0:T(8,128)S(1)} collective-permute-done((f32[824,128]{1,0:T(8,128)S(1)}, f32[824,128]{1,0:T(8,128)S(1)}, u32[]{:S(2)}, u32[]{:S(2)}) %collective-permute-start.3) | collective-permute-done | bytes 421920 | tf_op jit(solution)/shard_map/ppermute | solution.py:313
  63.2 14.5 %window.1 = (f32[2,4,32,128]{3,2,1,0:T(8,128)}, f32[32,128]{1,0:T(8,128)S(1)}) custom-call(f32[32,16]{1,0:T(8,128)S(1)} %multiply_divide_fusion.coef, f32[1]{0:T(128)S(6)} %mul.87.scale, f32[1184,128]{1,0:T(8,128)S(1)} %get-tuple-element.8.own, f32[512,128]{1,0:T(8,128)S(1)} %bitcast.8, f32[1184,128]{1,0:T(8,128)S(1)} %collective-permute-done.above, ...), custom_call_target="tpu_custom_call" | custom-call | tf_op jit(solution)/shard_map/window/pallas_call | solution.py:331
  77.8 6.7 %all-gather = f32[128,128]{1,0:T(8,128)S(1)} all-gather(f32[32,128]{1,0:T(8,128)S(1)} %get-tuple-element.12), channel_id=2, replica_groups=mesh['vec'=4,'row'=8,'col'=16] {'vec'}, dimensions={0}, use_global_device_ids=true | all-gather | bytes 81920 | tf_op jit(solution)/shard_map/all_gather | solution.py:351
  84.5 0.6 reduce_sum.9
  (2 shorter events, 0.1 us)
Async XLA Ops:
  1.3 36.7 %copy-start = (f32[2,2,4,32,128]{4,3,2,1,0:T(8,128)S(1)}, f32[2,2,4,32,128]{4,3,2,1,0:T(8,128)}, u32[]{:S(2)}) copy-start(f32[2,2,4,32,128]{4,3,2,1,0:T(8,128)} %param.8) | copy-start | bytes 786436
  3.0 28.7 %collective-permute-start = (f32[1184,128]{1,0:T(8,128)S(1)}, f32[1184,128]{1,0:T(8,128)S(1)}, u32[]{:S(2)}, u32[]{:S(2)}) collective-permute-start(f32[1184,128]{1,0:T(8,128)S(1)} %get-tuple-element.8.own), channel_id=1, source_target_pairs={{0,16},{16,32},{32,48},{48,64},{64,80},{80,96},{96,112},{112,0},{1... | collective-permute-start | bytes 1818632 | tf_op jit(solution)/shard_map/ppermute | solution.py:313
  8.7 29.3 %collective-permute-start.1 = (f32[1184,128]{1,0:T(8,128)S(1)}, f32[1184,128]{1,0:T(8,128)S(1)}, u32[]{:S(2)}, u32[]{:S(2)}) collective-permute-start(f32[1184,128]{1,0:T(8,128)S(1)} %get-tuple-element.9), channel_id=1, source_target_pairs={{0,112},{16,0},{32,16},{48,32},{64,48},{80,64},{96,80},{112,96},{1... | collective-permute-start | bytes 1818632 | tf_op jit(solution)/shard_map/ppermute | solution.py:313
  38.5 13.1 %copy-start.1 = (f32[16]{0:T(128)S(1)}, f32[16]{0:T(128)}, u32[]{:S(2)}) copy-start(f32[16]{0:T(128)} %param.13) | copy-start | bytes 196
  38.5 19.7 %collective-permute-start.2 = (f32[824,128]{1,0:T(8,128)S(1)}, f32[824,128]{1,0:T(8,128)S(1)}, u32[]{:S(2)}, u32[]{:S(2)}) collective-permute-start(f32[824,128]{1,0:T(8,128)S(1)} %get-tuple-element.10), channel_id=1, source_target_pairs={{0,15},{1,0},{2,1},{3,2},{4,3},{5,4},{6,5},{7,6},{8,7},{9,8},{10,9... | collective-permute-start | bytes 1265672 | tf_op jit(solution)/shard_map/ppermute | solution.py:313
  49.6 13.6 %collective-permute-start.3 = (f32[824,128]{1,0:T(8,128)S(1)}, f32[824,128]{1,0:T(8,128)S(1)}, u32[]{:S(2)}, u32[]{:S(2)}) collective-permute-start(f32[824,128]{1,0:T(8,128)S(1)} %get-tuple-element.11), channel_id=1, source_target_pairs={{0,1},{1,2},{2,3},{3,4},{4,5},{5,6},{6,7},{7,8},{8,9},{9,10},{10,1... | collective-permute-start | bytes 1265672 | tf_op jit(solution)/shard_map/ppermute | solution.py:313

commit v3 on v2

v3 whole, which is shorter than its diff:
```python
import functools
import math

import jax
import jax.numpy as jnp
from jax import lax
from jax.experimental import pallas as pl
from jax.experimental.pallas import tpu as pltpu
from jax.sharding import PartitionSpec as P

SEG = 16
MOMENTS = 1024
QMAX = 32767
TERMS = 2 * SEG
NVEC = 16
F32 = jnp.float32

ADJ, SGN, RES, ONS = 0, 8, 12, 20
PLANES = 21
HALF = 8
ROWS = 32
HALO = 32
EXT = ROWS + 2 * HALO
FHALO = 16
FEXT = ROWS + 2 * FHALO
LANES = 128
FPLANES = 16
MAIN = PLANES * ROWS
GROUPS = 5
G_RES = 3 * EXT
G_ADJ = GROUPS * EXT
G_ONS = EXT // 4
G_ROWS = G_ADJ + G_ONS + 2 * FEXT


def window_coefs(first_segment, energies):
    moment_order = first_segment[0] * SEG + jnp.arange(TERMS, dtype=jnp.int32)
    degree = moment_order.astype(jnp.float32)
    kernel_norm = float(MOMENTS + 1)
    angle_step = math.pi / kernel_norm
    jackson = (
        (kernel_norm - degree) * jnp.cos(angle_step * degree)
        + jnp.sin(angle_step * degree) * (math.cos(angle_step) / math.sin(angle_step))
    ) / kernel_norm
    factor = jnp.where(moment_order == 0, 1.0, 2.0).astype(jnp.float32)
    angles = jnp.arccos(energies)
    cosines = jnp.cos(degree[:, None] * angles[None, :])
    return (jackson * factor)[:, None] * cosines / (math.pi * jnp.sin(angles))[None, :]


def lane_iota():
    return lax.broadcasted_iota(jnp.int32, (8, LANES), 1)


def tile(ref, row):
    return ref[pl.ds(row, 8), :]


def main_tile(own, above, below, plane, t):
    section = (above, own, below)[t // 4]
    return tile(section, plane * ROWS + (t % 4) * 8)


def fwd_tile(chk, above, below, plane, t):
    if t < 2:
        return tile(above, MAIN + plane * FHALO + t * 8)
    if t < 6:
        return tile(chk, plane * ROWS + (t - 2) * 8)
    return tile(below, MAIN + plane * FHALO + (t - 6) * 8)


def prepare_kernel(
    factor, core, adj, bits, pot, res, chk, to_below, to_above, chk_v, bits_v, pot_v, sems
):
    copies = []

    def start(src, dst):
        copy = pltpu.make_async_copy(src, dst, sems.at[len(copies)])
        copy.start()
        copies.append(copy)

    first_res = pl.multiple_of(core[0] * (HALF * ROWS), HALF * ROWS)
    start(bits, bits_v)
    start(pot, pot_v)
    for out, first in ((to_below, ROWS - FHALO), (to_above, 0)):
        start(adj, out.at[pl.ds(ADJ * ROWS, 8 * ROWS)])
        start(res.at[pl.ds(first_res, HALF * ROWS)], out.at[pl.ds(RES * ROWS, HALF * ROWS)])
        for plane in range(FPLANES):
            start(
                chk.at[pl.ds(plane * ROWS + first, FHALO)],
                out.at[pl.ds(MAIN + plane * FHALO, FHALO)],
            )
    start(chk, chk_v)
    copies[0].wait()
    signs = (2 * bits_v[...] - 1).astype(F32) * (1.0 / NVEC)
    copies[1].wait()
    onsite = pot_v[...].astype(F32) * factor[0]
    for out in (to_below, to_above):
        out[pl.ds(SGN * ROWS, 4 * ROWS), :] = signs
        out[pl.ds(ONS * ROWS, ROWS), :] = onsite
    for copy in copies[2:]:
        copy.wait()


def pack_kernel(own, chk, above, below, to_left, to_right, to_core):
    lane = lane_iota()

    def pack(tiles, row):
        count = len(tiles)
        width = LANES // count
        group = lane // width
        left = right = None
        for j, value in enumerate(tiles):
            rolled = pltpu.roll(value, width * j, 1) if j else value
            left = rolled if j == 0 else jnp.where(group == j, rolled, left)
            right = rolled if j == 0 else jnp.where(group == (j + count - 1) % count, rolled, right)
        to_left[pl.ds(row, 8), :] = left
        to_right[pl.ds(row, 8), :] = right

    for g in range(GROUPS):
        for t in range(EXT // 8):
            pack([main_tile(own, above, below, 4 * g + j, t) for j in range(4)], g * EXT + t * 8)
    for m in range(3):
        pack([main_tile(own, above, below, ONS, 3 * j + m) for j in range(4)], G_ADJ + m * 8)
    for g in range(2):
        for t in range(FEXT // 8):
            pack(
                [fwd_tile(chk, above, below, 8 * g + j, t) for j in range(8)],
                G_ADJ + G_ONS + g * FEXT + t * 8,
            )
    size = HALF * ROWS
    to_core[pl.ds(0, size), :] = above[pl.ds(RES * ROWS, size), :]
    to_core[pl.ds(size, size), :] = below[pl.ds(RES * ROWS, size), :]


def unpack_strip(from_right, from_left, lane, right_row, left_row, j, count):
    width = LANES // count
    mixed = jnp.where(lane // width == j, tile(from_right, right_row), tile(from_left, left_row))
    return pltpu.roll(mixed, (LANES - width * j) % LANES, 1) if j else mixed


def weigh(coef, t_term, planes):
    total = None
    for e, value in enumerate(planes):
        term = value * coef[t_term, e]
        total = term if total is None else total + term
    return total


def phase_tiles(phase):
    return phase, EXT // 8 - phase


def weights_kernel(coef, core, own, res, above, below, swapped, out):
    other = (1 - core[0]) * (HALF * ROWS)
    for t in range(EXT // 8):
        def body(t_term, carry, t=t):
            planes = [main_tile(own, above, below, RES + e, t) for e in range(HALF)]
            for e in range(HALF):
                if t < 4:
                    planes.append(tile(swapped, e * ROWS + t * 8))
                elif t < 8:
                    row = pl.multiple_of(other + e * ROWS + (t - 4) * 8, 8)
                    planes.append(tile(res, row))
                else:
                    planes.append(tile(swapped, (HALF + e) * ROWS + (t - 8) * 8))
            out[t_term, pl.ds(t * 8, 8), :] = weigh(coef, t_term, planes)
            return carry
        phase = min(t, EXT // 8 - 1 - t, 3)
        lax.fori_loop(TERMS - 8 * (phase + 1), TERMS, body, 0, unroll=4)


class Stencil:
    def __init__(self):
        lane, sub = lane_iota(), lax.broadcasted_iota(jnp.int32, (8, LANES), 0)
        self.lane = lane
        self.first_lane, self.last_lane = lane == 0, lane == LANES - 1
        self.first_sub, self.last_sub = sub == 0, sub == 7

    def tiles(self, cref, href, plane, lo, hi, count):
        def load(t):
            return cref[plane, pl.ds(t * 8, 8), :], href[plane, pl.ds(t * 8, 8), :]

        def rolled(pair, shift):
            return tuple(pltpu.roll(p, shift, 0) for p in pair)

        here = load(lo)
        here_up, here_down = rolled(here, 1), rolled(here, 7)
        prev_up = rolled(load(lo - 1), 1) if lo > 0 else here_up
        for t in range(lo, hi):
            after = load(t + 1) if t + 1 < count else here
            after_up, after_down = rolled(after, 1), rolled(after, 7)
            c, h = here
            cl, cr = pltpu.roll(c, 1, 1), pltpu.roll(c, LANES - 1, 1)
            hl, hr = pltpu.roll(h, 1, 1), pltpu.roll(h, LANES - 1, 1)
            side_c = jnp.where(self.first_lane, hl, cl) + jnp.where(self.last_lane, hr, cr)
            side_h = jnp.where(self.first_lane, cl, hl) + jnp.where(self.last_lane, cr, hr)
            vert = [
                jnp.where(self.first_sub, prev_up[k], here_up[k])
                + jnp.where(self.last_sub, after_down[k], here_down[k])
                for k in range(2)
            ]
            yield t, c, h, side_c + vert[0], side_h + vert[1]
            here, prev_up, here_up, here_down = after, here_up, after_up, after_down


def forward_kernel(scale, own, chk, above, below, from_right, from_left, vs, fc, fh, onc, onh):
    stencil = Stencil()
    lane = stencil.lane
    s = scale[0]
    for t in range(FEXT // 8):
        row = pl.ds(t * 8, 8)
        for plane in range(FPLANES):
            at = G_ADJ + G_ONS + (plane // 8) * FEXT + t * 8
            fc[plane, row, :] = fwd_tile(chk, above, below, plane, t)
            fh[plane, row, :] = unpack_strip(from_right, from_left, lane, at, at, plane % 8, 8)
        e = t + (HALO - FHALO) // 8
        at = G_ADJ + (e % 3) * 8
        onc[row, :] = main_tile(own, above, below, ONS, e)
        onh[row, :] = unpack_strip(from_right, from_left, lane, at, at, e // 3, 4)
    for segment in range(2):
        for which in range(2):
            for v in range(4):
                for i in range(4):
                    vs[segment * SEG + which, v, pl.ds(i * 8, 8), :] = tile(
                        chk, (segment * 8 + which * 4 + v) * ROWS + i * 8
                    )

    def forward(k, new, old, lo, hi):
        for segment in range(2):
            for v in range(4):
                p_new = segment * 8 + new * 4 + v
                p_old = segment * 8 + old * 4 + v
                for t, c, h, nc, nh in stencil.tiles(fc, fh, p_new, lo, hi, FEXT // 8):
                    row = pl.ds(t * 8, 8)
                    out_c = onc[row, :] * c - s * nc - fc[p_old, row, :]
                    out_h = onh[row, :] * h - s * nh - fh[p_old, row, :]
                    fc[p_old, row, :] = out_c
                    fh[p_old, row, :] = out_h
                    if 2 <= t < 6:
                        vs[segment * SEG + k, v, pl.ds((t - 2) * 8, 8), :] = out_c

    for start, stop, lo, hi in ((1, 4, 0, 8), (4, 8, 1, 7)):
        def body(i, carry, lo=lo, hi=hi):
            forward(2 * i, 1, 0, lo, hi)
            forward(2 * i + 1, 0, 1, lo, hi)
            return carry
        lax.fori_loop(start, stop, body, 0)


def adjoint_kernel(
    coef, scale, own, above, below, from_right, from_left, swapped, vs, wcs,
    adj_out, grad_out,
    xc, xh, sgc, sgh, rsh, onc, onh, whr,
):
    stencil = Stencil()
    lane = stencil.lane
    s = scale[0]

    def strip(row, j, count):
        return unpack_strip(from_right, from_left, lane, row, row, j, count)

    for t in range(EXT // 8):
        row = pl.ds(t * 8, 8)
        for plane in range(8):
            xc[plane, row, :] = main_tile(own, above, below, plane, t)
            xh[plane, row, :] = strip((plane // 4) * EXT + t * 8, plane % 4, 4)
        for v in range(4):
            sgc[v, row, :] = main_tile(own, above, below, SGN + v, t)
            sgh[v, row, :] = strip(2 * EXT + t * 8, v, 4)
        for e in range(HALF):
            at = (e // 4) * EXT + t * 8
            rsh[e, row, :] = strip(G_RES + at, e % 4, 4)
            rsh[HALF + e, row, :] = unpack_strip(
                swapped, swapped, lane, at, 2 * EXT + at, e % 4, 4
            )
        onc[row, :] = main_tile(own, above, below, ONS, t)
        onh[row, :] = strip(G_ADJ + (t % 3) * 8, t // 3, 4)

    def adjoint(t_term, new, old, lo, hi, grads):
        grads = list(grads)
        for t in range(lo, hi):
            row = pl.ds(t * 8, 8)
            whr[row, :] = weigh(coef, t_term, [rsh[e, row, :] for e in range(2 * HALF)])
        for v in range(4):
            p_new, p_old = new * 4 + v, old * 4 + v
            for t, c, h, nc, nh in stencil.tiles(xc, xh, p_new, lo, hi, EXT // 8):
                row = pl.ds(t * 8, 8)
                if 4 <= t < 8:
                    grads[t - 4] = grads[t - 4] + c * vs[t_term, v, pl.ds((t - 4) * 8, 8), :]
                xc[p_old, row, :] = (
                    wcs[t_term, row, :] * sgc[v, row, :]
                    + (onc[row, :] * c - s * nc)
                    - xc[p_old, row, :]
                )
                xh[p_old, row, :] = (
                    whr[row, :] * sgh[v, row, :]
                    + (onh[row, :] * h - s * nh)
                    - xh[p_old, row, :]
                )
        return tuple(grads)

    grads = tuple(jnp.zeros((8, LANES), F32) for _ in range(4))
    for phase in range(4):
        lo, hi = phase_tiles(phase)
        def body(i, carry, phase=phase, lo=lo, hi=hi):
            t_term = TERMS - 1 - 8 * phase - 2 * i
            carry = adjoint(t_term, 0, 1, lo, hi, carry)
            return adjoint(t_term - 1, 1, 0, lo, hi, carry)
        grads = lax.fori_loop(0, 4, body, grads)
    for i in range(4):
        grad_out[pl.ds(i * 8, 8), :] = grads[i] * s
    for which in range(2):
        for v in range(4):
            for i in range(4):
                adj_out[which, v, pl.ds(i * 8, 8), :] = xc[which * 4 + v, pl.ds(HALO + i * 8, 8), :]


VMEM_SPEC = pl.BlockSpec(memory_space=pltpu.VMEM)
SMEM_SPEC = pl.BlockSpec(memory_space=pltpu.SMEM)
HBM_SPEC = pl.BlockSpec(memory_space=pltpu.HBM)


def params(mib):
    return pltpu.CompilerParams(vmem_limit_bytes=mib * 1024 * 1024)


def per_device(
    checkpoints,
    adjoints_in,
    vector_bits,
    potential_int,
    pot_scale,
    energies,
    residual,
    first_segment,
):
    pot_factor = pot_scale[0]
    inv_span = 1.0 / (4.5 + QMAX * pot_factor)
    core = lax.axis_index("vec") % 2
    coefs = window_coefs(first_segment, energies)
    coefs = jnp.where(core == 0, coefs, jnp.roll(coefs, HALF, axis=1))
    core = core[None]
    chk = checkpoints.reshape(FPLANES * ROWS, LANES)
    res = residual.reshape(2 * HALF * ROWS, LANES)
    scale = (2.0 * inv_span)[None]
    send = jax.ShapeDtypeStruct((MAIN + FPLANES * FHALO, LANES), F32)
    own, to_above, chk = pl.pallas_call(
        prepare_kernel,
        out_shape=(send, send, jax.ShapeDtypeStruct((FPLANES * ROWS, LANES), F32)),
        in_specs=[SMEM_SPEC] * 2 + [HBM_SPEC] * 5,
        out_specs=(VMEM_SPEC,) * 3,
        scratch_shapes=[
            pltpu.VMEM((4 * ROWS, LANES), jnp.int32),
            pltpu.VMEM((ROWS, LANES), jnp.int32),
            pltpu.SemaphoreType.DMA((3 + 2 * (2 + FPLANES),)),
        ],
        compiler_params=params(4),
        name="prepare",
    )(
        pot_factor * scale,
        core,
        *(
            pltpu.with_memory_space_constraint(value, pltpu.HBM)
            for value in (
                adjoints_in.reshape(8 * ROWS, LANES),
                vector_bits.reshape(4 * ROWS, LANES),
                potential_int,
                res,
                chk,
            )
        ),
    )

    def shift(value, axis, step):
        n = lax.axis_size(axis)
        return lax.ppermute(value, axis, [(i, (i + step) % n) for i in range(n)])

    def swap_cores(value):
        return lax.ppermute(value, "vec", [(0, 1), (1, 0), (2, 3), (3, 2)])

    above = shift(own, "row", 1)
    below = shift(to_above, "row", -1)

    strips = jax.ShapeDtypeStruct((G_ROWS, LANES), F32)
    to_left, to_right, to_core = pl.pallas_call(
        pack_kernel,
        out_shape=(strips, strips, jax.ShapeDtypeStruct((2 * HALF * ROWS, LANES), F32)),
        in_specs=[VMEM_SPEC] * 4,
        out_specs=(VMEM_SPEC,) * 3,
        compiler_params=params(6),
        name="pack_columns",
    )(own, chk, above, below)
    from_left = shift(to_right, "col", 1)
    from_right = shift(to_left, "col", -1)
    swapped_rows = swap_cores(to_core)
    weights = pl.pallas_call(
        weights_kernel,
        out_shape=jax.ShapeDtypeStruct((TERMS, EXT, LANES), F32),
        in_specs=[SMEM_SPEC] * 2 + [VMEM_SPEC] * 5,
        out_specs=VMEM_SPEC,
        compiler_params=params(6),
        cost_estimate=pl.CostEstimate(flops=12_000_000, bytes_accessed=4_000_000, transcendentals=0),
        name="weights",
    )(coefs, core, own, res, above, below, swapped_rows)

    weights, from_right, from_left = lax.optimization_barrier((weights, from_right, from_left))
    strip_rows = slice(G_RES, G_RES + 2 * EXT)
    swapped_strips = swap_cores(
        jnp.concatenate([from_right[strip_rows], from_left[strip_rows]], axis=0)
    )
    frame = (FPLANES, FEXT, LANES)
    states = pl.pallas_call(
        forward_kernel,
        out_shape=jax.ShapeDtypeStruct((TERMS, 4, ROWS, LANES), F32),
        in_specs=[SMEM_SPEC] + [VMEM_SPEC] * 6,
        out_specs=VMEM_SPEC,
        scratch_shapes=[
            pltpu.VMEM(frame, F32), pltpu.VMEM(frame, F32),
            pltpu.VMEM(frame[1:], F32), pltpu.VMEM(frame[1:], F32),
        ],
        compiler_params=params(8),
        cost_estimate=pl.CostEstimate(flops=20_000_000, bytes_accessed=6_000_000, transcendentals=0),
        name="forward",
    )(scale, own, chk, above, below, from_right, from_left)

    ext = (EXT, LANES)
    adjoint_out, grad = pl.pallas_call(
        adjoint_kernel,
        out_shape=(
            jax.ShapeDtypeStruct((2, 4, ROWS, LANES), F32),
            jax.ShapeDtypeStruct((ROWS, LANES), F32),
        ),
        in_specs=[SMEM_SPEC, SMEM_SPEC] + [VMEM_SPEC] * 8,
        out_specs=(VMEM_SPEC, VMEM_SPEC),
        scratch_shapes=[
            pltpu.VMEM((8, *ext), F32), pltpu.VMEM((8, *ext), F32),
            pltpu.VMEM((4, *ext), F32), pltpu.VMEM((4, *ext), F32),
            pltpu.VMEM((2 * HALF, *ext), F32),
            pltpu.VMEM(ext, F32), pltpu.VMEM(ext, F32), pltpu.VMEM(ext, F32),
        ],
        compiler_params=params(10),
        name="adjoint",
    )(coefs, scale, own, above, below, from_right, from_left, swapped_strips, states, weights)

    grad = jnp.sum(lax.all_gather(grad, "vec"), axis=0)
    return grad, adjoint_out


def solution(mesh):
    return jax.shard_map(
        per_device,
        mesh=mesh,
        in_specs=(
            P(None, None, "vec", "row", "col"),
            P(None, "vec", "row", "col"),
            P("vec", "row", "col"),
            P("row", "col"),
            P(),
            P(),
            P(None, "row", "col"),
            P(),
        ),
        out_specs=(P("row", "col"), P(None, "vec", "row", "col")),
        check_vma=False,
    )
```

time: 85.3 us -> 81.3 us (0.953)
  waiting for transfers between devices: 35.9 us -> 22.4 us
  starting transfers between devices: 22.8 us -> 29.4 us
  Pallas kernels: 16.7 us -> 20.2 us
  blocking collectives: 6.72 us -> 5.07 us
    ppermute x4, waiting for transfers between devices: 35.9 us -> 22.4 us  [shift(): return lax.ppermute(value, axis, [(i, (i + step) % n) for i in range(n)])]
    ppermute x0 -> x2, starting transfers between devices: none -> 6.57 us  [swap_cores(): return lax.ppermute(value, 'vec', [(0, 1), (1, 0), (2, 3), (3, 2)])]
    pallas_call x3 -> x5, Pallas kernels: 16.7 us -> 20.2 us  [the longest x1 9.19 us: per_device(): pl.pallas_call(adjoint_kernel, out_shape=(jax.ShapeDtypeStruct((2, 4, ROW...]
    all_gather x1, blocking collectives: 6.72 us -> 5.07 us  [per_device(): grad = jnp.sum(lax.all_gather(grad, 'vec'), axis=0)]
  transfers between devices with their start and end apart: 4 -> 6, of which waited for: 4 -> 4; matrix products, arithmetic and copies ran while one was open for 0% -> 1% of each run, Pallas kernels for 0% -> 10%
where the time goes in v3:
time: 81.3 us; the launch traced here: 81 us
  starting transfers between devices  29.4 us (36%)
  waiting for transfers between devices  22.4 us (28%)
  Pallas kernels  20.2 us (25%)
  blocking collectives  5.07 us (6%)
  between operations  2.17 us (3%)
  other arithmetic  1.69 us (2%)
    ppermute x4, starting transfers between devices, shift(): return lax.ppermute(value, axis, [(i, (i + step) % n) for i in range(n)])  22.8 us
    ppermute x4, waiting for transfers between devices, shift(): return lax.ppermute(value, axis, [(i, (i + step) % n) for i in range(n)])  22.4 us
    pallas_call x1, Pallas kernels, per_device(): pl.pallas_call(adjoint_kernel, out_shape=(jax.ShapeDtypeStruct((2, 4, ROW...  9.19 us
    ppermute x2, starting transfers between devices, swap_cores(): return lax.ppermute(value, 'vec', [(0, 1), (1, 0), (2, 3), (3, 2)])  6.57 us
    all_gather x1, blocking collectives, per_device(): grad = jnp.sum(lax.all_gather(grad, 'vec'), axis=0)  5.07 us
    pallas_call x1, Pallas kernels, per_device(): pl.pallas_call(weights_kernel, out_shape=jax.ShapeDtypeStruct((TERMS, EXT...  4.25 us
    pallas_call x1, Pallas kernels, per_device(): pl.pallas_call(forward_kernel, out_shape=jax.ShapeDtypeStruct((TERMS, 4,...  3.96 us
    pallas_call x1, Pallas kernels, per_device(): pl.pallas_call(prepare_kernel, out_shape=(send, send, jax.ShapeDtypeStruc...  1.76 us
  transfers between devices with their start and end apart: 6, of which 4 were waited for; matrix products, arithmetic and copies ran while one was open for 1% of the time, Pallas kernels for 10%

profile of v3, /device:TPU:1, one launch (start us, length us, event | category | flops | bytes accessed | tf_op | source)
XLA Modules:
  0.0 81.0 jit_solution(16725346703306195941)
XLA Ops:
  0.6 0.0 copy-start
  1.4 1.8 %prepare.1 = (f32[928,128]{1,0:T(8,128)S(1)}, f32[928,128]{1,0:T(8,128)S(1)}, f32[512,128]{1,0:T(8,128)S(1)}) custom-call(f32[1]{0:T(128)S(6)} %mul.83.factor, s32[1]{0:T(128)} %bitcast.1.core, f32[256,128]{1,0:T(8,128)} %bitcast.11, s32[128,128]{1,0:T(8,128)} %bitcast.12, s32[32,128]{1,0:T(8,128)} %pot.1, f32[512,128]{1,0:T(8,128)} %bitcast.7, ...), custom_call_target="tpu_custom_call" | custom-call | tf_op jit(solution)/shard_map/prepare/pallas_call | solution.py:348
  3.2 5.7 %collective-permute-start = (f32[928,128]{1,0:T(8,128)S(1)}, f32[928,128]{1,0:T(8,128)S(1)}, u32[]{:S(2)}, u32[]{:S(2)}) collective-permute-start(f32[928,128]{1,0:T(8,128)S(1)} %get-tuple-element.13.own), channel_id=1, source_target_pairs={{0,16},{16,32},{32,48},{48,64},{64,80},{80,96},{96,112},{112,0},{1... | collective-permute-start | bytes 1425416 | tf_op jit(solution)/shard_map/ppermute | solution.py:377
  8.8 4.1 %collective-permute-start.1 = (f32[928,128]{1,0:T(8,128)S(1)}, f32[928,128]{1,0:T(8,128)S(1)}, u32[]{:S(2)}, u32[]{:S(2)}) collective-permute-start(f32[928,128]{1,0:T(8,128)S(1)} %get-tuple-element.14), channel_id=1, source_target_pairs={{0,112},{16,0},{32,16},{48,32},{64,48},{80,64},{96,80},{112,96},{1... | collective-permute-start | bytes 1425416 | tf_op jit(solution)/shard_map/ppermute | solution.py:377
  13.6 0.7 sine_multiply_fusion
  14.4 0.1 multiply_divide_fusion
  14.5 11.7 %collective-permute-done.above = f32[928,128]{1,0:T(8,128)S(1)} collective-permute-done((f32[928,128]{1,0:T(8,128)S(1)}, f32[928,128]{1,0:T(8,128)S(1)}, u32[]{:S(2)}, u32[]{:S(2)}) %collective-permute-start) | collective-permute-done | bytes 475168 | tf_op jit(solution)/shard_map/ppermute | solution.py:377
  26.3 5.1 %collective-permute-done.1.below = f32[928,128]{1,0:T(8,128)S(1)} collective-permute-done((f32[928,128]{1,0:T(8,128)S(1)}, f32[928,128]{1,0:T(8,128)S(1)}, u32[]{:S(2)}, u32[]{:S(2)}) %collective-permute-start.1) | collective-permute-done | bytes 475168 | tf_op jit(solution)/shard_map/ppermute | solution.py:377
  31.3 1.0 %pack_columns.1 = (f32[632,128]{1,0:T(8,128)S(1)}, f32[632,128]{1,0:T(8,128)S(1)}, f32[512,128]{1,0:T(8,128)}) custom-call(f32[928,128]{1,0:T(8,128)S(1)} %get-tuple-element.13.own, f32[512,128]{1,0:T(8,128)S(1)} %get-tuple-element.15.chk, f32[928,128]{1,0:T(8,128)S(1)} %collective-permute-done.above, f32[928,128]{1,0:T(8,128)S(1)} %collective-permute-done.1.below), custom_call_target="tpu_custom_call" | custom-call | tf_op jit(solution)/shard_map/pack_columns/pallas_call | solution.py:386
  32.4 3.6 %collective-permute-start.2 = (f32[512,128]{1,0:T(8,128)}, f32[512,128]{1,0:T(8,128)S(1)}, u32[]{:S(2)}, u32[]{:S(2)}) collective-permute-start(f32[512,128]{1,0:T(8,128)} %get-tuple-element.16), channel_id=1, source_target_pairs={{0,128},{128,0},{256,384},{384,256},{1,129},{129,1},{257,385},{385... | collective-permute-start | bytes 786440 | tf_op jit(solution)/shard_map/ppermute | solution.py:380
  35.9 11.1 %collective-permute-start.3 = (f32[632,128]{1,0:T(8,128)S(1)}, f32[632,128]{1,0:T(8,128)S(1)}, u32[]{:S(2)}, u32[]{:S(2)}) collective-permute-start(f32[632,128]{1,0:T(8,128)S(1)} %get-tuple-element.17), channel_id=1, source_target_pairs={{0,15},{1,0},{2,1},{3,2},{4,3},{5,4},{6,5},{7,6},{8,7},{9,8},{10,9... | collective-permute-start | bytes 970760 | tf_op jit(solution)/shard_map/ppermute | solution.py:377
  47.1 1.9 %collective-permute-start.4 = (f32[632,128]{1,0:T(8,128)S(1)}, f32[632,128]{1,0:T(8,128)S(1)}, u32[]{:S(2)}, u32[]{:S(2)}) collective-permute-start(f32[632,128]{1,0:T(8,128)S(1)} %get-tuple-element.18), channel_id=1, source_target_pairs={{0,1},{1,2},{2,3},{3,4},{4,5},{5,6},{6,7},{7,8},{8,9},{9,10},{10,1... | collective-permute-start | bytes 970760 | tf_op jit(solution)/shard_map/ppermute | solution.py:377
  49.0 0.1 fusion.2
  49.1 0.1 maximum_select_fusion.coef
  49.2 0.0 collective-permute-done.2.swapped
  49.2 0.0 copy-done
  49.2 4.3 %weights.1.wcs = f32[32,96,128]{2,1,0:T(8,128)S(1)} custom-call(f32[32,16]{1,0:T(8,128)S(1)} %maximum_select_fusion.coef, s32[1]{0:T(128)} %bitcast.1.core, f32[928,128]{1,0:T(8,128)S(1)} %get-tuple-element.13.own, f32[512,128]{1,0:T(8,128)S(1)} %bitcast.8, f32[928,128]{1,0:T(8,128)S(1)} %collective-permute-done.above, ...), custom_call_target="tpu_custom_call" | custom-call | flops 12000000 | bytes 4000000 | tf_op jit(solution)/shard_map/weights/pallas_call | solution.py:397
  53.5 0.6 collective-permute-done.3.from_right
  54.1 5.0 %collective-permute-done.4.from_left = f32[632,128]{1,0:T(8,128)S(1)} collective-permute-done((f32[632,128]{1,0:T(8,128)S(1)}, f32[632,128]{1,0:T(8,128)S(1)}, u32[]{:S(2)}, u32[]{:S(2)}) %collective-permute-start.4) | collective-permute-done | bytes 323616 | tf_op jit(solution)/shard_map/ppermute | solution.py:377
  59.1 3.0 %collective-permute-start.5 = (f32[384,128]{1,0:T(8,128)S(1)}, f32[384,128]{1,0:T(8,128)S(1)}, u32[]{:S(2)}, u32[]{:S(2)}) collective-permute-start(f32[384,128]{1,0:T(8,128)S(1)} %pad_maximum_fusion), channel_id=1, source_target_pairs={{0,128},{128,0},{256,384},{384,256},{1,129},{129,1},{257,385},{385... | collective-permute-start | bytes 589832 | tf_op jit(solution)/shard_map/ppermute | solution.py:380
  62.2 4.0 %forward.1.vs = f32[32,4,32,128]{3,2,1,0:T(8,128)S(1)} custom-call(f32[1]{0:T(128)S(6)} %mul.82.scale, f32[928,128]{1,0:T(8,128)S(1)} %get-tuple-element.13.own, f32[512,128]{1,0:T(8,128)S(1)} %get-tuple-element.15.chk, f32[928,128]{1,0:T(8,128)S(1)} %collective-permute-done.above, f32[928,128]{1,0:T(8,128)S(1)} %collective-permute-done.1.below, ...), custom_call_target="tpu_custom_call" | custom-call | flops 20000000 | bytes 6000000 | tf_op jit(solution)/shard_map/forward/pallas_call | solution.py:413
  66.1 0.0 collective-permute-done.5.swapped
  66.1 9.2 %adjoint.1 = (f32[2,4,32,128]{3,2,1,0:T(8,128)}, f32[32,128]{1,0:T(8,128)S(1)}) custom-call(f32[32,16]{1,0:T(8,128)S(1)} %maximum_select_fusion.coef, f32[1]{0:T(128)S(6)} %mul.82.scale, f32[928,128]{1,0:T(8,128)S(1)} %get-tuple-element.13.own, f32[928,128]{1,0:T(8,128)S(1)} %collective-permute-done.above, f32[928,128]{1,0:T(8,128)S(1)} %collective-permute-done.1.below, ...), custom_call_target="tpu_custom_call" | custom-call | tf_op jit(solution)/shard_map/adjoint/pallas_call | solution.py:428
  75.3 5.1 %all-gather = f32[128,128]{1,0:T(8,128)S(1)} all-gather(f32[32,128]{1,0:T(8,128)S(1)} %get-tuple-element.22), channel_id=2, replica_groups=mesh['vec'=4,'row'=8,'col'=16] {'vec'}, dimensions={0}, use_global_device_ids=true | all-gather | bytes 81920 | tf_op jit(solution)/shard_map/all_gather | solution.py:446
  80.4 0.6 reduce_sum.9
  (5 shorter events, 0.1 us)
Async XLA Ops:
  0.6 48.6 %copy-start = (f32[16,32,128]{2,1,0:T(8,128)S(1)}, f32[16,32,128]{2,1,0:T(8,128)}, u32[]{:S(2)}) copy-start(f32[16,32,128]{2,1,0:T(8,128)} %param.14) | copy-start | bytes 786436
  3.2 23.1 %collective-permute-start = (f32[928,128]{1,0:T(8,128)S(1)}, f32[928,128]{1,0:T(8,128)S(1)}, u32[]{:S(2)}, u32[]{:S(2)}) collective-permute-start(f32[928,128]{1,0:T(8,128)S(1)} %get-tuple-element.13.own), channel_id=1, source_target_pairs={{0,16},{16,32},{32,48},{48,64},{64,80},{80,96},{96,112},{112,0},{1... | collective-permute-start | bytes 1425416 | tf_op jit(solution)/shard_map/ppermute | solution.py:377
  8.8 22.5 %collective-permute-start.1 = (f32[928,128]{1,0:T(8,128)S(1)}, f32[928,128]{1,0:T(8,128)S(1)}, u32[]{:S(2)}, u32[]{:S(2)}) collective-permute-start(f32[928,128]{1,0:T(8,128)S(1)} %get-tuple-element.14), channel_id=1, source_target_pairs={{0,112},{16,0},{32,16},{48,32},{64,48},{80,64},{96,80},{112,96},{1... | collective-permute-start | bytes 1425416 | tf_op jit(solution)/shard_map/ppermute | solution.py:377
  32.4 16.8 %collective-permute-start.2 = (f32[512,128]{1,0:T(8,128)}, f32[512,128]{1,0:T(8,128)S(1)}, u32[]{:S(2)}, u32[]{:S(2)}) collective-permute-start(f32[512,128]{1,0:T(8,128)} %get-tuple-element.16), channel_id=1, source_target_pairs={{0,128},{128,0},{256,384},{384,256},{1,129},{129,1},{257,385},{385... | collective-permute-start | bytes 786440 | tf_op jit(solution)/shard_map/ppermute | solution.py:380
  35.9 18.2 %collective-permute-start.3 = (f32[632,128]{1,0:T(8,128)S(1)}, f32[632,128]{1,0:T(8,128)S(1)}, u32[]{:S(2)}, u32[]{:S(2)}) collective-permute-start(f32[632,128]{1,0:T(8,128)S(1)} %get-tuple-element.17), channel_id=1, source_target_pairs={{0,15},{1,0},{2,1},{3,2},{4,3},{5,4},{6,5},{7,6},{8,7},{9,8},{10,9... | collective-permute-start | bytes 970760 | tf_op jit(solution)/shard_map/ppermute | solution.py:377
  47.1 12.0 %collective-permute-start.4 = (f32[632,128]{1,0:T(8,128)S(1)}, f32[632,128]{1,0:T(8,128)S(1)}, u32[]{:S(2)}, u32[]{:S(2)}) collective-permute-start(f32[632,128]{1,0:T(8,128)S(1)} %get-tuple-element.18), channel_id=1, source_target_pairs={{0,1},{1,2},{2,3},{3,4},{4,5},{5,6},{6,7},{7,8},{8,9},{9,10},{10,1... | collective-permute-start | bytes 970760 | tf_op jit(solution)/shard_map/ppermute | solution.py:377
  59.1 7.0 %collective-permute-start.5 = (f32[384,128]{1,0:T(8,128)S(1)}, f32[384,128]{1,0:T(8,128)S(1)}, u32[]{:S(2)}, u32[]{:S(2)}) collective-permute-start(f32[384,128]{1,0:T(8,128)S(1)} %pad_maximum_fusion), channel_id=1, source_target_pairs={{0,128},{128,0},{256,384},{384,256},{1,129},{129,1},{257,385},{385... | collective-permute-start | bytes 589832 | tf_op jit(solution)/shard_map/ppermute | solution.py:380

commit v4 on v3

--- a/solution.py
+++ b/solution.py
@@ -26,6 +26,7 @@
 LANES = 128
 FPLANES = 16
 MAIN = PLANES * ROWS
+WIDE = EXT // 8
 GROUPS = 5
 G_RES = 3 * EXT
 G_ADJ = GROUPS * EXT
@@ -70,7 +71,8 @@
 
 
 def prepare_kernel(
-    factor, core, adj, bits, pot, res, chk, to_below, to_above, chk_v, bits_v, pot_v, sems
+    core, scalar, adj, bits, pot, res, chk,
+    to_below, to_above, chk_v, res_v, scale_v, bits_v, pot_v, sems
 ):
     copies = []
 
@@ -91,10 +93,14 @@
                 out.at[pl.ds(MAIN + plane * FHALO, FHALO)],
             )
     start(chk, chk_v)
+    start(res.at[pl.ds(pl.multiple_of(HALF * ROWS - first_res, HALF * ROWS), HALF * ROWS)], res_v)
     copies[0].wait()
     signs = (2 * bits_v[...] - 1).astype(F32) * (1.0 / NVEC)
     copies[1].wait()
-    onsite = pot_v[...].astype(F32) * factor[0]
+    pot_factor = scalar[0]
+    scale = 2.0 / (4.5 + QMAX * pot_factor)
+    scale_v[0] = scale
+    onsite = pot_v[...].astype(F32) * (pot_factor * scale)
     for out in (to_below, to_above):
         out[pl.ds(SGN * ROWS, 4 * ROWS), :] = signs
         out[pl.ds(ONS * ROWS, ROWS), :] = onsite
@@ -102,7 +108,7 @@
         copy.wait()
 
 
-def pack_kernel(own, chk, above, below, to_left, to_right, to_core):
+def pack_kernel(own, chk, above, below, to_left, to_right):
     lane = lane_iota()
 
     def pack(tiles, row):
@@ -128,9 +134,6 @@
                 [fwd_tile(chk, above, below, 8 * g + j, t) for j in range(8)],
                 G_ADJ + G_ONS + g * FEXT + t * 8,
             )
-    size = HALF * ROWS
-    to_core[pl.ds(0, size), :] = above[pl.ds(RES * ROWS, size), :]
-    to_core[pl.ds(size, size), :] = below[pl.ds(RES * ROWS, size), :]
 
 
 def unpack_strip(from_right, from_left, lane, right_row, left_row, j, count):
@@ -139,35 +142,44 @@
     return pltpu.roll(mixed, (LANES - width * j) % LANES, 1) if j else mixed
 
 
-def weigh(coef, t_term, planes):
-    total = None
-    for e, value in enumerate(planes):
-        term = value * coef[t_term, e]
-        total = term if total is None else total + term
-    return total
+def splats(coef, t_term):
+    return [jnp.full((8, LANES), coef[t_term, e], F32) for e in range(2 * HALF)]
+
+
+def weigh(factors, planes):
+    terms = [value * factor for value, factor in zip(planes, factors)]
+    while len(terms) > 1:
+        terms = [x + y for x, y in zip(terms[::2], terms[1::2])]
+    return terms[0]
 
 
 def phase_tiles(phase):
     return phase, EXT // 8 - phase
 
 
-def weights_kernel(coef, core, own, res, above, below, swapped, out):
-    other = (1 - core[0]) * (HALF * ROWS)
-    for t in range(EXT // 8):
-        def body(t_term, carry, t=t):
-            planes = [main_tile(own, above, below, RES + e, t) for e in range(HALF)]
-            for e in range(HALF):
-                if t < 4:
-                    planes.append(tile(swapped, e * ROWS + t * 8))
-                elif t < 8:
-                    row = pl.multiple_of(other + e * ROWS + (t - 4) * 8, 8)
-                    planes.append(tile(res, row))
-                else:
-                    planes.append(tile(swapped, (HALF + e) * ROWS + (t - 8) * 8))
-            out[t_term, pl.ds(t * 8, 8), :] = weigh(coef, t_term, planes)
+def weights_kernel(coef, own, res_other, above, below, swapped, out):
+    def residuals(t):
+        planes = [main_tile(own, above, below, RES + e, t) for e in range(HALF)]
+        for e in range(HALF):
+            if t < 4:
+                planes.append(tile(swapped, e * ROWS + t * 8))
+            elif t < 8:
+                planes.append(tile(res_other, e * ROWS + (t - 4) * 8))
+            else:
+                planes.append(tile(swapped, (HALF + e) * ROWS + (t - 8) * 8))
+        return planes
+
+    for phase in range(4):
+        lo, hi = phase_tiles(phase)
+
+        def body(i, carry, phase=phase, lo=lo, hi=hi):
+            t_term = TERMS - 8 * (phase + 1) + i
+            factors = splats(coef, t_term)
+            for t in range(lo, hi):
+                out[t_term, pl.ds(t * 8, 8), :] = weigh(factors, residuals(t))
             return carry
-        phase = min(t, EXT // 8 - 1 - t, 3)
-        lax.fori_loop(TERMS - 8 * (phase + 1), TERMS, body, 0, unroll=4)
+
+        lax.fori_loop(0, 8, body, 0)
 
 
 class Stencil:
@@ -207,7 +219,7 @@
 def forward_kernel(scale, own, chk, above, below, from_right, from_left, vs, fc, fh, onc, onh):
     stencil = Stencil()
     lane = stencil.lane
-    s = scale[0]
+    s = jnp.full((8, LANES), scale[0], F32)
     for t in range(FEXT // 8):
         row = pl.ds(t * 8, 8)
         for plane in range(FPLANES):
@@ -255,7 +267,7 @@
 ):
     stencil = Stencil()
     lane = stencil.lane
-    s = scale[0]
+    s = jnp.full((8, LANES), scale[0], F32)
 
     def strip(row, j, count):
         return unpack_strip(from_right, from_left, lane, row, row, j, count)
@@ -279,9 +291,10 @@
 
     def adjoint(t_term, new, old, lo, hi, grads):
         grads = list(grads)
+        factors = splats(coef, t_term)
         for t in range(lo, hi):
             row = pl.ds(t * 8, 8)
-            whr[row, :] = weigh(coef, t_term, [rsh[e, row, :] for e in range(2 * HALF)])
+            whr[row, :] = weigh(factors, [rsh[e, row, :] for e in range(2 * HALF)])
         for v in range(4):
             p_new, p_old = new * 4 + v, old * 4 + v
             for t, c, h, nc, nh in stencil.tiles(xc, xh, p_new, lo, hi, EXT // 8):
@@ -335,31 +348,34 @@
     residual,
     first_segment,
 ):
-    pot_factor = pot_scale[0]
-    inv_span = 1.0 / (4.5 + QMAX * pot_factor)
     core = lax.axis_index("vec") % 2
     coefs = window_coefs(first_segment, energies)
     coefs = jnp.where(core == 0, coefs, jnp.roll(coefs, HALF, axis=1))
     core = core[None]
     chk = checkpoints.reshape(FPLANES * ROWS, LANES)
     res = residual.reshape(2 * HALF * ROWS, LANES)
-    scale = (2.0 * inv_span)[None]
     send = jax.ShapeDtypeStruct((MAIN + FPLANES * FHALO, LANES), F32)
-    own, to_above, chk = pl.pallas_call(
+    own, to_above, chk, res_other, scale = pl.pallas_call(
         prepare_kernel,
-        out_shape=(send, send, jax.ShapeDtypeStruct((FPLANES * ROWS, LANES), F32)),
+        out_shape=(
+            send,
+            send,
+            jax.ShapeDtypeStruct((FPLANES * ROWS, LANES), F32),
+            jax.ShapeDtypeStruct((HALF * ROWS, LANES), F32),
+            jax.ShapeDtypeStruct((1,), F32),
+        ),
         in_specs=[SMEM_SPEC] * 2 + [HBM_SPEC] * 5,
-        out_specs=(VMEM_SPEC,) * 3,
+        out_specs=(VMEM_SPEC,) * 4 + (SMEM_SPEC,),
         scratch_shapes=[
             pltpu.VMEM((4 * ROWS, LANES), jnp.int32),
             pltpu.VMEM((ROWS, LANES), jnp.int32),
-            pltpu.SemaphoreType.DMA((3 + 2 * (2 + FPLANES),)),
+            pltpu.SemaphoreType.DMA((4 + 2 * (2 + FPLANES),)),
         ],
         compiler_params=params(4),
         name="prepare",
     )(
-        pot_factor * scale,
         core,
+        pot_scale,
         *(
             pltpu.with_memory_space_constraint(value, pltpu.HBM)
             for value in (
@@ -383,26 +399,28 @@
     below = shift(to_above, "row", -1)
 
     strips = jax.ShapeDtypeStruct((G_ROWS, LANES), F32)
-    to_left, to_right, to_core = pl.pallas_call(
+    to_left, to_right = pl.pallas_call(
         pack_kernel,
-        out_shape=(strips, strips, jax.ShapeDtypeStruct((2 * HALF * ROWS, LANES), F32)),
+        out_shape=(strips, strips),
         in_specs=[VMEM_SPEC] * 4,
-        out_specs=(VMEM_SPEC,) * 3,
+        out_specs=(VMEM_SPEC,) * 2,
         compiler_params=params(6),
         name="pack_columns",
     )(own, chk, above, below)
+    to_left, res_above, res_below = lax.optimization_barrier((to_left, above, below))
     from_left = shift(to_right, "col", 1)
     from_right = shift(to_left, "col", -1)
-    swapped_rows = swap_cores(to_core)
+    res_rows = slice(RES * ROWS, (RES + HALF) * ROWS)
+    swapped_rows = swap_cores(jnp.concatenate([res_above[res_rows], res_below[res_rows]], axis=0))
     weights = pl.pallas_call(
         weights_kernel,
         out_shape=jax.ShapeDtypeStruct((TERMS, EXT, LANES), F32),
-        in_specs=[SMEM_SPEC] * 2 + [VMEM_SPEC] * 5,
+        in_specs=[SMEM_SPEC] + [VMEM_SPEC] * 5,
         out_specs=VMEM_SPEC,
         compiler_params=params(6),
         cost_estimate=pl.CostEstimate(flops=12_000_000, bytes_accessed=4_000_000, transcendentals=0),
         name="weights",
-    )(coefs, core, own, res, above, below, swapped_rows)
+    )(coefs, own, res_other, above, below, swapped_rows)
 
     weights, from_right, from_left = lax.optimization_barrier((weights, from_right, from_left))
     strip_rows = slice(G_RES, G_RES + 2 * EXT)

time: 81.3 us -> 83.1 us (1.022)
  waiting for transfers between devices: 22.4 us -> 24.3 us
    ppermute x4, waiting for transfers between devices: 22.4 us -> 24.3 us  [shift(): return lax.ppermute(value, axis, [(i, (i + step) % n) for i in range(n)])]
    pallas_call x1, Pallas kernels: 4.25 us -> 2.42 us  [per_device(): pl.pallas_call(weights_kernel, out_shape=jax.ShapeDtypeStruct((TERMS, EXT...]
  transfers between devices with their start and end apart: 6 -> 6, of which waited for: 4 -> 4; matrix products, arithmetic and copies ran while one was open for 1% -> 1% of each run, Pallas kernels for 10% -> 8%
where the time goes in v4:
time: 83.1 us; the launch traced here: 82.7 us
  starting transfers between devices  29.4 us (35%)
  waiting for transfers between devices  24.3 us (29%)
  Pallas kernels  19.4 us (23%)
  blocking collectives  5.07 us (6%)
  other arithmetic  2.4 us (3%)
  between operations  2.09 us (3%)
    ppermute x4, waiting for transfers between devices, shift(): return lax.ppermute(value, axis, [(i, (i + step) % n) for i in range(n)])  24.3 us
    ppermute x4, starting transfers between devices, shift(): return lax.ppermute(value, axis, [(i, (i + step) % n) for i in range(n)])  22.8 us
    pallas_call x1, Pallas kernels, per_device(): pl.pallas_call(adjoint_kernel, out_shape=(jax.ShapeDtypeStruct((2, 4, ROW...  9.69 us
    ppermute x2, starting transfers between devices, swap_cores(): return lax.ppermute(value, 'vec', [(0, 1), (1, 0), (2, 3), (3, 2)])  6.57 us
    all_gather x1, blocking collectives, per_device(): grad = jnp.sum(lax.all_gather(grad, 'vec'), axis=0)  5.07 us
    pallas_call x1, Pallas kernels, per_device(): pl.pallas_call(forward_kernel, out_shape=jax.ShapeDtypeStruct((TERMS, 4,...  4.59 us
    pallas_call x1, Pallas kernels, per_device(): pl.pallas_call(weights_kernel, out_shape=jax.ShapeDtypeStruct((TERMS, EXT...  2.42 us
    pallas_call x1, Pallas kernels, per_device(): pl.pallas_call(prepare_kernel, out_shape=(send, send, jax.ShapeDtypeStruc...  2.32 us
  transfers between devices with their start and end apart: 6, of which 4 were waited for; matrix products, arithmetic and copies ran while one was open for 1% of the time, Pallas kernels for 8%

profile of v4, /device:TPU:1, one launch (start us, length us, event | category | flops | bytes accessed | tf_op | source)
XLA Modules:
  0.0 82.7 jit_solution(11423100989573731162)
XLA Ops:
  1.3 2.3 %prepare.1 = (f32[928,128]{1,0:T(8,128)S(1)}, f32[928,128]{1,0:T(8,128)S(1)}, f32[512,128]{1,0:T(8,128)S(1)}, f32[256,128]{1,0:T(8,128)S(1)}, f32[1]{0:T(128)}) custom-call(s32[1]{0:T(128)} %bitcast.1.core, f32[1]{0:T(128)S(6)} %copy.10.scalar, f32[256,128]{1,0:T(8,128)} %bitcast.10, s32[128,128]{1,0:T(8,128)} %bitcast.11, s32[32,128]{1,0:T(8,128)} %pot.1, ...), custom_call_target="tpu_custom_call" | custom-call | tf_op jit(solution)/shard_map/prepare/pallas_call | solution.py:358
  3.6 5.7 %collective-permute-start = (f32[928,128]{1,0:T(8,128)S(1)}, f32[928,128]{1,0:T(8,128)S(1)}, u32[]{:S(2)}, u32[]{:S(2)}) collective-permute-start(f32[928,128]{1,0:T(8,128)S(1)} %get-tuple-element.18.own), channel_id=1, source_target_pairs={{0,16},{16,32},{32,48},{48,64},{64,80},{80,96},{96,112},{112,0},{1... | collective-permute-start | bytes 1425416 | tf_op jit(solution)/shard_map/ppermute | solution.py:393
  9.3 4.1 %collective-permute-start.1 = (f32[928,128]{1,0:T(8,128)S(1)}, f32[928,128]{1,0:T(8,128)S(1)}, u32[]{:S(2)}, u32[]{:S(2)}) collective-permute-start(f32[928,128]{1,0:T(8,128)S(1)} %get-tuple-element.19), channel_id=1, source_target_pairs={{0,112},{16,0},{32,16},{48,32},{64,48},{80,64},{96,80},{112,96},{1... | collective-permute-start | bytes 1425416 | tf_op jit(solution)/shard_map/ppermute | solution.py:393
  14.1 0.7 sine_multiply_fusion
  14.9 0.1 multiply_divide_fusion
  15.0 11.7 %collective-permute-done.above = f32[928,128]{1,0:T(8,128)S(1)} collective-permute-done((f32[928,128]{1,0:T(8,128)S(1)}, f32[928,128]{1,0:T(8,128)S(1)}, u32[]{:S(2)}, u32[]{:S(2)}) %collective-permute-start) | collective-permute-done | bytes 475168 | tf_op jit(solution)/shard_map/ppermute | solution.py:393
  26.7 5.1 %collective-permute-done.1.below = f32[928,128]{1,0:T(8,128)S(1)} collective-permute-done((f32[928,128]{1,0:T(8,128)S(1)}, f32[928,128]{1,0:T(8,128)S(1)}, u32[]{:S(2)}, u32[]{:S(2)}) %collective-permute-start.1) | collective-permute-done | bytes 475168 | tf_op jit(solution)/shard_map/ppermute | solution.py:393
  31.8 0.4 pack_columns.1
  32.2 0.7 pad_maximum_fusion
  32.9 3.6 %collective-permute-start.2 = (f32[512,128]{1,0:T(8,128)}, f32[512,128]{1,0:T(8,128)S(1)}, u32[]{:S(2)}, u32[]{:S(2)}) collective-permute-start(f32[512,128]{1,0:T(8,128)} %pad_maximum_fusion), channel_id=1, source_target_pairs={{0,128},{128,0},{256,384},{384,256},{1,129},{129,1},{257,385},{385... | collective-permute-start | bytes 786440 | tf_op jit(solution)/shard_map/ppermute | solution.py:396
  36.5 11.1 %collective-permute-start.3 = (f32[632,128]{1,0:T(8,128)S(1)}, f32[632,128]{1,0:T(8,128)S(1)}, u32[]{:S(2)}, u32[]{:S(2)}) collective-permute-start(f32[632,128]{1,0:T(8,128)S(1)} %get-tuple-element.25), channel_id=1, source_target_pairs={{0,15},{1,0},{2,1},{3,2},{4,3},{5,4},{6,5},{7,6},{8,7},{9,8},{10,9... | collective-permute-start | bytes 970760 | tf_op jit(solution)/shard_map/ppermute | solution.py:393
  47.6 1.9 %collective-permute-start.4 = (f32[632,128]{1,0:T(8,128)S(1)}, f32[632,128]{1,0:T(8,128)S(1)}, u32[]{:S(2)}, u32[]{:S(2)}) collective-permute-start(f32[632,128]{1,0:T(8,128)S(1)} %get-tuple-element.26), channel_id=1, source_target_pairs={{0,1},{1,2},{2,3},{3,4},{4,5},{5,6},{6,7},{7,8},{8,9},{9,10},{10,1... | collective-permute-start | bytes 970760 | tf_op jit(solution)/shard_map/ppermute | solution.py:393
  49.6 0.1 fusion.2
  49.6 0.1 maximum_select_fusion.coef
  49.8 0.0 collective-permute-done.2.swapped
  49.8 2.4 %weights.1.wcs = f32[32,96,128]{2,1,0:T(8,128)S(1)} custom-call(f32[32,16]{1,0:T(8,128)S(1)} %maximum_select_fusion.coef, f32[928,128]{1,0:T(8,128)S(1)} %get-tuple-element.18.own, f32[256,128]{1,0:T(8,128)S(1)} %get-tuple-element.20.res_other, f32[928,128]{1,0:T(8,128)S(1)} %collective-permute-done.above, f32[928,128]{1,0:T(8,128)S(1)} %collective-permute-done.1.below, ...), custom_call_target="tpu_custom_call" | custom-call | flops 12000000 | bytes 4000000 | tf_op jit(solution)/shard_map/weights/pallas_call | solution.py:415
  52.2 2.4 %collective-permute-done.3.from_right = f32[632,128]{1,0:T(8,128)S(1)} collective-permute-done((f32[632,128]{1,0:T(8,128)S(1)}, f32[632,128]{1,0:T(8,128)S(1)}, u32[]{:S(2)}, u32[]{:S(2)}) %collective-permute-start.3) | collective-permute-done | bytes 323616 | tf_op jit(solution)/shard_map/ppermute | solution.py:393
  54.7 5.0 %collective-permute-done.4.from_left = f32[632,128]{1,0:T(8,128)S(1)} collective-permute-done((f32[632,128]{1,0:T(8,128)S(1)}, f32[632,128]{1,0:T(8,128)S(1)}, u32[]{:S(2)}, u32[]{:S(2)}) %collective-permute-start.4) | collective-permute-done | bytes 323616 | tf_op jit(solution)/shard_map/ppermute | solution.py:393
  59.7 3.0 %collective-permute-start.5 = (f32[384,128]{1,0:T(8,128)S(1)}, f32[384,128]{1,0:T(8,128)S(1)}, u32[]{:S(2)}, u32[]{:S(2)}) collective-permute-start(f32[384,128]{1,0:T(8,128)S(1)} %pad_maximum_fusion.1), channel_id=1, source_target_pairs={{0,128},{128,0},{256,384},{384,256},{1,129},{129,1},{257,385},{385... | collective-permute-start | bytes 589832 | tf_op jit(solution)/shard_map/ppermute | solution.py:396
  62.7 4.6 %forward.1.vs = f32[32,4,32,128]{3,2,1,0:T(8,128)S(1)} custom-call(f32[1]{0:T(128)} %get-tuple-element.17.scale, f32[928,128]{1,0:T(8,128)S(1)} %get-tuple-element.18.own, f32[512,128]{1,0:T(8,128)S(1)} %get-tuple-element.21.chk, f32[928,128]{1,0:T(8,128)S(1)} %collective-permute-done.above, f32[928,128]{1,0:T(8,128)S(1)} %collective-permute-done.1.below, ...), custom_call_target="tpu_custom_call" | custom-call | flops 20000000 | bytes 6000000 | tf_op jit(solution)/shard_map/forward/pallas_call | solution.py:431
  67.3 0.0 collective-permute-done.5.swapped
  67.3 9.7 %adjoint.1 = (f32[2,4,32,128]{3,2,1,0:T(8,128)}, f32[32,128]{1,0:T(8,128)S(1)}) custom-call(f32[32,16]{1,0:T(8,128)S(1)} %maximum_select_fusion.coef, f32[1]{0:T(128)} %get-tuple-element.17.scale, f32[928,128]{1,0:T(8,128)S(1)} %get-tuple-element.18.own, f32[928,128]{1,0:T(8,128)S(1)} %collective-permute-done.above, ...), custom_call_target="tpu_custom_call" | custom-call | tf_op jit(solution)/shard_map/adjoint/pallas_call | solution.py:446
  77.0 5.1 %all-gather = f32[128,128]{1,0:T(8,128)S(1)} all-gather(f32[32,128]{1,0:T(8,128)S(1)} %get-tuple-element.30), channel_id=2, replica_groups=mesh['vec'=4,'row'=8,'col'=16] {'vec'}, dimensions={0}, use_global_device_ids=true | all-gather | bytes 81920 | tf_op jit(solution)/shard_map/all_gather | solution.py:464
  82.1 0.6 reduce_sum.9
  (7 shorter events, 0.1 us)
Async XLA Ops:
  3.6 23.1 %collective-permute-start = (f32[928,128]{1,0:T(8,128)S(1)}, f32[928,128]{1,0:T(8,128)S(1)}, u32[]{:S(2)}, u32[]{:S(2)}) collective-permute-start(f32[928,128]{1,0:T(8,128)S(1)} %get-tuple-element.18.own), channel_id=1, source_target_pairs={{0,16},{16,32},{32,48},{48,64},{64,80},{80,96},{96,112},{112,0},{1... | collective-permute-start | bytes 1425416 | tf_op jit(solution)/shard_map/ppermute | solution.py:393
  9.3 22.5 %collective-permute-start.1 = (f32[928,128]{1,0:T(8,128)S(1)}, f32[928,128]{1,0:T(8,128)S(1)}, u32[]{:S(2)}, u32[]{:S(2)}) collective-permute-start(f32[928,128]{1,0:T(8,128)S(1)} %get-tuple-element.19), channel_id=1, source_target_pairs={{0,112},{16,0},{32,16},{48,32},{64,48},{80,64},{96,80},{112,96},{1... | collective-permute-start | bytes 1425416 | tf_op jit(solution)/shard_map/ppermute | solution.py:393
  32.9 16.8 %collective-permute-start.2 = (f32[512,128]{1,0:T(8,128)}, f32[512,128]{1,0:T(8,128)S(1)}, u32[]{:S(2)}, u32[]{:S(2)}) collective-permute-start(f32[512,128]{1,0:T(8,128)} %pad_maximum_fusion), channel_id=1, source_target_pairs={{0,128},{128,0},{256,384},{384,256},{1,129},{129,1},{257,385},{385... | collective-permute-start | bytes 786440 | tf_op jit(solution)/shard_map/ppermute | solution.py:396
  36.5 18.2 %collective-permute-start.3 = (f32[632,128]{1,0:T(8,128)S(1)}, f32[632,128]{1,0:T(8,128)S(1)}, u32[]{:S(2)}, u32[]{:S(2)}) collective-permute-start(f32[632,128]{1,0:T(8,128)S(1)} %get-tuple-element.25), channel_id=1, source_target_pairs={{0,15},{1,0},{2,1},{3,2},{4,3},{5,4},{6,5},{7,6},{8,7},{9,8},{10,9... | collective-permute-start | bytes 970760 | tf_op jit(solution)/shard_map/ppermute | solution.py:393
  47.6 12.0 %collective-permute-start.4 = (f32[632,128]{1,0:T(8,128)S(1)}, f32[632,128]{1,0:T(8,128)S(1)}, u32[]{:S(2)}, u32[]{:S(2)}) collective-permute-start(f32[632,128]{1,0:T(8,128)S(1)} %get-tuple-element.26), channel_id=1, source_target_pairs={{0,1},{1,2},{2,3},{3,4},{4,5},{5,6},{6,7},{7,8},{8,9},{9,10},{10,1... | collective-permute-start | bytes 970760 | tf_op jit(solution)/shard_map/ppermute | solution.py:393
  59.7 7.6 %collective-permute-start.5 = (f32[384,128]{1,0:T(8,128)S(1)}, f32[384,128]{1,0:T(8,128)S(1)}, u32[]{:S(2)}, u32[]{:S(2)}) collective-permute-start(f32[384,128]{1,0:T(8,128)S(1)} %pad_maximum_fusion.1), channel_id=1, source_target_pairs={{0,128},{128,0},{256,384},{384,256},{1,129},{129,1},{257,385},{385... | collective-permute-start | bytes 589832 | tf_op jit(solution)/shard_map/ppermute | solution.py:396

commit v5 on v4

--- a/solution.py
+++ b/solution.py
@@ -72,7 +72,7 @@
 
 def prepare_kernel(
     core, scalar, adj, bits, pot, res, chk,
-    to_below, to_above, chk_v, res_v, scale_v, bits_v, pot_v, sems
+    to_below, to_above, chk_v, res_v, bits_v, pot_v, sems
 ):
     copies = []
 
@@ -99,7 +99,6 @@
     copies[1].wait()
     pot_factor = scalar[0]
     scale = 2.0 / (4.5 + QMAX * pot_factor)
-    scale_v[0] = scale
     onsite = pot_v[...].astype(F32) * (pot_factor * scale)
     for out in (to_below, to_above):
         out[pl.ds(SGN * ROWS, 4 * ROWS), :] = signs
@@ -157,16 +156,11 @@
     return phase, EXT // 8 - phase
 
 
-def weights_kernel(coef, own, res_other, above, below, swapped, out):
+def weights_kernel(coef, own, res_other, above, below, out):
     def residuals(t):
         planes = [main_tile(own, above, below, RES + e, t) for e in range(HALF)]
-        for e in range(HALF):
-            if t < 4:
-                planes.append(tile(swapped, e * ROWS + t * 8))
-            elif t < 8:
-                planes.append(tile(res_other, e * ROWS + (t - 4) * 8))
-            else:
-                planes.append(tile(swapped, (HALF + e) * ROWS + (t - 8) * 8))
+        if 4 <= t < 8:
+            planes += [tile(res_other, e * ROWS + (t - 4) * 8) for e in range(HALF)]
         return planes
 
     for phase in range(4):
@@ -263,7 +257,7 @@
 def adjoint_kernel(
     coef, scale, own, above, below, from_right, from_left, swapped, vs, wcs,
     adj_out, grad_out,
-    xc, xh, sgc, sgh, rsh, onc, onh, whr,
+    xc, xh, sgc, sgh, rsh, onc, onh, whr, wcr,
 ):
     stencil = Stencil()
     lane = stencil.lane
@@ -295,6 +289,10 @@
         for t in range(lo, hi):
             row = pl.ds(t * 8, 8)
             whr[row, :] = weigh(factors, [rsh[e, row, :] for e in range(2 * HALF)])
+            if not 4 <= t < 8:
+                at = 4 * EXT + t * 8 + (0 if t < 4 else (HALF - 2) * ROWS)
+                planes = [tile(swapped, at + e * ROWS) for e in range(HALF)]
+                wcr[row, :] = wcs[t_term, row, :] + weigh(factors[HALF:], planes)
         for v in range(4):
             p_new, p_old = new * 4 + v, old * 4 + v
             for t, c, h, nc, nh in stencil.tiles(xc, xh, p_new, lo, hi, EXT // 8):
@@ -302,7 +300,7 @@
                 if 4 <= t < 8:
                     grads[t - 4] = grads[t - 4] + c * vs[t_term, v, pl.ds((t - 4) * 8, 8), :]
                 xc[p_old, row, :] = (
-                    wcs[t_term, row, :] * sgc[v, row, :]
+                    (wcs[t_term, row, :] if 4 <= t < 8 else wcr[row, :]) * sgc[v, row, :]
                     + (onc[row, :] * c - s * nc)
                     - xc[p_old, row, :]
                 )
@@ -352,20 +350,20 @@
     coefs = window_coefs(first_segment, energies)
     coefs = jnp.where(core == 0, coefs, jnp.roll(coefs, HALF, axis=1))
     core = core[None]
+    scale = 2.0 / (4.5 + QMAX * pot_scale)
     chk = checkpoints.reshape(FPLANES * ROWS, LANES)
     res = residual.reshape(2 * HALF * ROWS, LANES)
     send = jax.ShapeDtypeStruct((MAIN + FPLANES * FHALO, LANES), F32)
-    own, to_above, chk, res_other, scale = pl.pallas_call(
+    own, to_above, chk, res_other = pl.pallas_call(
         prepare_kernel,
         out_shape=(
             send,
             send,
             jax.ShapeDtypeStruct((FPLANES * ROWS, LANES), F32),
             jax.ShapeDtypeStruct((HALF * ROWS, LANES), F32),
-            jax.ShapeDtypeStruct((1,), F32),
         ),
         in_specs=[SMEM_SPEC] * 2 + [HBM_SPEC] * 5,
-        out_specs=(VMEM_SPEC,) * 4 + (SMEM_SPEC,),
+        out_specs=(VMEM_SPEC,) * 4,
         scratch_shapes=[
             pltpu.VMEM((4 * ROWS, LANES), jnp.int32),
             pltpu.VMEM((ROWS, LANES), jnp.int32),
@@ -407,25 +405,25 @@
         compiler_params=params(6),
         name="pack_columns",
     )(own, chk, above, below)
-    to_left, res_above, res_below = lax.optimization_barrier((to_left, above, below))
     from_left = shift(to_right, "col", 1)
     from_right = shift(to_left, "col", -1)
-    res_rows = slice(RES * ROWS, (RES + HALF) * ROWS)
-    swapped_rows = swap_cores(jnp.concatenate([res_above[res_rows], res_below[res_rows]], axis=0))
     weights = pl.pallas_call(
         weights_kernel,
         out_shape=jax.ShapeDtypeStruct((TERMS, EXT, LANES), F32),
-        in_specs=[SMEM_SPEC] + [VMEM_SPEC] * 5,
+        in_specs=[SMEM_SPEC] + [VMEM_SPEC] * 4,
         out_specs=VMEM_SPEC,
         compiler_params=params(6),
         cost_estimate=pl.CostEstimate(flops=12_000_000, bytes_accessed=4_000_000, transcendentals=0),
         name="weights",
-    )(coefs, own, res_other, above, below, swapped_rows)
+    )(coefs, own, res_other, above, below)
 
     weights, from_right, from_left = lax.optimization_barrier((weights, from_right, from_left))
     strip_rows = slice(G_RES, G_RES + 2 * EXT)
-    swapped_strips = swap_cores(
-        jnp.concatenate([from_right[strip_rows], from_left[strip_rows]], axis=0)
+    res_rows = slice(RES * ROWS, (RES + HALF) * ROWS)
+    swapped = swap_cores(
+        jnp.concatenate(
+            [from_right[strip_rows], from_left[strip_rows], above[res_rows], below[res_rows]], axis=0
+        )
     )
     frame = (FPLANES, FEXT, LANES)
     states = pl.pallas_call(
@@ -455,11 +453,11 @@
             pltpu.VMEM((8, *ext), F32), pltpu.VMEM((8, *ext), F32),
             pltpu.VMEM((4, *ext), F32), pltpu.VMEM((4, *ext), F32),
             pltpu.VMEM((2 * HALF, *ext), F32),
-            pltpu.VMEM(ext, F32), pltpu.VMEM(ext, F32), pltpu.VMEM(ext, F32),
+            pltpu.VMEM(ext, F32), pltpu.VMEM(ext, F32), pltpu.VMEM(ext, F32), pltpu.VMEM(ext, F32),
         ],
         compiler_params=params(10),
         name="adjoint",
-    )(coefs, scale, own, above, below, from_right, from_left, swapped_strips, states, weights)
+    )(coefs, scale, own, above, below, from_right, from_left, swapped, states, weights)
 
     grad = jnp.sum(lax.all_gather(grad, "vec"), axis=0)
     return grad, adjoint_out

time: 83.1 us -> 78.1 us (0.940); the launches traced: 82.7 us -> 76.6 us
  starting transfers between devices: 29.4 us -> 26.4 us
  Pallas kernels: 19.4 us -> 18 us
  waiting for transfers between devices: 24.3 us -> 23.2 us
    ppermute x2 -> x1, starting transfers between devices: 6.57 us -> 3.57 us  [swap_cores(): return lax.ppermute(value, 'vec', [(0, 1), (1, 0), (2, 3), (3, 2)])]
    ppermute x4, waiting for transfers between devices: 24.3 us -> 23.2 us  [shift(): return lax.ppermute(value, axis, [(i, (i + step) % n) for i in range(n)])]
  transfers between devices with their start and end apart: 6 -> 5, of which waited for: 4 -> 4; matrix products, arithmetic and copies ran while one was open for 1% -> 2% of each run, Pallas kernels for 8% -> 8%
where the time goes in v5:
time: 78.1 us; the launch traced here: 76.6 us
  starting transfers between devices  26.4 us (34%)
  waiting for transfers between devices  23.2 us (30%)
  Pallas kernels  18 us (23%)
  blocking collectives  5.07 us (6%)
  between operations  2.12 us (3%)
  other arithmetic  1.71 us (2%)
    ppermute x4, waiting for transfers between devices, shift(): return lax.ppermute(value, axis, [(i, (i + step) % n) for i in range(n)])  23.2 us
    ppermute x4, starting transfers between devices, shift(): return lax.ppermute(value, axis, [(i, (i + step) % n) for i in range(n)])  22.8 us
    pallas_call x1, Pallas kernels, per_device(): pl.pallas_call(adjoint_kernel, out_shape=(jax.ShapeDtypeStruct((2, 4, ROW...  9.83 us
    all_gather x1, blocking collectives, per_device(): grad = jnp.sum(lax.all_gather(grad, 'vec'), axis=0)  5.07 us
    pallas_call x1, Pallas kernels, per_device(): pl.pallas_call(forward_kernel, out_shape=jax.ShapeDtypeStruct((TERMS, 4,...  3.96 us
    ppermute x1, starting transfers between devices, swap_cores(): return lax.ppermute(value, 'vec', [(0, 1), (1, 0), (2, 3), (3, 2)])  3.57 us
    pallas_call x1, Pallas kernels, per_device(): pl.pallas_call(weights_kernel, out_shape=jax.ShapeDtypeStruct((TERMS, EXT...  2.04 us
    pallas_call x1, Pallas kernels, per_device(): pl.pallas_call(prepare_kernel, out_shape=(send, send, jax.ShapeDtypeStruc...  1.8 us
  transfers between devices with their start and end apart: 5, of which 4 were waited for; matrix products, arithmetic and copies ran while one was open for 2% of the time, Pallas kernels for 8%

profile of v5, /device:TPU:1, one launch (start us, length us, event | category | flops | bytes accessed | tf_op | source)
XLA Modules:
  0.0 76.6 jit_solution(7024899535223405473)
XLA Ops:
  1.3 1.8 %prepare.1 = (f32[928,128]{1,0:T(8,128)S(1)}, f32[928,128]{1,0:T(8,128)S(1)}, f32[512,128]{1,0:T(8,128)S(1)}, f32[256,128]{1,0:T(8,128)S(1)}) custom-call(s32[1]{0:T(128)} %bitcast.1.core, f32[1]{0:T(128)S(6)} %copy.10.scalar, f32[256,128]{1,0:T(8,128)} %bitcast.10, s32[128,128]{1,0:T(8,128)} %bitcast.11, s32[32,128]{1,0:T(8,128)} %pot.1, ...), custom_call_target="tpu_custom_call" | custom-call | tf_op jit(solution)/shard_map/prepare/pallas_call | solution.py:357
  3.1 7.8 %collective-permute-start.1 = (f32[928,128]{1,0:T(8,128)S(1)}, f32[928,128]{1,0:T(8,128)S(1)}, u32[]{:S(2)}, u32[]{:S(2)}) collective-permute-start(f32[928,128]{1,0:T(8,128)S(1)} %get-tuple-element.14), channel_id=1, source_target_pairs={{0,112},{16,0},{32,16},{48,32},{64,48},{80,64},{96,80},{112,96},{1... | collective-permute-start | bytes 1425416 | tf_op jit(solution)/shard_map/ppermute | solution.py:391
  11.0 1.9 %collective-permute-start = (f32[928,128]{1,0:T(8,128)S(1)}, f32[928,128]{1,0:T(8,128)S(1)}, u32[]{:S(2)}, u32[]{:S(2)}) collective-permute-start(f32[928,128]{1,0:T(8,128)S(1)} %get-tuple-element.13.own), channel_id=1, source_target_pairs={{0,16},{16,32},{32,48},{48,64},{64,80},{80,96},{96,112},{112,0},{1... | collective-permute-start | bytes 1425416 | tf_op jit(solution)/shard_map/ppermute | solution.py:391
  13.6 0.7 sine_multiply_fusion
  14.3 0.1 multiply_divide_fusion
  14.5 6.0 %collective-permute-done.1.below = f32[928,128]{1,0:T(8,128)S(1)} collective-permute-done((f32[928,128]{1,0:T(8,128)S(1)}, f32[928,128]{1,0:T(8,128)S(1)}, u32[]{:S(2)}, u32[]{:S(2)}) %collective-permute-start.1) | collective-permute-done | bytes 475168 | tf_op jit(solution)/shard_map/ppermute | solution.py:391
  20.5 9.9 %collective-permute-done.above = f32[928,128]{1,0:T(8,128)S(1)} collective-permute-done((f32[928,128]{1,0:T(8,128)S(1)}, f32[928,128]{1,0:T(8,128)S(1)}, u32[]{:S(2)}, u32[]{:S(2)}) %collective-permute-start) | collective-permute-done | bytes 475168 | tf_op jit(solution)/shard_map/ppermute | solution.py:391
  30.4 0.4 pack_columns.1
  30.8 11.1 %collective-permute-start.2 = (f32[632,128]{1,0:T(8,128)S(1)}, f32[632,128]{1,0:T(8,128)S(1)}, u32[]{:S(2)}, u32[]{:S(2)}) collective-permute-start(f32[632,128]{1,0:T(8,128)S(1)} %get-tuple-element.17), channel_id=1, source_target_pairs={{0,15},{1,0},{2,1},{3,2},{4,3},{5,4},{6,5},{7,6},{8,7},{9,8},{10,9... | collective-permute-start | bytes 970760 | tf_op jit(solution)/shard_map/ppermute | solution.py:391
  41.9 1.9 %collective-permute-start.3 = (f32[632,128]{1,0:T(8,128)S(1)}, f32[632,128]{1,0:T(8,128)S(1)}, u32[]{:S(2)}, u32[]{:S(2)}) collective-permute-start(f32[632,128]{1,0:T(8,128)S(1)} %get-tuple-element.18), channel_id=1, source_target_pairs={{0,1},{1,2},{2,3},{3,4},{4,5},{5,6},{6,7},{7,8},{8,9},{9,10},{10,1... | collective-permute-start | bytes 970760 | tf_op jit(solution)/shard_map/ppermute | solution.py:391
  43.9 0.1 fusion.2
  43.9 0.1 maximum_select_fusion.coef
  44.1 2.0 %weights.1.wcs = f32[32,96,128]{2,1,0:T(8,128)S(1)} custom-call(f32[32,16]{1,0:T(8,128)S(1)} %maximum_select_fusion.coef, f32[928,128]{1,0:T(8,128)S(1)} %get-tuple-element.13.own, f32[256,128]{1,0:T(8,128)S(1)} %get-tuple-element.15.res_other, f32[928,128]{1,0:T(8,128)S(1)} %collective-permute-done.above, f32[928,128]{1,0:T(8,128)S(1)} %collective-permute-done.1.below), custom_call_target="tpu_custom_call" | custom-call | flops 12000000 | bytes 4000000 | tf_op jit(solution)/shard_map/weights/pallas_call | solution.py:410
  46.2 2.3 %collective-permute-done.2.from_right = f32[632,128]{1,0:T(8,128)S(1)} collective-permute-done((f32[632,128]{1,0:T(8,128)S(1)}, f32[632,128]{1,0:T(8,128)S(1)}, u32[]{:S(2)}, u32[]{:S(2)}) %collective-permute-start.2) | collective-permute-done | bytes 323616 | tf_op jit(solution)/shard_map/ppermute | solution.py:391
  48.4 5.0 %collective-permute-done.3.from_left = f32[632,128]{1,0:T(8,128)S(1)} collective-permute-done((f32[632,128]{1,0:T(8,128)S(1)}, f32[632,128]{1,0:T(8,128)S(1)}, u32[]{:S(2)}, u32[]{:S(2)}) %collective-permute-start.3) | collective-permute-done | bytes 323616 | tf_op jit(solution)/shard_map/ppermute | solution.py:391
  53.5 3.6 %collective-permute-start.4 = (f32[896,128]{1,0:T(8,128)S(1)}, f32[896,128]{1,0:T(8,128)S(1)}, u32[]{:S(2)}, u32[]{:S(2)}) collective-permute-start(f32[896,128]{1,0:T(8,128)S(1)} %pad_maximum_fusion), channel_id=1, source_target_pairs={{0,128},{128,0},{256,384},{384,256},{1,129},{129,1},{257,385},{385... | collective-permute-start | bytes 1376264 | tf_op jit(solution)/shard_map/ppermute | solution.py:394
  57.1 4.0 %forward.1.vs = f32[32,4,32,128]{3,2,1,0:T(8,128)S(1)} custom-call(f32[1]{0:T(128)S(6)} %div.17.scale, f32[928,128]{1,0:T(8,128)S(1)} %get-tuple-element.13.own, f32[512,128]{1,0:T(8,128)S(1)} %get-tuple-element.16.chk, f32[928,128]{1,0:T(8,128)S(1)} %collective-permute-done.above, f32[928,128]{1,0:T(8,128)S(1)} %collective-permute-done.1.below, ...), custom_call_target="tpu_custom_call" | custom-call | flops 20000000 | bytes 6000000 | tf_op jit(solution)/shard_map/forward/pallas_call | solution.py:429
  61.1 0.0 collective-permute-done.4.swapped
  61.1 9.8 %adjoint.1 = (f32[2,4,32,128]{3,2,1,0:T(8,128)}, f32[32,128]{1,0:T(8,128)S(1)}) custom-call(f32[32,16]{1,0:T(8,128)S(1)} %maximum_select_fusion.coef, f32[1]{0:T(128)S(6)} %div.17.scale, f32[928,128]{1,0:T(8,128)S(1)} %get-tuple-element.13.own, f32[928,128]{1,0:T(8,128)S(1)} %collective-permute-done.above, f32[928,128]{1,0:T(8,128)S(1)} %collective-permute-done.1.below, ...), custom_call_target="tpu_custom_call" | custom-call | tf_op jit(solution)/shard_map/adjoint/pallas_call | solution.py:444
  70.9 5.1 %all-gather = f32[128,128]{1,0:T(8,128)S(1)} all-gather(f32[32,128]{1,0:T(8,128)S(1)} %get-tuple-element.22), channel_id=2, replica_groups=mesh['vec'=4,'row'=8,'col'=16] {'vec'}, dimensions={0}, use_global_device_ids=true | all-gather | bytes 81920 | tf_op jit(solution)/shard_map/all_gather | solution.py:462
  76.0 0.6 reduce_sum.9
  (7 shorter events, 0.1 us)
Async XLA Ops:
  3.1 17.4 %collective-permute-start.1 = (f32[928,128]{1,0:T(8,128)S(1)}, f32[928,128]{1,0:T(8,128)S(1)}, u32[]{:S(2)}, u32[]{:S(2)}) collective-permute-start(f32[928,128]{1,0:T(8,128)S(1)} %get-tuple-element.14), channel_id=1, source_target_pairs={{0,112},{16,0},{32,16},{48,32},{64,48},{80,64},{96,80},{112,96},{1... | collective-permute-start | bytes 1425416 | tf_op jit(solution)/shard_map/ppermute | solution.py:391
  11.0 19.5 %collective-permute-start = (f32[928,128]{1,0:T(8,128)S(1)}, f32[928,128]{1,0:T(8,128)S(1)}, u32[]{:S(2)}, u32[]{:S(2)}) collective-permute-start(f32[928,128]{1,0:T(8,128)S(1)} %get-tuple-element.13.own), channel_id=1, source_target_pairs={{0,16},{16,32},{32,48},{48,64},{64,80},{80,96},{96,112},{112,0},{1... | collective-permute-start | bytes 1425416 | tf_op jit(solution)/shard_map/ppermute | solution.py:391
  30.8 17.6 %collective-permute-start.2 = (f32[632,128]{1,0:T(8,128)S(1)}, f32[632,128]{1,0:T(8,128)S(1)}, u32[]{:S(2)}, u32[]{:S(2)}) collective-permute-start(f32[632,128]{1,0:T(8,128)S(1)} %get-tuple-element.17), channel_id=1, source_target_pairs={{0,15},{1,0},{2,1},{3,2},{4,3},{5,4},{6,5},{7,6},{8,7},{9,8},{10,9... | collective-permute-start | bytes 970760 | tf_op jit(solution)/shard_map/ppermute | solution.py:391
  41.9 11.5 %collective-permute-start.3 = (f32[632,128]{1,0:T(8,128)S(1)}, f32[632,128]{1,0:T(8,128)S(1)}, u32[]{:S(2)}, u32[]{:S(2)}) collective-permute-start(f32[632,128]{1,0:T(8,128)S(1)} %get-tuple-element.18), channel_id=1, source_target_pairs={{0,1},{1,2},{2,3},{3,4},{4,5},{5,6},{6,7},{7,8},{8,9},{9,10},{10,1... | collective-permute-start | bytes 970760 | tf_op jit(solution)/shard_map/ppermute | solution.py:391
  53.5 7.6 %collective-permute-start.4 = (f32[896,128]{1,0:T(8,128)S(1)}, f32[896,128]{1,0:T(8,128)S(1)}, u32[]{:S(2)}, u32[]{:S(2)}) collective-permute-start(f32[896,128]{1,0:T(8,128)S(1)} %pad_maximum_fusion), channel_id=1, source_target_pairs={{0,128},{128,0},{256,384},{384,256},{1,129},{129,1},{257,385},{385... | collective-permute-start | bytes 1376264 | tf_op jit(solution)/shard_map/ppermute | solution.py:394

commit v6 on v5

--- a/solution.py
+++ b/solution.py
@@ -28,10 +28,13 @@
 MAIN = PLANES * ROWS
 WIDE = EXT // 8
 GROUPS = 5
-G_RES = 3 * EXT
-G_ADJ = GROUPS * EXT
-G_ONS = EXT // 4
-G_ROWS = G_ADJ + G_ONS + 2 * FEXT
+RES_GROUP = 3
+OWN_ONS = GROUPS * ROWS
+OWN_CHK = OWN_ONS + 8
+OWN_ROWS = OWN_CHK + 2 * ROWS
+EDGE_ONS = GROUPS * 2 * HALO
+EDGE_CHK = EDGE_ONS + 16
+EDGE_ROWS = EDGE_CHK + 4 * FHALO
 
 
 def window_coefs(first_segment, energies):
@@ -107,38 +110,90 @@
         copy.wait()
 
 
-def pack_kernel(own, chk, above, below, to_left, to_right):
+def pack(tiles, row, to_left, to_right):
     lane = lane_iota()
-
-    def pack(tiles, row):
-        count = len(tiles)
-        width = LANES // count
-        group = lane // width
-        left = right = None
-        for j, value in enumerate(tiles):
-            rolled = pltpu.roll(value, width * j, 1) if j else value
-            left = rolled if j == 0 else jnp.where(group == j, rolled, left)
-            right = rolled if j == 0 else jnp.where(group == (j + count - 1) % count, rolled, right)
-        to_left[pl.ds(row, 8), :] = left
-        to_right[pl.ds(row, 8), :] = right
-
+    count = len(tiles)
+    width = LANES // count
+    group = lane // width
+    left = right = None
+    for j, value in enumerate(tiles):
+        rolled = pltpu.roll(value, width * j, 1) if j else value
+        left = rolled if j == 0 else jnp.where(group == j, rolled, left)
+        right = rolled if j == 0 else jnp.where(group == (j + count - 1) % count, rolled, right)
+    to_left[pl.ds(row, 8), :] = left
+    to_right[pl.ds(row, 8), :] = right
+
+
+def pack_own_kernel(own, chk, to_left, to_right):
     for g in range(GROUPS):
-        for t in range(EXT // 8):
-            pack([main_tile(own, above, below, 4 * g + j, t) for j in range(4)], g * EXT + t * 8)
-    for m in range(3):
-        pack([main_tile(own, above, below, ONS, 3 * j + m) for j in range(4)], G_ADJ + m * 8)
+        for i in range(4):
+            tiles = [tile(own, (4 * g + j) * ROWS + i * 8) for j in range(4)]
+            pack(tiles, g * ROWS + i * 8, to_left, to_right)
+    pack([tile(own, ONS * ROWS + j * 8) for j in range(4)], OWN_ONS, to_left, to_right)
     for g in range(2):
-        for t in range(FEXT // 8):
-            pack(
-                [fwd_tile(chk, above, below, 8 * g + j, t) for j in range(8)],
-                G_ADJ + G_ONS + g * FEXT + t * 8,
-            )
-
-
-def unpack_strip(from_right, from_left, lane, right_row, left_row, j, count):
+        for i in range(4):
+            tiles = [tile(chk, (8 * g + j) * ROWS + i * 8) for j in range(8)]
+            pack(tiles, OWN_CHK + g * ROWS + i * 8, to_left, to_right)
+
+
+def pack_edge_kernel(above, below, to_left, to_right):
+    for side, ref in enumerate((above, below)):
+        for g in range(GROUPS):
+            for i in range(4):
+                tiles = [tile(ref, (4 * g + j) * ROWS + i * 8) for j in range(4)]
+                pack(tiles, g * 2 * HALO + side * HALO + i * 8, to_left, to_right)
+        tiles = [tile(ref, ONS * ROWS + j * 8) for j in range(4)]
+        pack(tiles, EDGE_ONS + side * 8, to_left, to_right)
+        for g in range(2):
+            for i in range(2):
+                tiles = [tile(ref, MAIN + (8 * g + j) * FHALO + i * 8) for j in range(8)]
+                pack(tiles, EDGE_CHK + g * 2 * FHALO + side * FHALO + i * 8, to_left, to_right)
+
+
+def unpack_strip(right, left, lane, j, count):
     width = LANES // count
-    mixed = jnp.where(lane // width == j, tile(from_right, right_row), tile(from_left, left_row))
+    mixed = jnp.where(lane // width == j, tile(*right), tile(*left))
     return pltpu.roll(mixed, (LANES - width * j) % LANES, 1) if j else mixed
+
+
+class Strips:
+    def __init__(self, own_right, own_left, edge_right, edge_left, lane):
+        self.own, self.edge, self.lane = (own_right, own_left), (edge_right, edge_left), lane
+
+    def unpack(self, refs, row, j, count):
+        return unpack_strip((refs[0], row), (refs[1], row), self.lane, j, count)
+
+    def plane(self, index, t):
+        g, j = index // 4, index % 4
+        if 4 <= t < 8:
+            return self.unpack(self.own, g * ROWS + (t - 4) * 8, j, 4)
+        return self.unpack(self.edge, g * 2 * HALO + (t if t < 4 else t - 4) * 8, j, 4)
+
+    def onsite(self, t):
+        if 4 <= t < 8:
+            return self.unpack(self.own, OWN_ONS, t - 4, 4)
+        return self.unpack(self.edge, EDGE_ONS + t // 8 * 8, t % 4, 4)
+
+    def checkpoint(self, plane, t):
+        g, j = plane // 8, plane % 8
+        if 2 <= t < 6:
+            return self.unpack(self.own, OWN_CHK + g * ROWS + (t - 2) * 8, j, 8)
+        at = EDGE_CHK + g * 2 * FHALO + (t if t < 2 else t - 4) * 8
+        return self.unpack(self.edge, at, j, 8)
+
+
+SWAP_OWN, SWAP_EDGE = 2 * ROWS, 4 * HALO
+SWAP_SIDE = SWAP_OWN + SWAP_EDGE
+SWAP_MAIN = 2 * SWAP_SIDE
+
+
+def swapped_strip(swapped, lane, e, t):
+    g, j = e // 4, e % 4
+    if 4 <= t < 8:
+        row = g * ROWS + (t - 4) * 8
+    else:
+        row = SWAP_OWN + g * 2 * HALO + (t if t < 4 else t - 4) * 8
+    return unpack_strip((swapped, row), (swapped, SWAP_SIDE + row), lane, j, 4)
 
 
 def splats(coef, t_term):
@@ -210,20 +265,21 @@
             here, prev_up, here_up, here_down = after, here_up, after_up, after_down
 
 
-def forward_kernel(scale, own, chk, above, below, from_right, from_left, vs, fc, fh, onc, onh):
+def forward_kernel(
+    scale, own, chk, above, below, own_right, own_left, edge_right, edge_left,
+    vs, fc, fh, onc, onh,
+):
     stencil = Stencil()
-    lane = stencil.lane
+    strips = Strips(own_right, own_left, edge_right, edge_left, stencil.lane)
     s = jnp.full((8, LANES), scale[0], F32)
     for t in range(FEXT // 8):
         row = pl.ds(t * 8, 8)
         for plane in range(FPLANES):
-            at = G_ADJ + G_ONS + (plane // 8) * FEXT + t * 8
             fc[plane, row, :] = fwd_tile(chk, above, below, plane, t)
-            fh[plane, row, :] = unpack_strip(from_right, from_left, lane, at, at, plane % 8, 8)
+            fh[plane, row, :] = strips.checkpoint(plane, t)
         e = t + (HALO - FHALO) // 8
-        at = G_ADJ + (e % 3) * 8
         onc[row, :] = main_tile(own, above, below, ONS, e)
-        onh[row, :] = unpack_strip(from_right, from_left, lane, at, at, e // 3, 4)
+        onh[row, :] = strips.onsite(e)
     for segment in range(2):
         for which in range(2):
             for v in range(4):
@@ -255,33 +311,27 @@
 
 
 def adjoint_kernel(
-    coef, scale, own, above, below, from_right, from_left, swapped, vs, wcs,
+    coef, scale, own, above, below, own_right, own_left, edge_right, edge_left, swapped, vs, wcs,
     adj_out, grad_out,
     xc, xh, sgc, sgh, rsh, onc, onh, whr, wcr,
 ):
     stencil = Stencil()
-    lane = stencil.lane
+    strips = Strips(own_right, own_left, edge_right, edge_left, stencil.lane)
     s = jnp.full((8, LANES), scale[0], F32)
-
-    def strip(row, j, count):
-        return unpack_strip(from_right, from_left, lane, row, row, j, count)
 
     for t in range(EXT // 8):
         row = pl.ds(t * 8, 8)
         for plane in range(8):
             xc[plane, row, :] = main_tile(own, above, below, plane, t)
-            xh[plane, row, :] = strip((plane // 4) * EXT + t * 8, plane % 4, 4)
+            xh[plane, row, :] = strips.plane(plane, t)
         for v in range(4):
             sgc[v, row, :] = main_tile(own, above, below, SGN + v, t)
-            sgh[v, row, :] = strip(2 * EXT + t * 8, v, 4)
+            sgh[v, row, :] = strips.plane(SGN + v, t)
         for e in range(HALF):
-            at = (e // 4) * EXT + t * 8
-            rsh[e, row, :] = strip(G_RES + at, e % 4, 4)
-            rsh[HALF + e, row, :] = unpack_strip(
-                swapped, swapped, lane, at, 2 * EXT + at, e % 4, 4
-            )
+            rsh[e, row, :] = strips.plane(RES + e, t)
+            rsh[HALF + e, row, :] = swapped_strip(swapped, stencil.lane, e, t)
         onc[row, :] = main_tile(own, above, below, ONS, t)
-        onh[row, :] = strip(G_ADJ + (t % 3) * 8, t // 3, 4)
+        onh[row, :] = strips.onsite(t)
 
     def adjoint(t_term, new, old, lo, hi, grads):
         grads = list(grads)
@@ -290,7 +340,7 @@
             row = pl.ds(t * 8, 8)
             whr[row, :] = weigh(factors, [rsh[e, row, :] for e in range(2 * HALF)])
             if not 4 <= t < 8:
-                at = 4 * EXT + t * 8 + (0 if t < 4 else (HALF - 2) * ROWS)
+                at = SWAP_MAIN + t * 8 + (0 if t < 4 else (HALF - 2) * ROWS)
                 planes = [tile(swapped, at + e * ROWS) for e in range(HALF)]
                 wcr[row, :] = wcs[t_term, row, :] + weigh(factors[HALF:], planes)
         for v in range(4):
@@ -396,17 +446,21 @@
     above = shift(own, "row", 1)
     below = shift(to_above, "row", -1)
 
-    strips = jax.ShapeDtypeStruct((G_ROWS, LANES), F32)
-    to_left, to_right = pl.pallas_call(
-        pack_kernel,
-        out_shape=(strips, strips),
-        in_specs=[VMEM_SPEC] * 4,
-        out_specs=(VMEM_SPEC,) * 2,
-        compiler_params=params(6),
-        name="pack_columns",
-    )(own, chk, above, below)
-    from_left = shift(to_right, "col", 1)
-    from_right = shift(to_left, "col", -1)
+    def packed(kernel, rows, name, *values):
+        shape = jax.ShapeDtypeStruct((rows, LANES), F32)
+        to_left, to_right = pl.pallas_call(
+            kernel,
+            out_shape=(shape, shape),
+            in_specs=[VMEM_SPEC] * len(values),
+            out_specs=(VMEM_SPEC,) * 2,
+            compiler_params=params(6),
+            name=name,
+        )(*values)
+        return shift(to_left, "col", -1), shift(to_right, "col", 1)
+
+    coefs, late_own, late_chk = lax.optimization_barrier((coefs, own, chk))
+    own_strips = packed(pack_own_kernel, OWN_ROWS, "pack_own", late_own, late_chk)
+    edge_strips = packed(pack_edge_kernel, EDGE_ROWS, "pack_edge", above, below)
     weights = pl.pallas_call(
         weights_kernel,
         out_shape=jax.ShapeDtypeStruct((TERMS, EXT, LANES), F32),
@@ -417,19 +471,25 @@
         name="weights",
     )(coefs, own, res_other, above, below)
 
-    weights, from_right, from_left = lax.optimization_barrier((weights, from_right, from_left))
-    strip_rows = slice(G_RES, G_RES + 2 * EXT)
+    weights, edge_strips = lax.optimization_barrier((weights, edge_strips))
     res_rows = slice(RES * ROWS, (RES + HALF) * ROWS)
+    own_rows = slice(RES_GROUP * ROWS, GROUPS * ROWS)
+    edge_rows = slice(RES_GROUP * 2 * HALO, GROUPS * 2 * HALO)
     swapped = swap_cores(
         jnp.concatenate(
-            [from_right[strip_rows], from_left[strip_rows], above[res_rows], below[res_rows]], axis=0
+            [
+                own_strips[0][own_rows], edge_strips[0][edge_rows],
+                own_strips[1][own_rows], edge_strips[1][edge_rows],
+                above[res_rows], below[res_rows],
+            ],
+            axis=0,
         )
     )
     frame = (FPLANES, FEXT, LANES)
     states = pl.pallas_call(
         forward_kernel,
         out_shape=jax.ShapeDtypeStruct((TERMS, 4, ROWS, LANES), F32),
-        in_specs=[SMEM_SPEC] + [VMEM_SPEC] * 6,
+        in_specs=[SMEM_SPEC] + [VMEM_SPEC] * 8,
         out_specs=VMEM_SPEC,
         scratch_shapes=[
             pltpu.VMEM(frame, F32), pltpu.VMEM(frame, F32),
@@ -438,7 +498,7 @@
         compiler_params=params(8),
         cost_estimate=pl.CostEstimate(flops=20_000_000, bytes_accessed=6_000_000, transcendentals=0),
         name="forward",
-    )(scale, own, chk, above, below, from_right, from_left)
+    )(scale, own, chk, above, below, *own_strips, *edge_strips)
 
     ext = (EXT, LANES)
     adjoint_out, grad = pl.pallas_call(
@@ -447,7 +507,7 @@
             jax.ShapeDtypeStruct((2, 4, ROWS, LANES), F32),
             jax.ShapeDtypeStruct((ROWS, LANES), F32),
         ),
-        in_specs=[SMEM_SPEC, SMEM_SPEC] + [VMEM_SPEC] * 8,
+        in_specs=[SMEM_SPEC, SMEM_SPEC] + [VMEM_SPEC] * 10,
         out_specs=(VMEM_SPEC, VMEM_SPEC),
         scratch_shapes=[
             pltpu.VMEM((8, *ext), F32), pltpu.VMEM((8, *ext), F32),
@@ -457,7 +517,9 @@
         ],
         compiler_params=params(10),
         name="adjoint",
-    )(coefs, scale, own, above, below, from_right, from_left, swapped, states, weights)
+    )(
+        coefs, scale, own, above, below, *own_strips, *edge_strips, swapped, states, weights
+    )
 
     grad = jnp.sum(lax.all_gather(grad, "vec"), axis=0)
     return grad, adjoint_out

time: 78.1 us -> 75.2 us (0.963)
  the two profiles are of different devices: /device:TPU:1 before, /device:TPU:23 now
where the time goes in v6:
time: 75.2 us; the launch traced here: 74.8 us
  starting transfers between devices  38.6 us (51%)
  Pallas kernels  17.7 us (24%)
  waiting for transfers between devices  9.49 us (13%)
  blocking collectives  5.07 us (7%)
  between operations  2.18 us (3%)
  other arithmetic  1.68 us (2%)
    ppermute x6, starting transfers between devices, shift(): return lax.ppermute(value, axis, [(i, (i + step) % n) for i in range(n)])  35 us
    pallas_call x1, Pallas kernels, per_device(): pl.pallas_call(adjoint_kernel, out_shape=(jax.ShapeDtypeStruct((2, 4, ROW...  9.55 us
    ppermute x6, waiting for transfers between devices, shift(): return lax.ppermute(value, axis, [(i, (i + step) % n) for i in range(n)])  9.49 us
    all_gather x1, blocking collectives, per_device(): grad = jnp.sum(lax.all_gather(grad, 'vec'), axis=0)  5.07 us
    pallas_call x1, Pallas kernels, per_device(): pl.pallas_call(forward_kernel, out_shape=jax.ShapeDtypeStruct((TERMS, 4,...  3.97 us
    ppermute x1, starting transfers between devices, swap_cores(): return lax.ppermute(value, 'vec', [(0, 1), (1, 0), (2, 3), (3, 2)])  3.57 us
    pallas_call x1, Pallas kernels, per_device(): pl.pallas_call(weights_kernel, out_shape=jax.ShapeDtypeStruct((TERMS, EXT...  1.97 us
    pallas_call x1, Pallas kernels, per_device(): pl.pallas_call(prepare_kernel, out_shape=(send, send, jax.ShapeDtypeStruc...  1.8 us
  transfers between devices with their start and end apart: 7, of which 2 were waited for; matrix products, arithmetic and copies ran while one was open for 2% of the time, Pallas kernels for 9%

profile of v6, /device:TPU:23, one launch (start us, length us, event | category | flops | bytes accessed | tf_op | source)
XLA Modules:
  0.0 74.8 jit_solution(16261602537145376581)
XLA Ops:
  1.3 1.8 %prepare.1 = (f32[928,128]{1,0:T(8,128)S(1)}, f32[928,128]{1,0:T(8,128)S(1)}, f32[512,128]{1,0:T(8,128)S(1)}, f32[256,128]{1,0:T(8,128)S(1)}) custom-call(s32[1]{0:T(128)} %bitcast.1.core, f32[1]{0:T(128)S(6)} %copy.15.scalar, f32[256,128]{1,0:T(8,128)} %bitcast.10, s32[128,128]{1,0:T(8,128)} %bitcast.11, s32[32,128]{1,0:T(8,128)} %pot.1, ...), custom_call_target="tpu_custom_call" | custom-call | tf_op jit(solution)/shard_map/prepare/pallas_call | solution.py:407
  3.1 2.0 %collective-permute-start.1 = (f32[928,128]{1,0:T(8,128)S(1)}, f32[928,128]{1,0:T(8,128)S(1)}, u32[]{:S(2)}, u32[]{:S(2)}) collective-permute-start(f32[928,128]{1,0:T(8,128)S(1)} %get-tuple-element.21), channel_id=1, source_target_pairs={{0,112},{16,0},{32,16},{48,32},{64,48},{80,64},{96,80},{112,96},{1... | collective-permute-start | bytes 1425416 | tf_op jit(solution)/shard_map/ppermute | solution.py:441
  5.1 6.9 %collective-permute-start = (f32[928,128]{1,0:T(8,128)S(1)}, f32[928,128]{1,0:T(8,128)S(1)}, u32[]{:S(2)}, u32[]{:S(2)}) collective-permute-start(f32[928,128]{1,0:T(8,128)S(1)} %get-tuple-element.22.own), channel_id=1, source_target_pairs={{0,16},{16,32},{32,48},{48,64},{64,80},{80,96},{96,112},{112,0},{1... | collective-permute-start | bytes 1425416 | tf_op jit(solution)/shard_map/ppermute | solution.py:441
  12.7 0.7 sine_multiply_fusion
  13.5 0.1 multiply_divide_fusion
  13.6 0.1 fusion.2
  13.7 0.1 maximum_select_fusion.coef
  13.8 0.2 pack_own.1
  14.0 11.1 %collective-permute-start.2 = (f32[232,128]{1,0:T(8,128)S(1)}, f32[232,128]{1,0:T(8,128)S(1)}, u32[]{:S(2)}, u32[]{:S(2)}) collective-permute-start(f32[232,128]{1,0:T(8,128)S(1)} %get-tuple-element.24), channel_id=1, source_target_pairs={{0,15},{1,0},{2,1},{3,2},{4,3},{5,4},{6,5},{7,6},{8,7},{9,8},{10,9... | collective-permute-start | bytes 356360 | tf_op jit(solution)/shard_map/ppermute | solution.py:441
  25.2 1.9 %collective-permute-start.3 = (f32[232,128]{1,0:T(8,128)S(1)}, f32[232,128]{1,0:T(8,128)S(1)}, u32[]{:S(2)}, u32[]{:S(2)}) collective-permute-start(f32[232,128]{1,0:T(8,128)S(1)} %get-tuple-element.25), channel_id=1, source_target_pairs={{0,1},{1,2},{2,3},{3,4},{4,5},{5,6},{6,7},{7,8},{8,9},{9,10},{10,1... | collective-permute-start | bytes 356360 | tf_op jit(solution)/shard_map/ppermute | solution.py:441
  27.1 0.0 collective-permute-done.1.below
  27.1 4.5 %collective-permute-done.above = f32[928,128]{1,0:T(8,128)S(1)} collective-permute-done((f32[928,128]{1,0:T(8,128)S(1)}, f32[928,128]{1,0:T(8,128)S(1)}, u32[]{:S(2)}, u32[]{:S(2)}) %collective-permute-start) | collective-permute-done | bytes 475168 | tf_op jit(solution)/shard_map/ppermute | solution.py:441
  31.6 0.3 pack_edge.1
  31.8 11.1 %collective-permute-start.4 = (f32[400,128]{1,0:T(8,128)S(1)}, f32[400,128]{1,0:T(8,128)S(1)}, u32[]{:S(2)}, u32[]{:S(2)}) collective-permute-start(f32[400,128]{1,0:T(8,128)S(1)} %get-tuple-element.27), channel_id=1, source_target_pairs={{0,15},{1,0},{2,1},{3,2},{4,3},{5,4},{6,5},{7,6},{8,7},{9,8},{10,9... | collective-permute-start | bytes 614408 | tf_op jit(solution)/shard_map/ppermute | solution.py:441
  43.0 1.9 %collective-permute-start.5 = (f32[400,128]{1,0:T(8,128)S(1)}, f32[400,128]{1,0:T(8,128)S(1)}, u32[]{:S(2)}, u32[]{:S(2)}) collective-permute-start(f32[400,128]{1,0:T(8,128)S(1)} %get-tuple-element.28), channel_id=1, source_target_pairs={{0,1},{1,2},{2,3},{3,4},{4,5},{5,6},{6,7},{7,8},{8,9},{9,10},{10,1... | collective-permute-start | bytes 614408 | tf_op jit(solution)/shard_map/ppermute | solution.py:441
  44.9 0.0 collective-permute-done.2.own_right
  44.9 2.0 %weights.1.wcs = f32[32,96,128]{2,1,0:T(8,128)S(1)} custom-call(f32[32,16]{1,0:T(8,128)S(1)} %maximum_select_fusion.coef, f32[928,128]{1,0:T(8,128)S(1)} %get-tuple-element.22.own, f32[256,128]{1,0:T(8,128)S(1)} %get-tuple-element.26.res_other, f32[928,128]{1,0:T(8,128)S(1)} %collective-permute-done.above, f32[928,128]{1,0:T(8,128)S(1)} %collective-permute-done.1.below), custom_call_target="tpu_custom_call" | custom-call | flops 12000000 | bytes 4000000 | tf_op jit(solution)/shard_map/weights/pallas_call | solution.py:464
  46.9 0.0 collective-permute-done.4.edge_right
  46.9 5.0 %collective-permute-done.5.edge_left = f32[400,128]{1,0:T(8,128)S(1)} collective-permute-done((f32[400,128]{1,0:T(8,128)S(1)}, f32[400,128]{1,0:T(8,128)S(1)}, u32[]{:S(2)}, u32[]{:S(2)}) %collective-permute-start.5) | collective-permute-done | bytes 204832 | tf_op jit(solution)/shard_map/ppermute | solution.py:441
  51.9 0.0 collective-permute-done.3.own_left
  52.0 3.6 %collective-permute-start.6 = (f32[896,128]{1,0:T(8,128)S(1)}, f32[896,128]{1,0:T(8,128)S(1)}, u32[]{:S(2)}, u32[]{:S(2)}) collective-permute-start(f32[896,128]{1,0:T(8,128)S(1)} %slice_dynamic-update-slice_fusion), channel_id=1, source_target_pairs={{0,128},{128,0},{256,384},{384,256},{1,129},{129,1},{257,385},{385... | collective-permute-start | bytes 1376264 | tf_op jit(solution)/shard_map/ppermute | solution.py:444
  55.6 4.0 %forward.1.vs = f32[32,4,32,128]{3,2,1,0:T(8,128)S(1)} custom-call(f32[1]{0:T(128)S(6)} %div.17.scale, f32[928,128]{1,0:T(8,128)S(1)} %get-tuple-element.22.own, f32[512,128]{1,0:T(8,128)S(1)} %get-tuple-element.23.chk, f32[928,128]{1,0:T(8,128)S(1)} %collective-permute-done.above, f32[928,128]{1,0:T(8,128)S(1)} %collective-permute-done.1.below, ...), custom_call_target="tpu_custom_call" | custom-call | flops 20000000 | bytes 6000000 | tf_op jit(solution)/shard_map/forward/pallas_call | solution.py:489
  59.6 0.0 collective-permute-done.6.swapped
  59.6 9.6 %adjoint.1 = (f32[2,4,32,128]{3,2,1,0:T(8,128)}, f32[32,128]{1,0:T(8,128)S(1)}) custom-call(f32[32,16]{1,0:T(8,128)S(1)} %maximum_select_fusion.coef, f32[1]{0:T(128)S(6)} %div.17.scale, f32[928,128]{1,0:T(8,128)S(1)} %get-tuple-element.22.own, f32[928,128]{1,0:T(8,128)S(1)} %collective-permute-done.above, f32[928,128]{1,0:T(8,128)S(1)} %collective-permute-done.1.below, ...), custom_call_target="tpu_custom_call" | custom-call | tf_op jit(solution)/shard_map/adjoint/pallas_call | solution.py:504
  69.1 5.1 %all-gather = f32[128,128]{1,0:T(8,128)S(1)} all-gather(f32[32,128]{1,0:T(8,128)S(1)} %get-tuple-element.32), channel_id=2, replica_groups=mesh['vec'=4,'row'=8,'col'=16] {'vec'}, dimensions={0}, use_global_device_ids=true | all-gather | bytes 81920 | tf_op jit(solution)/shard_map/all_gather | solution.py:524
  74.2 0.6 reduce_sum.9
  (8 shorter events, 0.1 us)
Async XLA Ops:
  3.1 24.0 %collective-permute-start.1 = (f32[928,128]{1,0:T(8,128)S(1)}, f32[928,128]{1,0:T(8,128)S(1)}, u32[]{:S(2)}, u32[]{:S(2)}) collective-permute-start(f32[928,128]{1,0:T(8,128)S(1)} %get-tuple-element.21), channel_id=1, source_target_pairs={{0,112},{16,0},{32,16},{48,32},{64,48},{80,64},{96,80},{112,96},{1... | collective-permute-start | bytes 1425416 | tf_op jit(solution)/shard_map/ppermute | solution.py:441
  5.1 26.5 %collective-permute-start = (f32[928,128]{1,0:T(8,128)S(1)}, f32[928,128]{1,0:T(8,128)S(1)}, u32[]{:S(2)}, u32[]{:S(2)}) collective-permute-start(f32[928,128]{1,0:T(8,128)S(1)} %get-tuple-element.22.own), channel_id=1, source_target_pairs={{0,16},{16,32},{32,48},{48,64},{64,80},{80,96},{96,112},{112,0},{1... | collective-permute-start | bytes 1425416 | tf_op jit(solution)/shard_map/ppermute | solution.py:441
  14.0 30.9 %collective-permute-start.2 = (f32[232,128]{1,0:T(8,128)S(1)}, f32[232,128]{1,0:T(8,128)S(1)}, u32[]{:S(2)}, u32[]{:S(2)}) collective-permute-start(f32[232,128]{1,0:T(8,128)S(1)} %get-tuple-element.24), channel_id=1, source_target_pairs={{0,15},{1,0},{2,1},{3,2},{4,3},{5,4},{6,5},{7,6},{8,7},{9,8},{10,9... | collective-permute-start | bytes 356360 | tf_op jit(solution)/shard_map/ppermute | solution.py:441
  25.2 26.8 %collective-permute-start.3 = (f32[232,128]{1,0:T(8,128)S(1)}, f32[232,128]{1,0:T(8,128)S(1)}, u32[]{:S(2)}, u32[]{:S(2)}) collective-permute-start(f32[232,128]{1,0:T(8,128)S(1)} %get-tuple-element.25), channel_id=1, source_target_pairs={{0,1},{1,2},{2,3},{3,4},{4,5},{5,6},{6,7},{7,8},{8,9},{9,10},{10,1... | collective-permute-start | bytes 356360 | tf_op jit(solution)/shard_map/ppermute | solution.py:441
  31.8 15.1 %collective-permute-start.4 = (f32[400,128]{1,0:T(8,128)S(1)}, f32[400,128]{1,0:T(8,128)S(1)}, u32[]{:S(2)}, u32[]{:S(2)}) collective-permute-start(f32[400,128]{1,0:T(8,128)S(1)} %get-tuple-element.27), channel_id=1, source_target_pairs={{0,15},{1,0},{2,1},{3,2},{4,3},{5,4},{6,5},{7,6},{8,7},{9,8},{10,9... | collective-permute-start | bytes 614408 | tf_op jit(solution)/shard_map/ppermute | solution.py:441
  43.0 8.9 %collective-permute-start.5 = (f32[400,128]{1,0:T(8,128)S(1)}, f32[400,128]{1,0:T(8,128)S(1)}, u32[]{:S(2)}, u32[]{:S(2)}) collective-permute-start(f32[400,128]{1,0:T(8,128)S(1)} %get-tuple-element.28), channel_id=1, source_target_pairs={{0,1},{1,2},{2,3},{3,4},{4,5},{5,6},{6,7},{7,8},{8,9},{9,10},{10,1... | collective-permute-start | bytes 614408 | tf_op jit(solution)/shard_map/ppermute | solution.py:441
  52.0 7.6 %collective-permute-start.6 = (f32[896,128]{1,0:T(8,128)S(1)}, f32[896,128]{1,0:T(8,128)S(1)}, u32[]{:S(2)}, u32[]{:S(2)}) collective-permute-start(f32[896,128]{1,0:T(8,128)S(1)} %slice_dynamic-update-slice_fusion), channel_id=1, source_target_pairs={{0,128},{128,0},{256,384},{384,256},{1,129},{129,1},{257,385},{385... | collective-permute-start | bytes 1376264 | tf_op jit(solution)/shard_map/ppermute | solution.py:444

commit v7 on v6

--- a/solution.py
+++ b/solution.py
@@ -211,24 +211,33 @@
     return phase, EXT // 8 - phase
 
 
-def weights_kernel(coef, own, res_other, above, below, out):
-    def residuals(t):
-        planes = [main_tile(own, above, below, RES + e, t) for e in range(HALF)]
-        if 4 <= t < 8:
-            planes += [tile(res_other, e * ROWS + (t - 4) * 8) for e in range(HALF)]
-        return planes
-
-    for phase in range(4):
-        lo, hi = phase_tiles(phase)
-
-        def body(i, carry, phase=phase, lo=lo, hi=hi):
-            t_term = TERMS - 8 * (phase + 1) + i
-            factors = splats(coef, t_term)
-            for t in range(lo, hi):
-                out[t_term, pl.ds(t * 8, 8), :] = weigh(factors, residuals(t))
-            return carry
-
-        lax.fori_loop(0, 8, body, 0)
+def weights_kernel(coef, own, res_other, out):
+    def body(t_term, carry):
+        factors = splats(coef, t_term)
+        for i in range(4):
+            planes = [tile(own, (RES + e) * ROWS + i * 8) for e in range(HALF)]
+            planes += [tile(res_other, e * ROWS + i * 8) for e in range(HALF)]
+            out[t_term, pl.ds(i * 8, 8), :] = weigh(factors, planes)
+        return carry
+
+    lax.fori_loop(0, TERMS, body, 0)
+
+
+def weigh_stacks(high, low, stacks, out, t):
+    first = TERMS - 8 * (min(t, 3) + 1)
+    rows = slice(8 * first, 8 * TERMS)
+    stack = jnp.concatenate([jnp.concatenate(stack, axis=0) for stack in stacks], axis=1)
+    upper = stack.astype(jnp.bfloat16)
+    lower = (stack - upper.astype(F32)).astype(jnp.bfloat16)
+
+    def product(x, y):
+        return jnp.dot(x[rows, :], y, preferred_element_type=F32)
+
+    result = product(high, upper) + (product(high, lower) + product(low, upper))
+    for n in range(first, TERMS):
+        part = result[8 * (n - first) : 8 * (n - first) + 8]
+        out[n, pl.ds(t * 8, 8), :] = part[:, :LANES]
+        out[n, pl.ds(EXT - 8 - t * 8, 8), :] = part[:, LANES:]
 
 
 class Stencil:
@@ -311,9 +320,10 @@
 
 
 def adjoint_kernel(
-    coef, scale, own, above, below, own_right, own_left, edge_right, edge_left, swapped, vs, wcs,
+    scale, high, low, own, above, below, own_right, own_left, edge_right, edge_left, swapped,
+    vs, own_weights,
     adj_out, grad_out,
-    xc, xh, sgc, sgh, rsh, onc, onh, whr, wcr,
+    xc, xh, sgc, sgh, onc, onh, wcs, whs,
 ):
     stencil = Stencil()
     strips = Strips(own_right, own_left, edge_right, edge_left, stencil.lane)
@@ -327,35 +337,44 @@
         for v in range(4):
             sgc[v, row, :] = main_tile(own, above, below, SGN + v, t)
             sgh[v, row, :] = strips.plane(SGN + v, t)
-        for e in range(HALF):
-            rsh[e, row, :] = strips.plane(RES + e, t)
-            rsh[HALF + e, row, :] = swapped_strip(swapped, stencil.lane, e, t)
         onc[row, :] = main_tile(own, above, below, ONS, t)
         onh[row, :] = strips.onsite(t)
 
+    def halo_stack(t):
+        return [strips.plane(RES + e, t) for e in range(HALF)] + [
+            swapped_strip(swapped, stencil.lane, e, t) for e in range(HALF)
+        ]
+
+    def centre_stack(t):
+        at = SWAP_MAIN + t * 8 + (0 if t < 4 else (HALF - 2) * ROWS)
+        return [main_tile(own, above, below, RES + e, t) for e in range(HALF)] + [
+            tile(swapped, at + e * ROWS) for e in range(HALF)
+        ]
+
+    for t in range(EXT // 16):
+        other = EXT // 8 - 1 - t
+        weigh_stacks(high, low, (halo_stack(t), halo_stack(other)), whs, t)
+        if t < 4:
+            weigh_stacks(high, low, (centre_stack(t), centre_stack(other)), wcs, t)
+
     def adjoint(t_term, new, old, lo, hi, grads):
         grads = list(grads)
-        factors = splats(coef, t_term)
-        for t in range(lo, hi):
-            row = pl.ds(t * 8, 8)
-            whr[row, :] = weigh(factors, [rsh[e, row, :] for e in range(2 * HALF)])
-            if not 4 <= t < 8:
-                at = SWAP_MAIN + t * 8 + (0 if t < 4 else (HALF - 2) * ROWS)
-                planes = [tile(swapped, at + e * ROWS) for e in range(HALF)]
-                wcr[row, :] = wcs[t_term, row, :] + weigh(factors[HALF:], planes)
         for v in range(4):
             p_new, p_old = new * 4 + v, old * 4 + v
             for t, c, h, nc, nh in stencil.tiles(xc, xh, p_new, lo, hi, EXT // 8):
                 row = pl.ds(t * 8, 8)
                 if 4 <= t < 8:
+                    weight = own_weights[t_term, pl.ds((t - 4) * 8, 8), :]
                     grads[t - 4] = grads[t - 4] + c * vs[t_term, v, pl.ds((t - 4) * 8, 8), :]
+                else:
+                    weight = wcs[t_term, row, :]
                 xc[p_old, row, :] = (
-                    (wcs[t_term, row, :] if 4 <= t < 8 else wcr[row, :]) * sgc[v, row, :]
+                    weight * sgc[v, row, :]
                     + (onc[row, :] * c - s * nc)
                     - xc[p_old, row, :]
                 )
                 xh[p_old, row, :] = (
-                    whr[row, :] * sgh[v, row, :]
+                    whs[t_term, row, :] * sgh[v, row, :]
                     + (onh[row, :] * h - s * nh)
                     - xh[p_old, row, :]
                 )
@@ -458,18 +477,23 @@
         )(*values)
         return shift(to_left, "col", -1), shift(to_right, "col", 1)
 
-    coefs, late_own, late_chk = lax.optimization_barrier((coefs, own, chk))
+    spread = (coefs[:, None, :, None] * jnp.eye(8, dtype=F32)[None, :, None, :]).reshape(
+        8 * TERMS, 16 * HALF
+    )
+    rounded = lax.reduce_precision(spread, exponent_bits=8, mantissa_bits=7)
+    high, low = rounded.astype(jnp.bfloat16), (spread - rounded).astype(jnp.bfloat16)
+    coefs, high, low, late_own, late_chk = lax.optimization_barrier((coefs, high, low, own, chk))
     own_strips = packed(pack_own_kernel, OWN_ROWS, "pack_own", late_own, late_chk)
     edge_strips = packed(pack_edge_kernel, EDGE_ROWS, "pack_edge", above, below)
     weights = pl.pallas_call(
         weights_kernel,
-        out_shape=jax.ShapeDtypeStruct((TERMS, EXT, LANES), F32),
-        in_specs=[SMEM_SPEC] + [VMEM_SPEC] * 4,
+        out_shape=jax.ShapeDtypeStruct((TERMS, ROWS, LANES), F32),
+        in_specs=[SMEM_SPEC] + [VMEM_SPEC] * 2,
         out_specs=VMEM_SPEC,
-        compiler_params=params(6),
-        cost_estimate=pl.CostEstimate(flops=12_000_000, bytes_accessed=4_000_000, transcendentals=0),
+        compiler_params=params(4),
+        cost_estimate=pl.CostEstimate(flops=4_000_000, bytes_accessed=1_000_000, transcendentals=0),
         name="weights",
-    )(coefs, own, res_other, above, below)
+    )(coefs, late_own, res_other)
 
     weights, edge_strips = lax.optimization_barrier((weights, edge_strips))
     res_rows = slice(RES * ROWS, (RES + HALF) * ROWS)
@@ -507,18 +531,18 @@
             jax.ShapeDtypeStruct((2, 4, ROWS, LANES), F32),
             jax.ShapeDtypeStruct((ROWS, LANES), F32),
         ),
-        in_specs=[SMEM_SPEC, SMEM_SPEC] + [VMEM_SPEC] * 10,
+        in_specs=[SMEM_SPEC] + [VMEM_SPEC] * 12,
         out_specs=(VMEM_SPEC, VMEM_SPEC),
         scratch_shapes=[
             pltpu.VMEM((8, *ext), F32), pltpu.VMEM((8, *ext), F32),
             pltpu.VMEM((4, *ext), F32), pltpu.VMEM((4, *ext), F32),
-            pltpu.VMEM((2 * HALF, *ext), F32),
-            pltpu.VMEM(ext, F32), pltpu.VMEM(ext, F32), pltpu.VMEM(ext, F32), pltpu.VMEM(ext, F32),
+            pltpu.VMEM(ext, F32), pltpu.VMEM(ext, F32),
+            pltpu.VMEM((TERMS, *ext), F32), pltpu.VMEM((TERMS, *ext), F32),
         ],
         compiler_params=params(10),
         name="adjoint",
     )(
-        coefs, scale, own, above, below, *own_strips, *edge_strips, swapped, states, weights
+        scale, high, low, own, above, below, *own_strips, *edge_strips, swapped, states, weights
     )
 
     grad = jnp.sum(lax.all_gather(grad, "vec"), axis=0)

time: 75.2 us -> 73.8 us (0.981)
  local copies, waits for them, and re-layouts: 0.12 us -> 2.77 us
  waiting for transfers between devices: 9.49 us -> 7 us
  Pallas kernels: 17.7 us -> 16.1 us
  other arithmetic: 1.68 us -> 3.25 us
  starting transfers between devices: 38.6 us -> 37.1 us
    mul x0 -> x1, local copies, waits for them, and re-layouts: none -> 2.65 us  [per_device(): coefs[:, None, :, None] * jnp.eye(8, dtype=F32)[None, :, None, :]]
    ppermute x6, waiting for transfers between devices: 9.49 us -> 6.99 us  [shift(): return lax.ppermute(value, axis, [(i, (i + step) % n) for i in range(n)])]
    mul x0 -> x1, other arithmetic: none -> 1.54 us  [per_device(): coefs[:, None, :, None] * jnp.eye(8, dtype=F32)[None, :, None, :]]
    ppermute x6, starting transfers between devices: 35 us -> 33.5 us  [shift(): return lax.ppermute(value, axis, [(i, (i + step) % n) for i in range(n)])]
    pallas_call x1, Pallas kernels: 9.55 us -> 8.17 us  [per_device(): pl.pallas_call(adjoint_kernel, out_shape=(jax.ShapeDtypeStruct((2, 4, ROW...]
  transfers between devices with their start and end apart: 7 -> 7, of which waited for: 2 -> 2; matrix products, arithmetic and copies ran while one was open for 2% -> 7% of each run, Pallas kernels for 9% -> 8%
where the time goes in v7:
time: 73.8 us; the launch traced here: 73.4 us
  starting transfers between devices  37.1 us (50%)
  Pallas kernels  16.1 us (22%)
  waiting for transfers between devices  7 us (9%)
  blocking collectives  5.07 us (7%)
  other arithmetic  3.25 us (4%)
  local copies, waits for them, and re-layouts  2.77 us (4%)
  between operations  2.2 us (3%)
    ppermute x6, starting transfers between devices, shift(): return lax.ppermute(value, axis, [(i, (i + step) % n) for i in range(n)])  33.5 us
    pallas_call x1, Pallas kernels, per_device(): pl.pallas_call(adjoint_kernel, out_shape=(jax.ShapeDtypeStruct((2, 4, ROW...  8.17 us
    ppermute x6, waiting for transfers between devices, shift(): return lax.ppermute(value, axis, [(i, (i + step) % n) for i in range(n)])  6.99 us
    all_gather x1, blocking collectives, per_device(): grad = jnp.sum(lax.all_gather(grad, 'vec'), axis=0)  5.07 us
    pallas_call x1, Pallas kernels, per_device(): pl.pallas_call(forward_kernel, out_shape=jax.ShapeDtypeStruct((TERMS, 4,...  3.96 us
    ppermute x1, starting transfers between devices, swap_cores(): return lax.ppermute(value, 'vec', [(0, 1), (1, 0), (2, 3), (3, 2)])  3.57 us
    mul x1, local copies, waits for them, and re-layouts, per_device(): coefs[:, None, :, None] * jnp.eye(8, dtype=F32)[None, :, None, :]  2.65 us
    pallas_call x1, Pallas kernels, per_device(): pl.pallas_call(prepare_kernel, out_shape=(send, send, jax.ShapeDtypeStruc...  1.8 us
  transfers between devices with their start and end apart: 7, of which 2 were waited for; matrix products, arithmetic and copies ran while one was open for 7% of the time, Pallas kernels for 8%

profile of v7, /device:TPU:23, one launch (start us, length us, event | category | flops | bytes accessed | tf_op | source)
XLA Modules:
  0.0 73.4 jit_solution(396616831921892881)
XLA Ops:
  1.3 1.8 %prepare.1 = (f32[928,128]{1,0:T(8,128)S(1)}, f32[928,128]{1,0:T(8,128)S(1)}, f32[512,128]{1,0:T(8,128)S(1)}, f32[256,128]{1,0:T(8,128)S(1)}) custom-call(s32[1]{0:T(128)} %bitcast.1.core, f32[1]{0:T(128)S(6)} %copy.15.scalar, f32[256,128]{1,0:T(8,128)} %bitcast.12, s32[128,128]{1,0:T(8,128)} %bitcast.13, s32[32,128]{1,0:T(8,128)} %pot.1, ...), custom_call_target="tpu_custom_call" | custom-call | tf_op jit(solution)/shard_map/prepare/pallas_call | solution.py:426
  3.1 2.0 %collective-permute-start.1 = (f32[928,128]{1,0:T(8,128)S(1)}, f32[928,128]{1,0:T(8,128)S(1)}, u32[]{:S(2)}, u32[]{:S(2)}) collective-permute-start(f32[928,128]{1,0:T(8,128)S(1)} %get-tuple-element.24), channel_id=1, source_target_pairs={{0,112},{16,0},{32,16},{48,32},{64,48},{80,64},{96,80},{112,96},{1... | collective-permute-start | bytes 1425416 | tf_op jit(solution)/shard_map/ppermute | solution.py:460
  5.1 6.9 %collective-permute-start = (f32[928,128]{1,0:T(8,128)S(1)}, f32[928,128]{1,0:T(8,128)S(1)}, u32[]{:S(2)}, u32[]{:S(2)}) collective-permute-start(f32[928,128]{1,0:T(8,128)S(1)} %get-tuple-element.25.own), channel_id=1, source_target_pairs={{0,16},{16,32},{32,48},{48,64},{64,80},{80,96},{96,112},{112,0},{1... | collective-permute-start | bytes 1425416 | tf_op jit(solution)/shard_map/ppermute | solution.py:460
  12.7 0.7 %sine_multiply_fusion = (f32[16]{0:T(128)S(1)}, f32[16]{0:T(128)S(1)}) fusion(f32[16]{0:T(128)} %param.13), kind=kLoop, calls=%fused_computation.16 | loop fusion | flops 64 | bytes 192 | tf_op jit(solution)/shard_map/mul | solution.py:52
  13.5 0.1 multiply_divide_fusion
  13.6 0.1 fusion.4
  13.7 0.1 maximum_select_fusion.coef
  13.8 1.5 %broadcast_multiply_fusion = f32[32,8,16,8]{3,2,1,0:T(8,128)} fusion(f32[8,8]{1,0:T(8,128)S(1)} %fusion.1, f32[32,16]{1,0:T(8,128)S(1)} %maximum_select_fusion.coef), kind=kLoop, calls=%fused_computation | loop fusion | flops 32768 | bytes 133376 | tf_op jit(solution)/shard_map/mul | solution.py:480
  15.4 2.6 %mul.107 = f32[256,128]{1,0:T(8,128)S(1)} reshape(f32[32,8,16,8]{3,2,1,0:T(8,128)} %broadcast_multiply_fusion) | data formatting | bytes 262144 | tf_op jit(solution)/shard_map/mul | solution.py:480
  18.1 0.2 pack_own.1
  18.3 11.1 %collective-permute-start.2 = (f32[232,128]{1,0:T(8,128)S(1)}, f32[232,128]{1,0:T(8,128)S(1)}, u32[]{:S(2)}, u32[]{:S(2)}) collective-permute-start(f32[232,128]{1,0:T(8,128)S(1)} %get-tuple-element.27), channel_id=1, source_target_pairs={{0,15},{1,0},{2,1},{3,2},{4,3},{5,4},{6,5},{7,6},{8,7},{9,8},{10,9... | collective-permute-start | bytes 356360 | tf_op jit(solution)/shard_map/ppermute | solution.py:460
  29.4 1.9 %collective-permute-start.3 = (f32[232,128]{1,0:T(8,128)S(1)}, f32[232,128]{1,0:T(8,128)S(1)}, u32[]{:S(2)}, u32[]{:S(2)}) collective-permute-start(f32[232,128]{1,0:T(8,128)S(1)} %get-tuple-element.28), channel_id=1, source_target_pairs={{0,1},{1,2},{2,3},{3,4},{4,5},{5,6},{6,7},{7,8},{8,9},{9,10},{10,1... | collective-permute-start | bytes 356360 | tf_op jit(solution)/shard_map/ppermute | solution.py:460
  31.3 1.7 %weights.1.own_weights = f32[32,32,128]{2,1,0:T(8,128)S(1)} custom-call(f32[32,16]{1,0:T(8,128)S(1)} %maximum_select_fusion.coef, f32[928,128]{1,0:T(8,128)S(1)} %get-tuple-element.25.own, f32[256,128]{1,0:T(8,128)S(1)} %get-tuple-element.30.res_other), custom_call_target="tpu_custom_call" | custom-call | flops 4000000 | bytes 1000000 | tf_op jit(solution)/shard_map/weights/pallas_call | solution.py:488
  33.0 0.0 collective-permute-done.1.below
  33.0 0.0 collective-permute-done.above
  33.0 0.3 pack_edge.1
  33.3 9.7 %collective-permute-start.4 = (f32[400,128]{1,0:T(8,128)S(1)}, f32[400,128]{1,0:T(8,128)S(1)}, u32[]{:S(2)}, u32[]{:S(2)}) collective-permute-start(f32[400,128]{1,0:T(8,128)S(1)} %get-tuple-element.31), channel_id=1, source_target_pairs={{0,15},{1,0},{2,1},{3,2},{4,3},{5,4},{6,5},{7,6},{8,7},{9,8},{10,9... | collective-permute-start | bytes 614408 | tf_op jit(solution)/shard_map/ppermute | solution.py:460
  43.0 1.9 %collective-permute-start.5 = (f32[400,128]{1,0:T(8,128)S(1)}, f32[400,128]{1,0:T(8,128)S(1)}, u32[]{:S(2)}, u32[]{:S(2)}) collective-permute-start(f32[400,128]{1,0:T(8,128)S(1)} %get-tuple-element.32), channel_id=1, source_target_pairs={{0,1},{1,2},{2,3},{3,4},{4,5},{5,6},{6,7},{7,8},{8,9},{9,10},{10,1... | collective-permute-start | bytes 614408 | tf_op jit(solution)/shard_map/ppermute | solution.py:460
  44.9 0.0 collective-permute-done.2.own_right
  44.9 2.0 %collective-permute-done.4.edge_right = f32[400,128]{1,0:T(8,128)S(1)} collective-permute-done((f32[400,128]{1,0:T(8,128)S(1)}, f32[400,128]{1,0:T(8,128)S(1)}, u32[]{:S(2)}, u32[]{:S(2)}) %collective-permute-start.4) | collective-permute-done | bytes 204832 | tf_op jit(solution)/shard_map/ppermute | solution.py:460
  46.9 5.0 %collective-permute-done.5.edge_left = f32[400,128]{1,0:T(8,128)S(1)} collective-permute-done((f32[400,128]{1,0:T(8,128)S(1)}, f32[400,128]{1,0:T(8,128)S(1)}, u32[]{:S(2)}, u32[]{:S(2)}) %collective-permute-start.5) | collective-permute-done | bytes 204832 | tf_op jit(solution)/shard_map/ppermute | solution.py:460
  51.9 0.0 collective-permute-done.3.own_left
  52.0 3.6 %collective-permute-start.6 = (f32[896,128]{1,0:T(8,128)S(1)}, f32[896,128]{1,0:T(8,128)S(1)}, u32[]{:S(2)}, u32[]{:S(2)}) collective-permute-start(f32[896,128]{1,0:T(8,128)S(1)} %slice_dynamic-update-slice_fusion), channel_id=1, source_target_pairs={{0,128},{128,0},{256,384},{384,256},{1,129},{129,1},{257,385},{385... | collective-permute-start | bytes 1376264 | tf_op jit(solution)/shard_map/ppermute | solution.py:463
  55.6 4.0 %forward.1.vs = f32[32,4,32,128]{3,2,1,0:T(8,128)S(1)} custom-call(f32[1]{0:T(128)S(6)} %div.18.scale, f32[928,128]{1,0:T(8,128)S(1)} %get-tuple-element.25.own, f32[512,128]{1,0:T(8,128)S(1)} %get-tuple-element.26.chk, f32[928,128]{1,0:T(8,128)S(1)} %collective-permute-done.above, f32[928,128]{1,0:T(8,128)S(1)} %collective-permute-done.1.below, ...), custom_call_target="tpu_custom_call" | custom-call | flops 20000000 | bytes 6000000 | tf_op jit(solution)/shard_map/forward/pallas_call | solution.py:513
  59.6 0.0 collective-permute-done.6.swapped
  59.6 8.2 %adjoint.1 = (f32[2,4,32,128]{3,2,1,0:T(8,128)}, f32[32,128]{1,0:T(8,128)S(1)}) custom-call(f32[1]{0:T(128)S(6)} %div.18.scale, bf16[256,128]{1,0:T(8,128)(2,1)S(1)} %get-tuple-element.22.high, bf16[256,128]{1,0:T(8,128)(2,1)S(1)} %get-tuple-element.23.low, f32[928,128]{1,0:T(8,128)S(1)} %get-tuple-element.25.own, ...), custom_call_target="tpu_custom_call" | custom-call | tf_op jit(solution)/shard_map/adjoint/pallas_call | solution.py:528
  67.8 5.1 %all-gather = f32[128,128]{1,0:T(8,128)S(1)} all-gather(f32[32,128]{1,0:T(8,128)S(1)} %get-tuple-element.36), channel_id=2, replica_groups=mesh['vec'=4,'row'=8,'col'=16] {'vec'}, dimensions={0}, use_global_device_ids=true | all-gather | bytes 81920 | tf_op jit(solution)/shard_map/all_gather | solution.py:548
  72.8 0.6 reduce_sum.9
  (10 shorter events, 0.1 us)
Async XLA Ops:
  3.1 29.9 %collective-permute-start.1 = (f32[928,128]{1,0:T(8,128)S(1)}, f32[928,128]{1,0:T(8,128)S(1)}, u32[]{:S(2)}, u32[]{:S(2)}) collective-permute-start(f32[928,128]{1,0:T(8,128)S(1)} %get-tuple-element.24), channel_id=1, source_target_pairs={{0,112},{16,0},{32,16},{48,32},{64,48},{80,64},{96,80},{112,96},{1... | collective-permute-start | bytes 1425416 | tf_op jit(solution)/shard_map/ppermute | solution.py:460
  5.1 28.0 %collective-permute-start = (f32[928,128]{1,0:T(8,128)S(1)}, f32[928,128]{1,0:T(8,128)S(1)}, u32[]{:S(2)}, u32[]{:S(2)}) collective-permute-start(f32[928,128]{1,0:T(8,128)S(1)} %get-tuple-element.25.own), channel_id=1, source_target_pairs={{0,16},{16,32},{32,48},{48,64},{64,80},{80,96},{96,112},{112,0},{1... | collective-permute-start | bytes 1425416 | tf_op jit(solution)/shard_map/ppermute | solution.py:460
  18.3 26.6 %collective-permute-start.2 = (f32[232,128]{1,0:T(8,128)S(1)}, f32[232,128]{1,0:T(8,128)S(1)}, u32[]{:S(2)}, u32[]{:S(2)}) collective-permute-start(f32[232,128]{1,0:T(8,128)S(1)} %get-tuple-element.27), channel_id=1, source_target_pairs={{0,15},{1,0},{2,1},{3,2},{4,3},{5,4},{6,5},{7,6},{8,7},{9,8},{10,9... | collective-permute-start | bytes 356360 | tf_op jit(solution)/shard_map/ppermute | solution.py:460
  29.4 22.5 %collective-permute-start.3 = (f32[232,128]{1,0:T(8,128)S(1)}, f32[232,128]{1,0:T(8,128)S(1)}, u32[]{:S(2)}, u32[]{:S(2)}) collective-permute-start(f32[232,128]{1,0:T(8,128)S(1)} %get-tuple-element.28), channel_id=1, source_target_pairs={{0,1},{1,2},{2,3},{3,4},{4,5},{5,6},{6,7},{7,8},{8,9},{9,10},{10,1... | collective-permute-start | bytes 356360 | tf_op jit(solution)/shard_map/ppermute | solution.py:460
  33.3 13.6 %collective-permute-start.4 = (f32[400,128]{1,0:T(8,128)S(1)}, f32[400,128]{1,0:T(8,128)S(1)}, u32[]{:S(2)}, u32[]{:S(2)}) collective-permute-start(f32[400,128]{1,0:T(8,128)S(1)} %get-tuple-element.31), channel_id=1, source_target_pairs={{0,15},{1,0},{2,1},{3,2},{4,3},{5,4},{6,5},{7,6},{8,7},{9,8},{10,9... | collective-permute-start | bytes 614408 | tf_op jit(solution)/shard_map/ppermute | solution.py:460
  43.0 8.9 %collective-permute-start.5 = (f32[400,128]{1,0:T(8,128)S(1)}, f32[400,128]{1,0:T(8,128)S(1)}, u32[]{:S(2)}, u32[]{:S(2)}) collective-permute-start(f32[400,128]{1,0:T(8,128)S(1)} %get-tuple-element.32), channel_id=1, source_target_pairs={{0,1},{1,2},{2,3},{3,4},{4,5},{5,6},{6,7},{7,8},{8,9},{9,10},{10,1... | collective-permute-start | bytes 614408 | tf_op jit(solution)/shard_map/ppermute | solution.py:460
  52.0 7.6 %collective-permute-start.6 = (f32[896,128]{1,0:T(8,128)S(1)}, f32[896,128]{1,0:T(8,128)S(1)}, u32[]{:S(2)}, u32[]{:S(2)}) collective-permute-start(f32[896,128]{1,0:T(8,128)S(1)} %slice_dynamic-update-slice_fusion), channel_id=1, source_target_pairs={{0,128},{128,0},{256,384},{384,256},{1,129},{129,1},{257,385},{385... | collective-permute-start | bytes 1376264 | tf_op jit(solution)/shard_map/ppermute | solution.py:463

commit v8 on v7

--- a/solution.py
+++ b/solution.py
@@ -150,36 +150,37 @@
                 pack(tiles, EDGE_CHK + g * 2 * FHALO + side * FHALO + i * 8, to_left, to_right)
 
 
-def unpack_strip(right, left, lane, j, count):
+def unpack_strip(right, left, lane, j, count, turns=(0,)):
     width = LANES // count
     mixed = jnp.where(lane // width == j, tile(*right), tile(*left))
-    return pltpu.roll(mixed, (LANES - width * j) % LANES, 1) if j else mixed
+    shifts = [(LANES - width * j + turn * (LANES // 2)) % LANES for turn in turns]
+    return [pltpu.roll(mixed, shift, 1) if shift else mixed for shift in shifts]
 
 
 class Strips:
     def __init__(self, own_right, own_left, edge_right, edge_left, lane):
         self.own, self.edge, self.lane = (own_right, own_left), (edge_right, edge_left), lane
 
-    def unpack(self, refs, row, j, count):
-        return unpack_strip((refs[0], row), (refs[1], row), self.lane, j, count)
-
-    def plane(self, index, t):
+    def unpack(self, refs, row, j, count, turns):
+        return unpack_strip((refs[0], row), (refs[1], row), self.lane, j, count, turns)
+
+    def plane(self, index, t, turns=(0, 1)):
         g, j = index // 4, index % 4
         if 4 <= t < 8:
-            return self.unpack(self.own, g * ROWS + (t - 4) * 8, j, 4)
-        return self.unpack(self.edge, g * 2 * HALO + (t if t < 4 else t - 4) * 8, j, 4)
-
-    def onsite(self, t):
+            return self.unpack(self.own, g * ROWS + (t - 4) * 8, j, 4, turns)
+        return self.unpack(self.edge, g * 2 * HALO + (t if t < 4 else t - 4) * 8, j, 4, turns)
+
+    def onsite(self, t, turns=(0, 1)):
         if 4 <= t < 8:
-            return self.unpack(self.own, OWN_ONS, t - 4, 4)
-        return self.unpack(self.edge, EDGE_ONS + t // 8 * 8, t % 4, 4)
-
-    def checkpoint(self, plane, t):
+            return self.unpack(self.own, OWN_ONS, t - 4, 4, turns)
+        return self.unpack(self.edge, EDGE_ONS + t // 8 * 8, t % 4, 4, turns)
+
+    def checkpoint(self, plane, t, turns):
         g, j = plane // 8, plane % 8
         if 2 <= t < 6:
-            return self.unpack(self.own, OWN_CHK + g * ROWS + (t - 2) * 8, j, 8)
+            return self.unpack(self.own, OWN_CHK + g * ROWS + (t - 2) * 8, j, 8, turns)
         at = EDGE_CHK + g * 2 * FHALO + (t if t < 2 else t - 4) * 8
-        return self.unpack(self.edge, at, j, 8)
+        return self.unpack(self.edge, at, j, 8, turns)
 
 
 SWAP_OWN, SWAP_EDGE = 2 * ROWS, 4 * HALO
@@ -193,7 +194,7 @@
         row = g * ROWS + (t - 4) * 8
     else:
         row = SWAP_OWN + g * 2 * HALO + (t if t < 4 else t - 4) * 8
-    return unpack_strip((swapped, row), (swapped, SWAP_SIDE + row), lane, j, 4)
+    return unpack_strip((swapped, row), (swapped, SWAP_SIDE + row), lane, j, 4, (0, 1))
 
 
 def splats(coef, t_term):
@@ -217,13 +218,15 @@
         for i in range(4):
             planes = [tile(own, (RES + e) * ROWS + i * 8) for e in range(HALF)]
             planes += [tile(res_other, e * ROWS + i * 8) for e in range(HALF)]
-            out[t_term, pl.ds(i * 8, 8), :] = weigh(factors, planes)
+            value = weigh(factors, planes)
+            out[0, t_term, pl.ds(i * 8, 8), :] = value
+            out[1, t_term, pl.ds(i * 8, 8), :] = turned(value)
         return carry
 
     lax.fori_loop(0, TERMS, body, 0)
 
 
-def weigh_stacks(high, low, stacks, out, t):
+def weigh_stacks(high, low, stacks, out, out_turned, t):
     first = TERMS - 8 * (min(t, 3) + 1)
     rows = slice(8 * first, 8 * TERMS)
     stack = jnp.concatenate([jnp.concatenate(stack, axis=0) for stack in stacks], axis=1)
@@ -236,80 +239,110 @@
     result = product(high, upper) + (product(high, lower) + product(low, upper))
     for n in range(first, TERMS):
         part = result[8 * (n - first) : 8 * (n - first) + 8]
-        out[n, pl.ds(t * 8, 8), :] = part[:, :LANES]
-        out[n, pl.ds(EXT - 8 - t * 8, 8), :] = part[:, LANES:]
+        for at, value in ((t * 8, part[:, :LANES]), (EXT - 8 - t * 8, part[:, LANES:])):
+            out[n, pl.ds(at, 8), :] = value
+            if out_turned is not None:
+                out_turned[n, pl.ds(at, 8), :] = turned(value)
+
+
+def turned(value):
+    return pltpu.roll(value, LANES // 2, 1)
+
+
+def maybe_turned(value, turn):
+    return turned(value) if turn else value
+
+
+def paired(first, second_turned, lane):
+    inner = (lane >= HALO) & (lane < LANES - HALO)
+    return jnp.where(inner, second_turned, first)
 
 
 class Stencil:
     def __init__(self):
         lane, sub = lane_iota(), lax.broadcasted_iota(jnp.int32, (8, LANES), 0)
         self.lane = lane
-        self.first_lane, self.last_lane = lane == 0, lane == LANES - 1
+        self.seam = {p: lane == p for p in (0, LANES // 2 - 1, LANES // 2, LANES - 1)}
         self.first_sub, self.last_sub = sub == 0, sub == 7
 
-    def tiles(self, cref, href, plane, lo, hi, count):
+    def side(self, values, shift, at_a, at_b):
+        a, b, h = (pltpu.roll(v, shift, 1) for v in values)
+        seam_a, seam_b = self.seam[at_a], self.seam[at_b]
+        return (
+            jnp.where(seam_a, h, a),
+            jnp.where(seam_b, h, b),
+            jnp.where(seam_a, a, jnp.where(seam_b, b, h)),
+        )
+
+    def tiles(self, refs, lo, hi, count):
         def load(t):
-            return cref[plane, pl.ds(t * 8, 8), :], href[plane, pl.ds(t * 8, 8), :]
-
-        def rolled(pair, shift):
-            return tuple(pltpu.roll(p, shift, 0) for p in pair)
-
+            return [ref[pl.ds(t * 8, 8), :] for ref in refs]
+
+        def rolled(values, shift):
+            return [pltpu.roll(v, shift, 0) for v in values]
+
+        half = LANES // 2
         here = load(lo)
         here_up, here_down = rolled(here, 1), rolled(here, 7)
         prev_up = rolled(load(lo - 1), 1) if lo > 0 else here_up
         for t in range(lo, hi):
             after = load(t + 1) if t + 1 < count else here
             after_up, after_down = rolled(after, 1), rolled(after, 7)
-            c, h = here
-            cl, cr = pltpu.roll(c, 1, 1), pltpu.roll(c, LANES - 1, 1)
-            hl, hr = pltpu.roll(h, 1, 1), pltpu.roll(h, LANES - 1, 1)
-            side_c = jnp.where(self.first_lane, hl, cl) + jnp.where(self.last_lane, hr, cr)
-            side_h = jnp.where(self.first_lane, cl, hl) + jnp.where(self.last_lane, cr, hr)
-            vert = [
-                jnp.where(self.first_sub, prev_up[k], here_up[k])
-                + jnp.where(self.last_sub, after_down[k], here_down[k])
-                for k in range(2)
+            left = self.side(here, 1, 0, half)
+            right = self.side(here, LANES - 1, LANES - 1, half - 1)
+            sums = [
+                (left[m] + right[m])
+                + (
+                    jnp.where(self.first_sub, prev_up[m], here_up[m])
+                    + jnp.where(self.last_sub, after_down[m], here_down[m])
+                )
+                for m in range(3)
             ]
-            yield t, c, h, side_c + vert[0], side_h + vert[1]
+            yield t, here, sums
             here, prev_up, here_up, here_down = after, here_up, after_up, after_down
 
 
 def forward_kernel(
     scale, own, chk, above, below, own_right, own_left, edge_right, edge_left,
-    vs, fc, fh, onc, onh,
+    vs, fc, fh, on,
 ):
     stencil = Stencil()
-    strips = Strips(own_right, own_left, edge_right, edge_left, stencil.lane)
+    lane = stencil.lane
+    strips = Strips(own_right, own_left, edge_right, edge_left, lane)
     s = jnp.full((8, LANES), scale[0], F32)
     for t in range(FEXT // 8):
         row = pl.ds(t * 8, 8)
         for plane in range(FPLANES):
-            fc[plane, row, :] = fwd_tile(chk, above, below, plane, t)
-            fh[plane, row, :] = strips.checkpoint(plane, t)
+            value = maybe_turned(fwd_tile(chk, above, below, plane, t), plane % 2)
+            fc[plane, row, :] = value
+            if 2 <= t < 6:
+                segment, which, v = plane // 8, plane // 4 % 2, plane % 4
+                vs[segment * SEG + which, v, pl.ds((t - 2) * 8, 8), :] = value
+            if plane % 2:
+                fh[plane // 2, row, :] = paired(
+                    *strips.checkpoint(plane - 1, t, (0,)), *strips.checkpoint(plane, t, (1,)), lane
+                )
         e = t + (HALO - FHALO) // 8
-        onc[row, :] = main_tile(own, above, below, ONS, e)
-        onh[row, :] = strips.onsite(e)
-    for segment in range(2):
-        for which in range(2):
-            for v in range(4):
-                for i in range(4):
-                    vs[segment * SEG + which, v, pl.ds(i * 8, 8), :] = tile(
-                        chk, (segment * 8 + which * 4 + v) * ROWS + i * 8
-                    )
+        centre, edge = main_tile(own, above, below, ONS, e), strips.onsite(e)
+        on[0, row, :] = centre
+        on[1, row, :] = turned(centre)
+        on[2, row, :] = paired(*edge, lane)
+
+    def group(segment, which, pair):
+        at = segment * 4 + which * 2 + pair
+        return [fc.at[2 * at], fc.at[2 * at + 1], fh.at[at]]
 
     def forward(k, new, old, lo, hi):
         for segment in range(2):
-            for v in range(4):
-                p_new = segment * 8 + new * 4 + v
-                p_old = segment * 8 + old * 4 + v
-                for t, c, h, nc, nh in stencil.tiles(fc, fh, p_new, lo, hi, FEXT // 8):
+            for pair in range(2):
+                target = group(segment, old, pair)
+                for t, values, sums in stencil.tiles(group(segment, new, pair), lo, hi, FEXT // 8):
                     row = pl.ds(t * 8, 8)
-                    out_c = onc[row, :] * c - s * nc - fc[p_old, row, :]
-                    out_h = onh[row, :] * h - s * nh - fh[p_old, row, :]
-                    fc[p_old, row, :] = out_c
-                    fh[p_old, row, :] = out_h
-                    if 2 <= t < 6:
-                        vs[segment * SEG + k, v, pl.ds((t - 2) * 8, 8), :] = out_c
+                    for m in range(3):
+                        value = on[m, row, :] * values[m] - s * sums[m] - target[m][row, :]
+                        target[m][row, :] = value
+                        if m < 2 and 2 <= t < 6:
+                            vs[segment * SEG + k, 2 * pair + m, pl.ds((t - 2) * 8, 8), :] = value
 
     for start, stop, lo, hi in ((1, 4, 0, 8), (4, 8, 1, 7)):
         def body(i, carry, lo=lo, hi=hi):
@@ -323,27 +356,39 @@
     scale, high, low, own, above, below, own_right, own_left, edge_right, edge_left, swapped,
     vs, own_weights,
     adj_out, grad_out,
-    xc, xh, sgc, sgh, onc, onh, wcs, whs,
+    xc, xh, sg, on, wcs, wts, whs,
 ):
     stencil = Stencil()
-    strips = Strips(own_right, own_left, edge_right, edge_left, stencil.lane)
+    lane = stencil.lane
+    strips = Strips(own_right, own_left, edge_right, edge_left, lane)
     s = jnp.full((8, LANES), scale[0], F32)
 
     for t in range(EXT // 8):
         row = pl.ds(t * 8, 8)
         for plane in range(8):
-            xc[plane, row, :] = main_tile(own, above, below, plane, t)
-            xh[plane, row, :] = strips.plane(plane, t)
-        for v in range(4):
-            sgc[v, row, :] = main_tile(own, above, below, SGN + v, t)
-            sgh[v, row, :] = strips.plane(SGN + v, t)
-        onc[row, :] = main_tile(own, above, below, ONS, t)
-        onh[row, :] = strips.onsite(t)
+            xc[plane, row, :] = maybe_turned(main_tile(own, above, below, plane, t), plane % 2)
+        for at in range(4):
+            xh[at, row, :] = paired(
+                *strips.plane(2 * at, t, (0,)), *strips.plane(2 * at + 1, t, (1,)), lane
+            )
+        for pair in range(2):
+            first = SGN + 2 * pair
+            for m in range(2):
+                sg[3 * pair + m, row, :] = maybe_turned(
+                    main_tile(own, above, below, first + m, t), m
+                )
+            sg[3 * pair + 2, row, :] = paired(
+                *strips.plane(first, t, (0,)), *strips.plane(first + 1, t, (1,)), lane
+            )
+        centre, edge = main_tile(own, above, below, ONS, t), strips.onsite(t)
+        on[0, row, :] = centre
+        on[1, row, :] = turned(centre)
+        on[2, row, :] = paired(*edge, lane)
 
     def halo_stack(t):
-        return [strips.plane(RES + e, t) for e in range(HALF)] + [
-            swapped_strip(swapped, stencil.lane, e, t) for e in range(HALF)
-        ]
+        values = [strips.plane(RES + e, t) for e in range(HALF)]
+        values += [swapped_strip(swapped, lane, e, t) for e in range(HALF)]
+        return [paired(*value, lane) for value in values]
 
     def centre_stack(t):
         at = SWAP_MAIN + t * 8 + (0 if t < 4 else (HALF - 2) * ROWS)
@@ -353,34 +398,44 @@
 
     for t in range(EXT // 16):
         other = EXT // 8 - 1 - t
-        weigh_stacks(high, low, (halo_stack(t), halo_stack(other)), whs, t)
+        weigh_stacks(high, low, (halo_stack(t), halo_stack(other)), whs, None, t)
         if t < 4:
-            weigh_stacks(high, low, (centre_stack(t), centre_stack(other)), wcs, t)
+            weigh_stacks(high, low, (centre_stack(t), centre_stack(other)), wcs, wts, t)
+
+    def group(which, pair):
+        at = which * 2 + pair
+        return [xc.at[2 * at], xc.at[2 * at + 1], xh.at[at]]
+
+    def weights_of(t_term, t):
+        row = pl.ds(t * 8, 8)
+        if 4 <= t < 8:
+            local = pl.ds((t - 4) * 8, 8)
+            centre = [own_weights[m, t_term, local, :] for m in range(2)]
+        else:
+            centre = [wcs[t_term, row, :], wts[t_term, row, :]]
+        return centre + [whs[t_term, row, :]]
 
     def adjoint(t_term, new, old, lo, hi, grads):
         grads = list(grads)
-        for v in range(4):
-            p_new, p_old = new * 4 + v, old * 4 + v
-            for t, c, h, nc, nh in stencil.tiles(xc, xh, p_new, lo, hi, EXT // 8):
+        for pair in range(2):
+            target = group(old, pair)
+            for t, values, sums in stencil.tiles(group(new, pair), lo, hi, EXT // 8):
                 row = pl.ds(t * 8, 8)
                 if 4 <= t < 8:
-                    weight = own_weights[t_term, pl.ds((t - 4) * 8, 8), :]
-                    grads[t - 4] = grads[t - 4] + c * vs[t_term, v, pl.ds((t - 4) * 8, 8), :]
-                else:
-                    weight = wcs[t_term, row, :]
-                xc[p_old, row, :] = (
-                    weight * sgc[v, row, :]
-                    + (onc[row, :] * c - s * nc)
-                    - xc[p_old, row, :]
-                )
-                xh[p_old, row, :] = (
-                    whs[t_term, row, :] * sgh[v, row, :]
-                    + (onh[row, :] * h - s * nh)
-                    - xh[p_old, row, :]
-                )
+                    for m in range(2):
+                        at = 4 * m + t - 4
+                        state = vs[t_term, 2 * pair + m, pl.ds((t - 4) * 8, 8), :]
+                        grads[at] = grads[at] + values[m] * state
+                weights = weights_of(t_term, t)
+                for m in range(3):
+                    target[m][row, :] = (
+                        weights[m] * sg[3 * pair + m, row, :]
+                        + (on[m, row, :] * values[m] - s * sums[m])
+                        - target[m][row, :]
+                    )
         return tuple(grads)
 
-    grads = tuple(jnp.zeros((8, LANES), F32) for _ in range(4))
+    grads = tuple(jnp.zeros((8, LANES), F32) for _ in range(8))
     for phase in range(4):
         lo, hi = phase_tiles(phase)
         def body(i, carry, phase=phase, lo=lo, hi=hi):
@@ -389,11 +444,12 @@
             return adjoint(t_term - 1, 1, 0, lo, hi, carry)
         grads = lax.fori_loop(0, 4, body, grads)
     for i in range(4):
-        grad_out[pl.ds(i * 8, 8), :] = grads[i] * s
+        grad_out[pl.ds(i * 8, 8), :] = (grads[i] + turned(grads[4 + i])) * s
     for which in range(2):
         for v in range(4):
             for i in range(4):
-                adj_out[which, v, pl.ds(i * 8, 8), :] = xc[which * 4 + v, pl.ds(HALO + i * 8, 8), :]
+                value = xc[which * 4 + v, pl.ds(HALO + i * 8, 8), :]
+                adj_out[which, v, pl.ds(i * 8, 8), :] = maybe_turned(value, v % 2)
 
 
 VMEM_SPEC = pl.BlockSpec(memory_space=pltpu.VMEM)
@@ -487,7 +543,7 @@
     edge_strips = packed(pack_edge_kernel, EDGE_ROWS, "pack_edge", above, below)
     weights = pl.pallas_call(
         weights_kernel,
-        out_shape=jax.ShapeDtypeStruct((TERMS, ROWS, LANES), F32),
+        out_shape=jax.ShapeDtypeStruct((2, TERMS, ROWS, LANES), F32),
         in_specs=[SMEM_SPEC] + [VMEM_SPEC] * 2,
         out_specs=VMEM_SPEC,
         compiler_params=params(4),
@@ -516,8 +572,8 @@
         in_specs=[SMEM_SPEC] + [VMEM_SPEC] * 8,
         out_specs=VMEM_SPEC,
         scratch_shapes=[
-            pltpu.VMEM(frame, F32), pltpu.VMEM(frame, F32),
-            pltpu.VMEM(frame[1:], F32), pltpu.VMEM(frame[1:], F32),
+            pltpu.VMEM(frame, F32), pltpu.VMEM((FPLANES // 2, *frame[1:]), F32),
+            pltpu.VMEM((3, *frame[1:]), F32),
         ],
         compiler_params=params(8),
         cost_estimate=pl.CostEstimate(flops=20_000_000, bytes_accessed=6_000_000, transcendentals=0),
@@ -534,12 +590,12 @@
         in_specs=[SMEM_SPEC] + [VMEM_SPEC] * 12,
         out_specs=(VMEM_SPEC, VMEM_SPEC),
         scratch_shapes=[
-            pltpu.VMEM((8, *ext), F32), pltpu.VMEM((8, *ext), F32),
-            pltpu.VMEM((4, *ext), F32), pltpu.VMEM((4, *ext), F32),
-            pltpu.VMEM(ext, F32), pltpu.VMEM(ext, F32),
+            pltpu.VMEM((8, *ext), F32), pltpu.VMEM((4, *ext), F32),
+            pltpu.VMEM((6, *ext), F32), pltpu.VMEM((3, *ext), F32),
             pltpu.VMEM((TERMS, *ext), F32), pltpu.VMEM((TERMS, *ext), F32),
+            pltpu.VMEM((TERMS, *ext), F32),
         ],
-        compiler_params=params(10),
+        compiler_params=params(12),
         name="adjoint",
     )(
         scale, high, low, own, above, below, *own_strips, *edge_strips, swapped, states, weights

time: 73.8 us -> 72.1 us (0.977)
  the two profiles are of different devices: /device:TPU:23 before, /device:TPU:31 now
where the time goes in v8:
time: 72.1 us; the launch traced here: 71.7 us
  starting transfers between devices  34.9 us (48%)
  Pallas kernels  16.5 us (23%)
  waiting for transfers between devices  7 us (10%)
  blocking collectives  5.07 us (7%)
  other arithmetic  3.25 us (5%)
  local copies, waits for them, and re-layouts  2.77 us (4%)
  between operations  2.19 us (3%)
    ppermute x6, starting transfers between devices, shift(): return lax.ppermute(value, axis, [(i, (i + step) % n) for i in range(n)])  31.4 us
    pallas_call x1, Pallas kernels, per_device(): pl.pallas_call(adjoint_kernel, out_shape=(jax.ShapeDtypeStruct((2, 4, ROW...  7.13 us
    ppermute x6, waiting for transfers between devices, shift(): return lax.ppermute(value, axis, [(i, (i + step) % n) for i in range(n)])  6.99 us
    all_gather x1, blocking collectives, per_device(): grad = jnp.sum(lax.all_gather(grad, 'vec'), axis=0)  5.07 us
    pallas_call x1, Pallas kernels, per_device(): pl.pallas_call(weights_kernel, out_shape=jax.ShapeDtypeStruct((2, TERMS,...  3.85 us
    ppermute x1, starting transfers between devices, swap_cores(): return lax.ppermute(value, 'vec', [(0, 1), (1, 0), (2, 3), (3, 2)])  3.57 us
    pallas_call x1, Pallas kernels, per_device(): pl.pallas_call(forward_kernel, out_shape=jax.ShapeDtypeStruct((TERMS, 4,...  3.23 us
    mul x1, local copies, waits for them, and re-layouts, per_device(): coefs[:, None, :, None] * jnp.eye(8, dtype=F32)[None, :, None, :]  2.65 us
  transfers between devices with their start and end apart: 7, of which 2 were waited for; matrix products, arithmetic and copies ran while one was open for 7% of the time, Pallas kernels for 11%

profile of v8, /device:TPU:31, one launch (start us, length us, event | category | flops | bytes accessed | tf_op | source)
XLA Modules:
  0.0 71.7 jit_solution(1454254769563775125)
XLA Ops:
  1.3 1.8 %prepare.1 = (f32[928,128]{1,0:T(8,128)S(1)}, f32[928,128]{1,0:T(8,128)S(1)}, f32[512,128]{1,0:T(8,128)S(1)}, f32[256,128]{1,0:T(8,128)S(1)}) custom-call(s32[1]{0:T(128)} %bitcast.1.core, f32[1]{0:T(128)S(6)} %copy.15.scalar, f32[256,128]{1,0:T(8,128)} %bitcast.12, s32[128,128]{1,0:T(8,128)} %bitcast.13, s32[32,128]{1,0:T(8,128)} %pot.1, ...), custom_call_target="tpu_custom_call" | custom-call | tf_op jit(solution)/shard_map/prepare/pallas_call | solution.py:482
  3.1 2.9 %collective-permute-start.1 = (f32[928,128]{1,0:T(8,128)S(1)}, f32[928,128]{1,0:T(8,128)S(1)}, u32[]{:S(2)}, u32[]{:S(2)}) collective-permute-start(f32[928,128]{1,0:T(8,128)S(1)} %get-tuple-element.24), channel_id=1, source_target_pairs={{0,112},{16,0},{32,16},{48,32},{64,48},{80,64},{96,80},{112,96},{1... | collective-permute-start | bytes 1425416 | tf_op jit(solution)/shard_map/ppermute | solution.py:516
  6.0 6.0 %collective-permute-start = (f32[928,128]{1,0:T(8,128)S(1)}, f32[928,128]{1,0:T(8,128)S(1)}, u32[]{:S(2)}, u32[]{:S(2)}) collective-permute-start(f32[928,128]{1,0:T(8,128)S(1)} %get-tuple-element.25.own), channel_id=1, source_target_pairs={{0,16},{16,32},{32,48},{48,64},{64,80},{80,96},{96,112},{112,0},{1... | collective-permute-start | bytes 1425416 | tf_op jit(solution)/shard_map/ppermute | solution.py:516
  12.7 0.7 %sine_multiply_fusion = (f32[16]{0:T(128)S(1)}, f32[16]{0:T(128)S(1)}) fusion(f32[16]{0:T(128)} %param.13), kind=kLoop, calls=%fused_computation.16 | loop fusion | flops 64 | bytes 192 | tf_op jit(solution)/shard_map/mul | solution.py:52
  13.5 0.1 multiply_divide_fusion
  13.6 0.1 fusion.4
  13.7 0.1 maximum_select_fusion.coef
  13.8 1.5 %broadcast_multiply_fusion = f32[32,8,16,8]{3,2,1,0:T(8,128)} fusion(f32[8,8]{1,0:T(8,128)S(1)} %fusion.1, f32[32,16]{1,0:T(8,128)S(1)} %maximum_select_fusion.coef), kind=kLoop, calls=%fused_computation | loop fusion | flops 32768 | bytes 133376 | tf_op jit(solution)/shard_map/mul | solution.py:536
  15.4 2.6 %mul.107 = f32[256,128]{1,0:T(8,128)S(1)} reshape(f32[32,8,16,8]{3,2,1,0:T(8,128)} %broadcast_multiply_fusion) | data formatting | bytes 262144 | tf_op jit(solution)/shard_map/mul | solution.py:536
  18.1 0.2 pack_own.1
  18.3 11.1 %collective-permute-start.2 = (f32[232,128]{1,0:T(8,128)S(1)}, f32[232,128]{1,0:T(8,128)S(1)}, u32[]{:S(2)}, u32[]{:S(2)}) collective-permute-start(f32[232,128]{1,0:T(8,128)S(1)} %get-tuple-element.27), channel_id=1, source_target_pairs={{0,15},{1,0},{2,1},{3,2},{4,3},{5,4},{6,5},{7,6},{8,7},{9,8},{10,9... | collective-permute-start | bytes 356360 | tf_op jit(solution)/shard_map/ppermute | solution.py:516
  29.4 1.9 %collective-permute-start.3 = (f32[232,128]{1,0:T(8,128)S(1)}, f32[232,128]{1,0:T(8,128)S(1)}, u32[]{:S(2)}, u32[]{:S(2)}) collective-permute-start(f32[232,128]{1,0:T(8,128)S(1)} %get-tuple-element.28), channel_id=1, source_target_pairs={{0,1},{1,2},{2,3},{3,4},{4,5},{5,6},{6,7},{7,8},{8,9},{9,10},{10,1... | collective-permute-start | bytes 356360 | tf_op jit(solution)/shard_map/ppermute | solution.py:516
  31.3 3.9 %weights.1.own_weights = f32[2,32,32,128]{3,2,1,0:T(8,128)S(1)} custom-call(f32[32,16]{1,0:T(8,128)S(1)} %maximum_select_fusion.coef, f32[928,128]{1,0:T(8,128)S(1)} %get-tuple-element.25.own, f32[256,128]{1,0:T(8,128)S(1)} %get-tuple-element.30.res_other), custom_call_target="tpu_custom_call" | custom-call | flops 4000000 | bytes 1000000 | tf_op jit(solution)/shard_map/weights/pallas_call | solution.py:544
  35.2 0.0 collective-permute-done.1.below
  35.2 0.0 collective-permute-done.above
  35.2 0.3 pack_edge.1
  35.5 7.5 %collective-permute-start.4 = (f32[400,128]{1,0:T(8,128)S(1)}, f32[400,128]{1,0:T(8,128)S(1)}, u32[]{:S(2)}, u32[]{:S(2)}) collective-permute-start(f32[400,128]{1,0:T(8,128)S(1)} %get-tuple-element.31), channel_id=1, source_target_pairs={{0,15},{1,0},{2,1},{3,2},{4,3},{5,4},{6,5},{7,6},{8,7},{9,8},{10,9... | collective-permute-start | bytes 614408 | tf_op jit(solution)/shard_map/ppermute | solution.py:516
  43.0 1.9 %collective-permute-start.5 = (f32[400,128]{1,0:T(8,128)S(1)}, f32[400,128]{1,0:T(8,128)S(1)}, u32[]{:S(2)}, u32[]{:S(2)}) collective-permute-start(f32[400,128]{1,0:T(8,128)S(1)} %get-tuple-element.32), channel_id=1, source_target_pairs={{0,1},{1,2},{2,3},{3,4},{4,5},{5,6},{6,7},{7,8},{8,9},{9,10},{10,1... | collective-permute-start | bytes 614408 | tf_op jit(solution)/shard_map/ppermute | solution.py:516
  44.9 0.0 collective-permute-done.2.own_right
  44.9 2.0 %collective-permute-done.4.edge_right = f32[400,128]{1,0:T(8,128)S(1)} collective-permute-done((f32[400,128]{1,0:T(8,128)S(1)}, f32[400,128]{1,0:T(8,128)S(1)}, u32[]{:S(2)}, u32[]{:S(2)}) %collective-permute-start.4) | collective-permute-done | bytes 204832 | tf_op jit(solution)/shard_map/ppermute | solution.py:516
  46.9 5.0 %collective-permute-done.5.edge_left = f32[400,128]{1,0:T(8,128)S(1)} collective-permute-done((f32[400,128]{1,0:T(8,128)S(1)}, f32[400,128]{1,0:T(8,128)S(1)}, u32[]{:S(2)}, u32[]{:S(2)}) %collective-permute-start.5) | collective-permute-done | bytes 204832 | tf_op jit(solution)/shard_map/ppermute | solution.py:516
  51.9 0.0 collective-permute-done.3.own_left
  52.0 3.6 %collective-permute-start.6 = (f32[896,128]{1,0:T(8,128)S(1)}, f32[896,128]{1,0:T(8,128)S(1)}, u32[]{:S(2)}, u32[]{:S(2)}) collective-permute-start(f32[896,128]{1,0:T(8,128)S(1)} %slice_dynamic-update-slice_fusion), channel_id=1, source_target_pairs={{0,128},{128,0},{256,384},{384,256},{1,129},{129,1},{257,385},{385... | collective-permute-start | bytes 1376264 | tf_op jit(solution)/shard_map/ppermute | solution.py:519
  55.6 3.2 %forward.1.vs = f32[32,4,32,128]{3,2,1,0:T(8,128)S(1)} custom-call(f32[1]{0:T(128)S(6)} %div.18.scale, f32[928,128]{1,0:T(8,128)S(1)} %get-tuple-element.25.own, f32[512,128]{1,0:T(8,128)S(1)} %get-tuple-element.26.chk, f32[928,128]{1,0:T(8,128)S(1)} %collective-permute-done.above, f32[928,128]{1,0:T(8,128)S(1)} %collective-permute-done.1.below, ...), custom_call_target="tpu_custom_call" | custom-call | flops 20000000 | bytes 6000000 | tf_op jit(solution)/shard_map/forward/pallas_call | solution.py:569
  58.9 0.0 collective-permute-done.6.swapped
  58.9 7.1 %adjoint.1 = (f32[2,4,32,128]{3,2,1,0:T(8,128)}, f32[32,128]{1,0:T(8,128)S(1)}) custom-call(f32[1]{0:T(128)S(6)} %div.18.scale, bf16[256,128]{1,0:T(8,128)(2,1)S(1)} %get-tuple-element.22.high, bf16[256,128]{1,0:T(8,128)(2,1)S(1)} %get-tuple-element.23.low, f32[928,128]{1,0:T(8,128)S(1)} %get-tuple-element.25.own, ...), custom_call_target="tpu_custom_call" | custom-call | tf_op jit(solution)/shard_map/adjoint/pallas_call | solution.py:584
  66.0 5.1 %all-gather = f32[128,128]{1,0:T(8,128)S(1)} all-gather(f32[32,128]{1,0:T(8,128)S(1)} %get-tuple-element.36), channel_id=2, replica_groups=mesh['vec'=4,'row'=8,'col'=16] {'vec'}, dimensions={0}, use_global_device_ids=true | all-gather | bytes 81920 | tf_op jit(solution)/shard_map/all_gather | solution.py:604
  71.1 0.6 reduce_sum.9
  (10 shorter events, 0.1 us)
Async XLA Ops:
  3.1 32.1 %collective-permute-start.1 = (f32[928,128]{1,0:T(8,128)S(1)}, f32[928,128]{1,0:T(8,128)S(1)}, u32[]{:S(2)}, u32[]{:S(2)}) collective-permute-start(f32[928,128]{1,0:T(8,128)S(1)} %get-tuple-element.24), channel_id=1, source_target_pairs={{0,112},{16,0},{32,16},{48,32},{64,48},{80,64},{96,80},{112,96},{1... | collective-permute-start | bytes 1425416 | tf_op jit(solution)/shard_map/ppermute | solution.py:516
  6.0 29.2 %collective-permute-start = (f32[928,128]{1,0:T(8,128)S(1)}, f32[928,128]{1,0:T(8,128)S(1)}, u32[]{:S(2)}, u32[]{:S(2)}) collective-permute-start(f32[928,128]{1,0:T(8,128)S(1)} %get-tuple-element.25.own), channel_id=1, source_target_pairs={{0,16},{16,32},{32,48},{48,64},{64,80},{80,96},{96,112},{112,0},{1... | collective-permute-start | bytes 1425416 | tf_op jit(solution)/shard_map/ppermute | solution.py:516
  18.3 26.6 %collective-permute-start.2 = (f32[232,128]{1,0:T(8,128)S(1)}, f32[232,128]{1,0:T(8,128)S(1)}, u32[]{:S(2)}, u32[]{:S(2)}) collective-permute-start(f32[232,128]{1,0:T(8,128)S(1)} %get-tuple-element.27), channel_id=1, source_target_pairs={{0,15},{1,0},{2,1},{3,2},{4,3},{5,4},{6,5},{7,6},{8,7},{9,8},{10,9... | collective-permute-start | bytes 356360 | tf_op jit(solution)/shard_map/ppermute | solution.py:516
  29.4 22.5 %collective-permute-start.3 = (f32[232,128]{1,0:T(8,128)S(1)}, f32[232,128]{1,0:T(8,128)S(1)}, u32[]{:S(2)}, u32[]{:S(2)}) collective-permute-start(f32[232,128]{1,0:T(8,128)S(1)} %get-tuple-element.28), channel_id=1, source_target_pairs={{0,1},{1,2},{2,3},{3,4},{4,5},{5,6},{6,7},{7,8},{8,9},{9,10},{10,1... | collective-permute-start | bytes 356360 | tf_op jit(solution)/shard_map/ppermute | solution.py:516
  35.5 11.5 %collective-permute-start.4 = (f32[400,128]{1,0:T(8,128)S(1)}, f32[400,128]{1,0:T(8,128)S(1)}, u32[]{:S(2)}, u32[]{:S(2)}) collective-permute-start(f32[400,128]{1,0:T(8,128)S(1)} %get-tuple-element.31), channel_id=1, source_target_pairs={{0,15},{1,0},{2,1},{3,2},{4,3},{5,4},{6,5},{7,6},{8,7},{9,8},{10,9... | collective-permute-start | bytes 614408 | tf_op jit(solution)/shard_map/ppermute | solution.py:516
  43.0 8.9 %collective-permute-start.5 = (f32[400,128]{1,0:T(8,128)S(1)}, f32[400,128]{1,0:T(8,128)S(1)}, u32[]{:S(2)}, u32[]{:S(2)}) collective-permute-start(f32[400,128]{1,0:T(8,128)S(1)} %get-tuple-element.32), channel_id=1, source_target_pairs={{0,1},{1,2},{2,3},{3,4},{4,5},{5,6},{6,7},{7,8},{8,9},{9,10},{10,1... | collective-permute-start | bytes 614408 | tf_op jit(solution)/shard_map/ppermute | solution.py:516
  52.0 6.9 %collective-permute-start.6 = (f32[896,128]{1,0:T(8,128)S(1)}, f32[896,128]{1,0:T(8,128)S(1)}, u32[]{:S(2)}, u32[]{:S(2)}) collective-permute-start(f32[896,128]{1,0:T(8,128)S(1)} %slice_dynamic-update-slice_fusion), channel_id=1, source_target_pairs={{0,128},{128,0},{256,384},{384,256},{1,129},{129,1},{257,385},{385... | collective-permute-start | bytes 1376264 | tf_op jit(solution)/shard_map/ppermute | solution.py:519

commit v9 on v8

--- a/solution.py
+++ b/solution.py
@@ -32,9 +32,19 @@
 OWN_ONS = GROUPS * ROWS
 OWN_CHK = OWN_ONS + 8
 OWN_ROWS = OWN_CHK + 2 * ROWS
-EDGE_ONS = GROUPS * 2 * HALO
-EDGE_CHK = EDGE_ONS + 16
+EDGE_FAR = GROUPS * HALO
+FAR_GROUPS = ((ADJ, 8), (RES, 8), (SGN, 4))
+EDGE_ONS = EDGE_FAR + len(FAR_GROUPS) * HALO
+EDGE_CHK = EDGE_ONS + 8
 EDGE_ROWS = EDGE_CHK + 4 * FHALO
+
+
+def near_index(t):
+    return t - 2 if t < 4 else t - 6
+
+
+def far_index(t):
+    return t if t < 2 else t - 8
 
 
 def window_coefs(first_segment, energies):
@@ -137,13 +147,21 @@
 
 
 def pack_edge_kernel(above, below, to_left, to_right):
+    def at(plane, t):
+        return main_tile(None, above, below, plane, t)
+
+    near, far = (2, 3, 8, 9), (0, 1, 10, 11)
+    for t in near:
+        for g in range(GROUPS):
+            tiles = [at(4 * g + j, t) for j in range(4)]
+            pack(tiles, g * HALO + near_index(t) * 8, to_left, to_right)
+    for t in far:
+        for g, (first, count) in enumerate(FAR_GROUPS):
+            tiles = [at(first + j, t) for j in range(count)]
+            tiles += [at(ONS, t)] * (8 - count)
+            pack(tiles, EDGE_FAR + g * HALO + far_index(t) * 8, to_left, to_right)
+    pack([at(ONS, t) for t in near], EDGE_ONS, to_left, to_right)
     for side, ref in enumerate((above, below)):
-        for g in range(GROUPS):
-            for i in range(4):
-                tiles = [tile(ref, (4 * g + j) * ROWS + i * 8) for j in range(4)]
-                pack(tiles, g * 2 * HALO + side * HALO + i * 8, to_left, to_right)
-        tiles = [tile(ref, ONS * ROWS + j * 8) for j in range(4)]
-        pack(tiles, EDGE_ONS + side * 8, to_left, to_right)
         for g in range(2):
             for i in range(2):
                 tiles = [tile(ref, MAIN + (8 * g + j) * FHALO + i * 8) for j in range(8)]
@@ -168,12 +186,19 @@
         g, j = index // 4, index % 4
         if 4 <= t < 8:
             return self.unpack(self.own, g * ROWS + (t - 4) * 8, j, 4, turns)
-        return self.unpack(self.edge, g * 2 * HALO + (t if t < 4 else t - 4) * 8, j, 4, turns)
+        if 2 <= t < 10:
+            return self.unpack(self.edge, g * HALO + near_index(t) * 8, j, 4, turns)
+        for g, (first, count) in enumerate(FAR_GROUPS):
+            if first <= index < first + count:
+                row = EDGE_FAR + g * HALO + far_index(t) * 8
+                return self.unpack(self.edge, row, index - first, 8, turns)
 
     def onsite(self, t, turns=(0, 1)):
         if 4 <= t < 8:
             return self.unpack(self.own, OWN_ONS, t - 4, 4, turns)
-        return self.unpack(self.edge, EDGE_ONS + t // 8 * 8, t % 4, 4, turns)
+        if 2 <= t < 10:
+            return self.unpack(self.edge, EDGE_ONS, near_index(t), 4, turns)
+        return self.unpack(self.edge, EDGE_FAR + 2 * HALO + far_index(t) * 8, 4, 8, turns)
 
     def checkpoint(self, plane, t, turns):
         g, j = plane // 8, plane % 8
@@ -183,18 +208,20 @@
         return self.unpack(self.edge, at, j, 8, turns)
 
 
-SWAP_OWN, SWAP_EDGE = 2 * ROWS, 4 * HALO
-SWAP_SIDE = SWAP_OWN + SWAP_EDGE
+SWAP_NEAR, SWAP_FAR = 2 * ROWS, 2 * ROWS + 2 * HALO
+SWAP_SIDE = SWAP_FAR + HALO
 SWAP_MAIN = 2 * SWAP_SIDE
 
 
 def swapped_strip(swapped, lane, e, t):
-    g, j = e // 4, e % 4
+    g, j, count = e // 4, e % 4, 4
     if 4 <= t < 8:
         row = g * ROWS + (t - 4) * 8
+    elif 2 <= t < 10:
+        row = SWAP_NEAR + g * HALO + near_index(t) * 8
     else:
-        row = SWAP_OWN + g * 2 * HALO + (t if t < 4 else t - 4) * 8
-    return unpack_strip((swapped, row), (swapped, SWAP_SIDE + row), lane, j, 4, (0, 1))
+        row, j, count = SWAP_FAR + far_index(t) * 8, e, 8
+    return unpack_strip((swapped, row), (swapped, SWAP_SIDE + row), lane, j, count, (0, 1))
 
 
 def splats(coef, t_term):
@@ -554,17 +581,13 @@
     weights, edge_strips = lax.optimization_barrier((weights, edge_strips))
     res_rows = slice(RES * ROWS, (RES + HALF) * ROWS)
     own_rows = slice(RES_GROUP * ROWS, GROUPS * ROWS)
-    edge_rows = slice(RES_GROUP * 2 * HALO, GROUPS * 2 * HALO)
-    swapped = swap_cores(
-        jnp.concatenate(
-            [
-                own_strips[0][own_rows], edge_strips[0][edge_rows],
-                own_strips[1][own_rows], edge_strips[1][edge_rows],
-                above[res_rows], below[res_rows],
-            ],
-            axis=0,
-        )
-    )
+    near_rows = slice(RES_GROUP * HALO, GROUPS * HALO)
+    far_rows = slice(EDGE_FAR + HALO, EDGE_FAR + 2 * HALO)
+    pieces = []
+    for mine, edge in zip(own_strips, edge_strips):
+        pieces += [mine[own_rows], edge[near_rows], edge[far_rows]]
+    pieces += [above[res_rows], below[res_rows]]
+    swapped = swap_cores(jnp.concatenate(pieces, axis=0))
     frame = (FPLANES, FEXT, LANES)
     states = pl.pallas_call(
         forward_kernel,

time: 72.1 us -> 71.2 us (0.988)
  the two profiles are of different devices: /device:TPU:31 before, /device:TPU:23 now
where the time goes in v9:
time: 71.2 us; the launch traced here: 70.9 us
  starting transfers between devices  34.9 us (49%)
  Pallas kernels  16.4 us (23%)
  waiting for transfers between devices  6.21 us (9%)
  blocking collectives  5.07 us (7%)
  other arithmetic  3.25 us (5%)
  local copies, waits for them, and re-layouts  2.77 us (4%)
  between operations  2.19 us (3%)
    ppermute x6, starting transfers between devices, shift(): return lax.ppermute(value, axis, [(i, (i + step) % n) for i in range(n)])  31.4 us
    pallas_call x1, Pallas kernels, per_device(): pl.pallas_call(adjoint_kernel, out_shape=(jax.ShapeDtypeStruct((2, 4, ROW...  7.09 us
    ppermute x6, waiting for transfers between devices, shift(): return lax.ppermute(value, axis, [(i, (i + step) % n) for i in range(n)])  6.2 us
    all_gather x1, blocking collectives, per_device(): grad = jnp.sum(lax.all_gather(grad, 'vec'), axis=0)  5.07 us
    pallas_call x1, Pallas kernels, per_device(): pl.pallas_call(weights_kernel, out_shape=jax.ShapeDtypeStruct((2, TERMS,...  3.85 us
    ppermute x1, starting transfers between devices, swap_cores(): return lax.ppermute(value, 'vec', [(0, 1), (1, 0), (2, 3), (3, 2)])  3.57 us
    pallas_call x1, Pallas kernels, per_device(): pl.pallas_call(forward_kernel, out_shape=jax.ShapeDtypeStruct((TERMS, 4,...  3.22 us
    mul x1, local copies, waits for them, and re-layouts, per_device(): coefs[:, None, :, None] * jnp.eye(8, dtype=F32)[None, :, None, :]  2.65 us
  transfers between devices with their start and end apart: 7, of which 2 were waited for; matrix products, arithmetic and copies ran while one was open for 8% of the time, Pallas kernels for 11%

profile of v9, /device:TPU:23, one launch (start us, length us, event | category | flops | bytes accessed | tf_op | source)
XLA Modules:
  0.0 70.9 jit_solution(15003082273462404345)
XLA Ops:
  1.3 1.8 %prepare.1 = (f32[928,128]{1,0:T(8,128)S(1)}, f32[928,128]{1,0:T(8,128)S(1)}, f32[512,128]{1,0:T(8,128)S(1)}, f32[256,128]{1,0:T(8,128)S(1)}) custom-call(s32[1]{0:T(128)} %bitcast.1.core, f32[1]{0:T(128)S(6)} %copy.17.scalar, f32[256,128]{1,0:T(8,128)} %bitcast.12, s32[128,128]{1,0:T(8,128)} %bitcast.13, s32[32,128]{1,0:T(8,128)} %pot.1, ...), custom_call_target="tpu_custom_call" | custom-call | tf_op jit(solution)/shard_map/prepare/pallas_call | solution.py:509
  3.1 2.0 %collective-permute-start.1 = (f32[928,128]{1,0:T(8,128)S(1)}, f32[928,128]{1,0:T(8,128)S(1)}, u32[]{:S(2)}, u32[]{:S(2)}) collective-permute-start(f32[928,128]{1,0:T(8,128)S(1)} %get-tuple-element.24), channel_id=1, source_target_pairs={{0,112},{16,0},{32,16},{48,32},{64,48},{80,64},{96,80},{112,96},{1... | collective-permute-start | bytes 1425416 | tf_op jit(solution)/shard_map/ppermute | solution.py:543
  5.1 6.9 %collective-permute-start = (f32[928,128]{1,0:T(8,128)S(1)}, f32[928,128]{1,0:T(8,128)S(1)}, u32[]{:S(2)}, u32[]{:S(2)}) collective-permute-start(f32[928,128]{1,0:T(8,128)S(1)} %get-tuple-element.25.own), channel_id=1, source_target_pairs={{0,16},{16,32},{32,48},{48,64},{64,80},{80,96},{96,112},{112,0},{1... | collective-permute-start | bytes 1425416 | tf_op jit(solution)/shard_map/ppermute | solution.py:543
  12.7 0.7 %sine_multiply_fusion = (f32[16]{0:T(128)S(1)}, f32[16]{0:T(128)S(1)}) fusion(f32[16]{0:T(128)} %param.13), kind=kLoop, calls=%fused_computation.18 | loop fusion | flops 64 | bytes 192 | tf_op jit(solution)/shard_map/mul | solution.py:62
  13.5 0.1 multiply_divide_fusion
  13.6 0.1 fusion.4
  13.7 0.1 maximum_select_fusion.coef
  13.8 1.5 %broadcast_multiply_fusion = f32[32,8,16,8]{3,2,1,0:T(8,128)} fusion(f32[8,8]{1,0:T(8,128)S(1)} %fusion.1, f32[32,16]{1,0:T(8,128)S(1)} %maximum_select_fusion.coef), kind=kLoop, calls=%fused_computation | loop fusion | flops 32768 | bytes 133376 | tf_op jit(solution)/shard_map/mul | solution.py:563
  15.4 2.6 %mul.107 = f32[256,128]{1,0:T(8,128)S(1)} reshape(f32[32,8,16,8]{3,2,1,0:T(8,128)} %broadcast_multiply_fusion) | data formatting | bytes 262144 | tf_op jit(solution)/shard_map/mul | solution.py:563
  18.1 0.2 pack_own.1
  18.3 11.1 %collective-permute-start.2 = (f32[232,128]{1,0:T(8,128)S(1)}, f32[232,128]{1,0:T(8,128)S(1)}, u32[]{:S(2)}, u32[]{:S(2)}) collective-permute-start(f32[232,128]{1,0:T(8,128)S(1)} %get-tuple-element.27), channel_id=1, source_target_pairs={{0,15},{1,0},{2,1},{3,2},{4,3},{5,4},{6,5},{7,6},{8,7},{9,8},{10,9... | collective-permute-start | bytes 356360 | tf_op jit(solution)/shard_map/ppermute | solution.py:543
  29.4 1.9 %collective-permute-start.3 = (f32[232,128]{1,0:T(8,128)S(1)}, f32[232,128]{1,0:T(8,128)S(1)}, u32[]{:S(2)}, u32[]{:S(2)}) collective-permute-start(f32[232,128]{1,0:T(8,128)S(1)} %get-tuple-element.28), channel_id=1, source_target_pairs={{0,1},{1,2},{2,3},{3,4},{4,5},{5,6},{6,7},{7,8},{8,9},{9,10},{10,1... | collective-permute-start | bytes 356360 | tf_op jit(solution)/shard_map/ppermute | solution.py:543
  31.3 3.9 %weights.1.own_weights = f32[2,32,32,128]{3,2,1,0:T(8,128)S(1)} custom-call(f32[32,16]{1,0:T(8,128)S(1)} %maximum_select_fusion.coef, f32[928,128]{1,0:T(8,128)S(1)} %get-tuple-element.25.own, f32[256,128]{1,0:T(8,128)S(1)} %get-tuple-element.30.res_other), custom_call_target="tpu_custom_call" | custom-call | flops 4000000 | bytes 1000000 | tf_op jit(solution)/shard_map/weights/pallas_call | solution.py:571
  35.2 0.0 collective-permute-done.1.below
  35.2 0.0 collective-permute-done.above
  35.2 0.3 pack_edge.1
  35.5 7.5 %collective-permute-start.4 = (f32[328,128]{1,0:T(8,128)S(1)}, f32[328,128]{1,0:T(8,128)S(1)}, u32[]{:S(2)}, u32[]{:S(2)}) collective-permute-start(f32[328,128]{1,0:T(8,128)S(1)} %get-tuple-element.31), channel_id=1, source_target_pairs={{0,15},{1,0},{2,1},{3,2},{4,3},{5,4},{6,5},{7,6},{8,7},{9,8},{10,9... | collective-permute-start | bytes 503816 | tf_op jit(solution)/shard_map/ppermute | solution.py:543
  43.0 1.9 %collective-permute-start.5 = (f32[328,128]{1,0:T(8,128)S(1)}, f32[328,128]{1,0:T(8,128)S(1)}, u32[]{:S(2)}, u32[]{:S(2)}) collective-permute-start(f32[328,128]{1,0:T(8,128)S(1)} %get-tuple-element.32), channel_id=1, source_target_pairs={{0,1},{1,2},{2,3},{3,4},{4,5},{5,6},{6,7},{7,8},{8,9},{9,10},{10,1... | collective-permute-start | bytes 503816 | tf_op jit(solution)/shard_map/ppermute | solution.py:543
  44.9 0.0 collective-permute-done.2.own_right
  44.9 1.2 %collective-permute-done.4.edge_right = f32[328,128]{1,0:T(8,128)S(1)} collective-permute-done((f32[328,128]{1,0:T(8,128)S(1)}, f32[328,128]{1,0:T(8,128)S(1)}, u32[]{:S(2)}, u32[]{:S(2)}) %collective-permute-start.4) | collective-permute-done | bytes 167968 | tf_op jit(solution)/shard_map/ppermute | solution.py:543
  46.1 5.0 %collective-permute-done.5.edge_left = f32[328,128]{1,0:T(8,128)S(1)} collective-permute-done((f32[328,128]{1,0:T(8,128)S(1)}, f32[328,128]{1,0:T(8,128)S(1)}, u32[]{:S(2)}, u32[]{:S(2)}) %collective-permute-start.5) | collective-permute-done | bytes 167968 | tf_op jit(solution)/shard_map/ppermute | solution.py:543
  51.1 0.0 collective-permute-done.3.own_left
  51.2 3.6 %collective-permute-start.6 = (f32[832,128]{1,0:T(8,128)S(1)}, f32[832,128]{1,0:T(8,128)S(1)}, u32[]{:S(2)}, u32[]{:S(2)}) collective-permute-start(f32[832,128]{1,0:T(8,128)S(1)} %slice_dynamic-update-slice_fusion), channel_id=1, source_target_pairs={{0,128},{128,0},{256,384},{384,256},{1,129},{129,1},{257,385},{385... | collective-permute-start | bytes 1277960 | tf_op jit(solution)/shard_map/ppermute | solution.py:546
  54.9 3.2 %forward.1.vs = f32[32,4,32,128]{3,2,1,0:T(8,128)S(1)} custom-call(f32[1]{0:T(128)S(6)} %div.18.scale, f32[928,128]{1,0:T(8,128)S(1)} %get-tuple-element.25.own, f32[512,128]{1,0:T(8,128)S(1)} %get-tuple-element.26.chk, f32[928,128]{1,0:T(8,128)S(1)} %collective-permute-done.above, f32[928,128]{1,0:T(8,128)S(1)} %collective-permute-done.1.below, ...), custom_call_target="tpu_custom_call" | custom-call | flops 20000000 | bytes 6000000 | tf_op jit(solution)/shard_map/forward/pallas_call | solution.py:592
  58.1 0.0 collective-permute-done.6.swapped
  58.1 7.1 %adjoint.1 = (f32[2,4,32,128]{3,2,1,0:T(8,128)}, f32[32,128]{1,0:T(8,128)S(1)}) custom-call(f32[1]{0:T(128)S(6)} %div.18.scale, bf16[256,128]{1,0:T(8,128)(2,1)S(1)} %get-tuple-element.22.high, bf16[256,128]{1,0:T(8,128)(2,1)S(1)} %get-tuple-element.23.low, f32[928,128]{1,0:T(8,128)S(1)} %get-tuple-element.25.own, ...), custom_call_target="tpu_custom_call" | custom-call | tf_op jit(solution)/shard_map/adjoint/pallas_call | solution.py:607
  65.2 5.1 %all-gather = f32[128,128]{1,0:T(8,128)S(1)} all-gather(f32[32,128]{1,0:T(8,128)S(1)} %get-tuple-element.36), channel_id=2, replica_groups=mesh['vec'=4,'row'=8,'col'=16] {'vec'}, dimensions={0}, use_global_device_ids=true | all-gather | bytes 81920 | tf_op jit(solution)/shard_map/all_gather | solution.py:627
  70.3 0.6 reduce_sum.9
  (12 shorter events, 0.1 us)
Async XLA Ops:
  3.1 32.1 %collective-permute-start.1 = (f32[928,128]{1,0:T(8,128)S(1)}, f32[928,128]{1,0:T(8,128)S(1)}, u32[]{:S(2)}, u32[]{:S(2)}) collective-permute-start(f32[928,128]{1,0:T(8,128)S(1)} %get-tuple-element.24), channel_id=1, source_target_pairs={{0,112},{16,0},{32,16},{48,32},{64,48},{80,64},{96,80},{112,96},{1... | collective-permute-start | bytes 1425416 | tf_op jit(solution)/shard_map/ppermute | solution.py:543
  5.1 30.1 %collective-permute-start = (f32[928,128]{1,0:T(8,128)S(1)}, f32[928,128]{1,0:T(8,128)S(1)}, u32[]{:S(2)}, u32[]{:S(2)}) collective-permute-start(f32[928,128]{1,0:T(8,128)S(1)} %get-tuple-element.25.own), channel_id=1, source_target_pairs={{0,16},{16,32},{32,48},{48,64},{64,80},{80,96},{96,112},{112,0},{1... | collective-permute-start | bytes 1425416 | tf_op jit(solution)/shard_map/ppermute | solution.py:543
  18.3 26.7 %collective-permute-start.2 = (f32[232,128]{1,0:T(8,128)S(1)}, f32[232,128]{1,0:T(8,128)S(1)}, u32[]{:S(2)}, u32[]{:S(2)}) collective-permute-start(f32[232,128]{1,0:T(8,128)S(1)} %get-tuple-element.27), channel_id=1, source_target_pairs={{0,15},{1,0},{2,1},{3,2},{4,3},{5,4},{6,5},{7,6},{8,7},{9,8},{10,9... | collective-permute-start | bytes 356360 | tf_op jit(solution)/shard_map/ppermute | solution.py:543
  29.4 21.7 %collective-permute-start.3 = (f32[232,128]{1,0:T(8,128)S(1)}, f32[232,128]{1,0:T(8,128)S(1)}, u32[]{:S(2)}, u32[]{:S(2)}) collective-permute-start(f32[232,128]{1,0:T(8,128)S(1)} %get-tuple-element.28), channel_id=1, source_target_pairs={{0,1},{1,2},{2,3},{3,4},{4,5},{5,6},{6,7},{7,8},{8,9},{9,10},{10,1... | collective-permute-start | bytes 356360 | tf_op jit(solution)/shard_map/ppermute | solution.py:543
  35.5 10.7 %collective-permute-start.4 = (f32[328,128]{1,0:T(8,128)S(1)}, f32[328,128]{1,0:T(8,128)S(1)}, u32[]{:S(2)}, u32[]{:S(2)}) collective-permute-start(f32[328,128]{1,0:T(8,128)S(1)} %get-tuple-element.31), channel_id=1, source_target_pairs={{0,15},{1,0},{2,1},{3,2},{4,3},{5,4},{6,5},{7,6},{8,7},{9,8},{10,9... | collective-permute-start | bytes 503816 | tf_op jit(solution)/shard_map/ppermute | solution.py:543
  43.0 8.1 %collective-permute-start.5 = (f32[328,128]{1,0:T(8,128)S(1)}, f32[328,128]{1,0:T(8,128)S(1)}, u32[]{:S(2)}, u32[]{:S(2)}) collective-permute-start(f32[328,128]{1,0:T(8,128)S(1)} %get-tuple-element.32), channel_id=1, source_target_pairs={{0,1},{1,2},{2,3},{3,4},{4,5},{5,6},{6,7},{7,8},{8,9},{9,10},{10,1... | collective-permute-start | bytes 503816 | tf_op jit(solution)/shard_map/ppermute | solution.py:543
  51.2 6.9 %collective-permute-start.6 = (f32[832,128]{1,0:T(8,128)S(1)}, f32[832,128]{1,0:T(8,128)S(1)}, u32[]{:S(2)}, u32[]{:S(2)}) collective-permute-start(f32[832,128]{1,0:T(8,128)S(1)} %slice_dynamic-update-slice_fusion), channel_id=1, source_target_pairs={{0,128},{128,0},{256,384},{384,256},{1,129},{129,1},{257,385},{385... | collective-permute-start | bytes 1277960 | tf_op jit(solution)/shard_map/ppermute | solution.py:546

commit v10 on v9

--- a/solution.py
+++ b/solution.py
@@ -359,24 +359,26 @@
         at = segment * 4 + which * 2 + pair
         return [fc.at[2 * at], fc.at[2 * at + 1], fh.at[at]]
 
-    def forward(k, new, old, lo, hi):
+    def forward(k, new, old, lo, hi, planes=3):
         for segment in range(2):
             for pair in range(2):
                 target = group(segment, old, pair)
                 for t, values, sums in stencil.tiles(group(segment, new, pair), lo, hi, FEXT // 8):
                     row = pl.ds(t * 8, 8)
-                    for m in range(3):
+                    for m in range(planes):
                         value = on[m, row, :] * values[m] - s * sums[m] - target[m][row, :]
                         target[m][row, :] = value
                         if m < 2 and 2 <= t < 6:
                             vs[segment * SEG + k, 2 * pair + m, pl.ds((t - 2) * 8, 8), :] = value
 
-    for start, stop, lo, hi in ((1, 4, 0, 8), (4, 8, 1, 7)):
+    for start, stop, lo, hi in ((1, 3, 0, 8), (4, 7, 1, 7)):
         def body(i, carry, lo=lo, hi=hi):
             forward(2 * i, 1, 0, lo, hi)
             forward(2 * i + 1, 0, 1, lo, hi)
             return carry
         lax.fori_loop(start, stop, body, 0)
+        forward(2 * stop, 1, 0, lo, hi)
+        forward(2 * stop + 1, 0, 1, lo + 1, hi - 1, 3 if lo == 0 else 2)
 
 
 def adjoint_kernel(
@@ -442,7 +444,7 @@
             centre = [wcs[t_term, row, :], wts[t_term, row, :]]
         return centre + [whs[t_term, row, :]]
 
-    def adjoint(t_term, new, old, lo, hi, grads):
+    def adjoint(t_term, new, old, lo, hi, grads, planes=3):
         grads = list(grads)
         for pair in range(2):
             target = group(old, pair)
@@ -454,7 +456,7 @@
                         state = vs[t_term, 2 * pair + m, pl.ds((t - 4) * 8, 8), :]
                         grads[at] = grads[at] + values[m] * state
                 weights = weights_of(t_term, t)
-                for m in range(3):
+                for m in range(planes):
                     target[m][row, :] = (
                         weights[m] * sg[3 * pair + m, row, :]
                         + (on[m, row, :] * values[m] - s * sums[m])
@@ -469,7 +471,10 @@
             t_term = TERMS - 1 - 8 * phase - 2 * i
             carry = adjoint(t_term, 0, 1, lo, hi, carry)
             return adjoint(t_term - 1, 1, 0, lo, hi, carry)
-        grads = lax.fori_loop(0, 4, body, grads)
+        grads = lax.fori_loop(0, 3, body, grads)
+        last = TERMS - 8 * (phase + 1)
+        grads = adjoint(last + 1, 0, 1, lo, hi, grads)
+        grads = adjoint(last, 1, 0, lo + 1, hi - 1, grads, 3 if phase < 3 else 2)
     for i in range(4):
         grad_out[pl.ds(i * 8, 8), :] = (grads[i] + turned(grads[4 + i])) * s
     for which in range(2):

time: 71.2 us -> 71 us (level)
  no operation moved by 1% of the time
where the time goes in v10:
time: 71 us; the launch traced here: 70.6 us
  starting transfers between devices  34.9 us (49%)
  Pallas kernels  16.2 us (23%)
  waiting for transfers between devices  6.21 us (9%)
  blocking collectives  5.07 us (7%)
  other arithmetic  3.25 us (5%)
  local copies, waits for them, and re-layouts  2.77 us (4%)
  between operations  2.19 us (3%)
    ppermute x6, starting transfers between devices, shift(): return lax.ppermute(value, axis, [(i, (i + step) % n) for i in range(n)])  31.4 us
    pallas_call x1, Pallas kernels, per_device(): pl.pallas_call(adjoint_kernel, out_shape=(jax.ShapeDtypeStruct((2, 4, ROW...  6.96 us
    ppermute x6, waiting for transfers between devices, shift(): return lax.ppermute(value, axis, [(i, (i + step) % n) for i in range(n)])  6.2 us
    all_gather x1, blocking collectives, per_device(): grad = jnp.sum(lax.all_gather(grad, 'vec'), axis=0)  5.07 us
    pallas_call x1, Pallas kernels, per_device(): pl.pallas_call(weights_kernel, out_shape=jax.ShapeDtypeStruct((2, TERMS,...  3.85 us
    ppermute x1, starting transfers between devices, swap_cores(): return lax.ppermute(value, 'vec', [(0, 1), (1, 0), (2, 3), (3, 2)])  3.57 us
    pallas_call x1, Pallas kernels, per_device(): pl.pallas_call(forward_kernel, out_shape=jax.ShapeDtypeStruct((TERMS, 4,...  3.11 us
    mul x1, local copies, waits for them, and re-layouts, per_device(): coefs[:, None, :, None] * jnp.eye(8, dtype=F32)[None, :, None, :]  2.65 us
  transfers between devices with their start and end apart: 7, of which 2 were waited for; matrix products, arithmetic and copies ran while one was open for 8% of the time, Pallas kernels for 11%

profile of v10, /device:TPU:23, one launch (start us, length us, event | category | flops | bytes accessed | tf_op | source)
XLA Modules:
  0.0 70.6 jit_solution(11629787754419790715)
XLA Ops:
  1.3 1.8 %prepare.1 = (f32[928,128]{1,0:T(8,128)S(1)}, f32[928,128]{1,0:T(8,128)S(1)}, f32[512,128]{1,0:T(8,128)S(1)}, f32[256,128]{1,0:T(8,128)S(1)}) custom-call(s32[1]{0:T(128)} %bitcast.1.core, f32[1]{0:T(128)S(6)} %copy.17.scalar, f32[256,128]{1,0:T(8,128)} %bitcast.12, s32[128,128]{1,0:T(8,128)} %bitcast.13, s32[32,128]{1,0:T(8,128)} %pot.1, ...), custom_call_target="tpu_custom_call" | custom-call | tf_op jit(solution)/shard_map/prepare/pallas_call | solution.py:514
  3.1 2.0 %collective-permute-start.1 = (f32[928,128]{1,0:T(8,128)S(1)}, f32[928,128]{1,0:T(8,128)S(1)}, u32[]{:S(2)}, u32[]{:S(2)}) collective-permute-start(f32[928,128]{1,0:T(8,128)S(1)} %get-tuple-element.24), channel_id=1, source_target_pairs={{0,112},{16,0},{32,16},{48,32},{64,48},{80,64},{96,80},{112,96},{1... | collective-permute-start | bytes 1425416 | tf_op jit(solution)/shard_map/ppermute | solution.py:548
  5.1 6.9 %collective-permute-start = (f32[928,128]{1,0:T(8,128)S(1)}, f32[928,128]{1,0:T(8,128)S(1)}, u32[]{:S(2)}, u32[]{:S(2)}) collective-permute-start(f32[928,128]{1,0:T(8,128)S(1)} %get-tuple-element.25.own), channel_id=1, source_target_pairs={{0,16},{16,32},{32,48},{48,64},{64,80},{80,96},{96,112},{112,0},{1... | collective-permute-start | bytes 1425416 | tf_op jit(solution)/shard_map/ppermute | solution.py:548
  12.7 0.7 %sine_multiply_fusion = (f32[16]{0:T(128)S(1)}, f32[16]{0:T(128)S(1)}) fusion(f32[16]{0:T(128)} %param.13), kind=kLoop, calls=%fused_computation.18 | loop fusion | flops 64 | bytes 192 | tf_op jit(solution)/shard_map/mul | solution.py:62
  13.5 0.1 multiply_divide_fusion
  13.6 0.1 fusion.4
  13.7 0.1 maximum_select_fusion.coef
  13.8 1.5 %broadcast_multiply_fusion = f32[32,8,16,8]{3,2,1,0:T(8,128)} fusion(f32[8,8]{1,0:T(8,128)S(1)} %fusion.1, f32[32,16]{1,0:T(8,128)S(1)} %maximum_select_fusion.coef), kind=kLoop, calls=%fused_computation | loop fusion | flops 32768 | bytes 133376 | tf_op jit(solution)/shard_map/mul | solution.py:568
  15.4 2.6 %mul.107 = f32[256,128]{1,0:T(8,128)S(1)} reshape(f32[32,8,16,8]{3,2,1,0:T(8,128)} %broadcast_multiply_fusion) | data formatting | bytes 262144 | tf_op jit(solution)/shard_map/mul | solution.py:568
  18.1 0.2 pack_own.1
  18.3 11.1 %collective-permute-start.2 = (f32[232,128]{1,0:T(8,128)S(1)}, f32[232,128]{1,0:T(8,128)S(1)}, u32[]{:S(2)}, u32[]{:S(2)}) collective-permute-start(f32[232,128]{1,0:T(8,128)S(1)} %get-tuple-element.27), channel_id=1, source_target_pairs={{0,15},{1,0},{2,1},{3,2},{4,3},{5,4},{6,5},{7,6},{8,7},{9,8},{10,9... | collective-permute-start | bytes 356360 | tf_op jit(solution)/shard_map/ppermute | solution.py:548
  29.4 1.9 %collective-permute-start.3 = (f32[232,128]{1,0:T(8,128)S(1)}, f32[232,128]{1,0:T(8,128)S(1)}, u32[]{:S(2)}, u32[]{:S(2)}) collective-permute-start(f32[232,128]{1,0:T(8,128)S(1)} %get-tuple-element.28), channel_id=1, source_target_pairs={{0,1},{1,2},{2,3},{3,4},{4,5},{5,6},{6,7},{7,8},{8,9},{9,10},{10,1... | collective-permute-start | bytes 356360 | tf_op jit(solution)/shard_map/ppermute | solution.py:548
  31.3 3.9 %weights.1.own_weights = f32[2,32,32,128]{3,2,1,0:T(8,128)S(1)} custom-call(f32[32,16]{1,0:T(8,128)S(1)} %maximum_select_fusion.coef, f32[928,128]{1,0:T(8,128)S(1)} %get-tuple-element.25.own, f32[256,128]{1,0:T(8,128)S(1)} %get-tuple-element.30.res_other), custom_call_target="tpu_custom_call" | custom-call | flops 4000000 | bytes 1000000 | tf_op jit(solution)/shard_map/weights/pallas_call | solution.py:576
  35.2 0.0 collective-permute-done.1.below
  35.2 0.0 collective-permute-done.above
  35.2 0.3 pack_edge.1
  35.5 7.5 %collective-permute-start.4 = (f32[328,128]{1,0:T(8,128)S(1)}, f32[328,128]{1,0:T(8,128)S(1)}, u32[]{:S(2)}, u32[]{:S(2)}) collective-permute-start(f32[328,128]{1,0:T(8,128)S(1)} %get-tuple-element.31), channel_id=1, source_target_pairs={{0,15},{1,0},{2,1},{3,2},{4,3},{5,4},{6,5},{7,6},{8,7},{9,8},{10,9... | collective-permute-start | bytes 503816 | tf_op jit(solution)/shard_map/ppermute | solution.py:548
  43.0 1.9 %collective-permute-start.5 = (f32[328,128]{1,0:T(8,128)S(1)}, f32[328,128]{1,0:T(8,128)S(1)}, u32[]{:S(2)}, u32[]{:S(2)}) collective-permute-start(f32[328,128]{1,0:T(8,128)S(1)} %get-tuple-element.32), channel_id=1, source_target_pairs={{0,1},{1,2},{2,3},{3,4},{4,5},{5,6},{6,7},{7,8},{8,9},{9,10},{10,1... | collective-permute-start | bytes 503816 | tf_op jit(solution)/shard_map/ppermute | solution.py:548
  44.9 0.0 collective-permute-done.2.own_right
  44.9 1.2 %collective-permute-done.4.edge_right = f32[328,128]{1,0:T(8,128)S(1)} collective-permute-done((f32[328,128]{1,0:T(8,128)S(1)}, f32[328,128]{1,0:T(8,128)S(1)}, u32[]{:S(2)}, u32[]{:S(2)}) %collective-permute-start.4) | collective-permute-done | bytes 167968 | tf_op jit(solution)/shard_map/ppermute | solution.py:548
  46.1 5.0 %collective-permute-done.5.edge_left = f32[328,128]{1,0:T(8,128)S(1)} collective-permute-done((f32[328,128]{1,0:T(8,128)S(1)}, f32[328,128]{1,0:T(8,128)S(1)}, u32[]{:S(2)}, u32[]{:S(2)}) %collective-permute-start.5) | collective-permute-done | bytes 167968 | tf_op jit(solution)/shard_map/ppermute | solution.py:548
  51.1 0.0 collective-permute-done.3.own_left
  51.2 3.6 %collective-permute-start.6 = (f32[832,128]{1,0:T(8,128)S(1)}, f32[832,128]{1,0:T(8,128)S(1)}, u32[]{:S(2)}, u32[]{:S(2)}) collective-permute-start(f32[832,128]{1,0:T(8,128)S(1)} %slice_dynamic-update-slice_fusion), channel_id=1, source_target_pairs={{0,128},{128,0},{256,384},{384,256},{1,129},{129,1},{257,385},{385... | collective-permute-start | bytes 1277960 | tf_op jit(solution)/shard_map/ppermute | solution.py:551
  54.9 3.1 %forward.1.vs = f32[32,4,32,128]{3,2,1,0:T(8,128)S(1)} custom-call(f32[1]{0:T(128)S(6)} %div.18.scale, f32[928,128]{1,0:T(8,128)S(1)} %get-tuple-element.25.own, f32[512,128]{1,0:T(8,128)S(1)} %get-tuple-element.26.chk, f32[928,128]{1,0:T(8,128)S(1)} %collective-permute-done.above, f32[928,128]{1,0:T(8,128)S(1)} %collective-permute-done.1.below, ...), custom_call_target="tpu_custom_call" | custom-call | flops 20000000 | bytes 6000000 | tf_op jit(solution)/shard_map/forward/pallas_call | solution.py:597
  58.0 0.0 collective-permute-done.6.swapped
  58.0 7.0 %adjoint.1 = (f32[2,4,32,128]{3,2,1,0:T(8,128)}, f32[32,128]{1,0:T(8,128)S(1)}) custom-call(f32[1]{0:T(128)S(6)} %div.18.scale, bf16[256,128]{1,0:T(8,128)(2,1)S(1)} %get-tuple-element.22.high, bf16[256,128]{1,0:T(8,128)(2,1)S(1)} %get-tuple-element.23.low, f32[928,128]{1,0:T(8,128)S(1)} %get-tuple-element.25.own, ...), custom_call_target="tpu_custom_call" | custom-call | tf_op jit(solution)/shard_map/adjoint/pallas_call | solution.py:612
  64.9 5.1 %all-gather = f32[128,128]{1,0:T(8,128)S(1)} all-gather(f32[32,128]{1,0:T(8,128)S(1)} %get-tuple-element.36), channel_id=2, replica_groups=mesh['vec'=4,'row'=8,'col'=16] {'vec'}, dimensions={0}, use_global_device_ids=true | all-gather | bytes 81920 | tf_op jit(solution)/shard_map/all_gather | solution.py:632
  70.0 0.6 reduce_sum.9
  (12 shorter events, 0.1 us)
Async XLA Ops:
  3.1 32.1 %collective-permute-start.1 = (f32[928,128]{1,0:T(8,128)S(1)}, f32[928,128]{1,0:T(8,128)S(1)}, u32[]{:S(2)}, u32[]{:S(2)}) collective-permute-start(f32[928,128]{1,0:T(8,128)S(1)} %get-tuple-element.24), channel_id=1, source_target_pairs={{0,112},{16,0},{32,16},{48,32},{64,48},{80,64},{96,80},{112,96},{1... | collective-permute-start | bytes 1425416 | tf_op jit(solution)/shard_map/ppermute | solution.py:548
  5.1 30.1 %collective-permute-start = (f32[928,128]{1,0:T(8,128)S(1)}, f32[928,128]{1,0:T(8,128)S(1)}, u32[]{:S(2)}, u32[]{:S(2)}) collective-permute-start(f32[928,128]{1,0:T(8,128)S(1)} %get-tuple-element.25.own), channel_id=1, source_target_pairs={{0,16},{16,32},{32,48},{48,64},{64,80},{80,96},{96,112},{112,0},{1... | collective-permute-start | bytes 1425416 | tf_op jit(solution)/shard_map/ppermute | solution.py:548
  18.3 26.7 %collective-permute-start.2 = (f32[232,128]{1,0:T(8,128)S(1)}, f32[232,128]{1,0:T(8,128)S(1)}, u32[]{:S(2)}, u32[]{:S(2)}) collective-permute-start(f32[232,128]{1,0:T(8,128)S(1)} %get-tuple-element.27), channel_id=1, source_target_pairs={{0,15},{1,0},{2,1},{3,2},{4,3},{5,4},{6,5},{7,6},{8,7},{9,8},{10,9... | collective-permute-start | bytes 356360 | tf_op jit(solution)/shard_map/ppermute | solution.py:548
  29.4 21.7 %collective-permute-start.3 = (f32[232,128]{1,0:T(8,128)S(1)}, f32[232,128]{1,0:T(8,128)S(1)}, u32[]{:S(2)}, u32[]{:S(2)}) collective-permute-start(f32[232,128]{1,0:T(8,128)S(1)} %get-tuple-element.28), channel_id=1, source_target_pairs={{0,1},{1,2},{2,3},{3,4},{4,5},{5,6},{6,7},{7,8},{8,9},{9,10},{10,1... | collective-permute-start | bytes 356360 | tf_op jit(solution)/shard_map/ppermute | solution.py:548
  35.5 10.7 %collective-permute-start.4 = (f32[328,128]{1,0:T(8,128)S(1)}, f32[328,128]{1,0:T(8,128)S(1)}, u32[]{:S(2)}, u32[]{:S(2)}) collective-permute-start(f32[328,128]{1,0:T(8,128)S(1)} %get-tuple-element.31), channel_id=1, source_target_pairs={{0,15},{1,0},{2,1},{3,2},{4,3},{5,4},{6,5},{7,6},{8,7},{9,8},{10,9... | collective-permute-start | bytes 503816 | tf_op jit(solution)/shard_map/ppermute | solution.py:548
  43.0 8.1 %collective-permute-start.5 = (f32[328,128]{1,0:T(8,128)S(1)}, f32[328,128]{1,0:T(8,128)S(1)}, u32[]{:S(2)}, u32[]{:S(2)}) collective-permute-start(f32[328,128]{1,0:T(8,128)S(1)} %get-tuple-element.32), channel_id=1, source_target_pairs={{0,1},{1,2},{2,3},{3,4},{4,5},{5,6},{6,7},{7,8},{8,9},{9,10},{10,1... | collective-permute-start | bytes 503816 | tf_op jit(solution)/shard_map/ppermute | solution.py:548
  51.2 6.7 %collective-permute-start.6 = (f32[832,128]{1,0:T(8,128)S(1)}, f32[832,128]{1,0:T(8,128)S(1)}, u32[]{:S(2)}, u32[]{:S(2)}) collective-permute-start(f32[832,128]{1,0:T(8,128)S(1)} %slice_dynamic-update-slice_fusion), channel_id=1, source_target_pairs={{0,128},{128,0},{256,384},{384,256},{1,129},{129,1},{257,385},{385... | collective-permute-start | bytes 1277960 | tf_op jit(solution)/shard_map/ppermute | solution.py:551

commit v11 on v10

--- a/solution.py
+++ b/solution.py
@@ -100,11 +100,10 @@
     for out, first in ((to_below, ROWS - FHALO), (to_above, 0)):
         start(adj, out.at[pl.ds(ADJ * ROWS, 8 * ROWS)])
         start(res.at[pl.ds(first_res, HALF * ROWS)], out.at[pl.ds(RES * ROWS, HALF * ROWS)])
-        for plane in range(FPLANES):
-            start(
-                chk.at[pl.ds(plane * ROWS + first, FHALO)],
-                out.at[pl.ds(MAIN + plane * FHALO, FHALO)],
-            )
+        start(
+            chk.reshape(FPLANES, ROWS, LANES).at[:, pl.ds(first, FHALO)],
+            out.at[pl.ds(MAIN, FPLANES * FHALO)].reshape(FPLANES, FHALO, LANES),
+        )
     start(chk, chk_v)
     start(res.at[pl.ds(pl.multiple_of(HALF * ROWS - first_res, HALF * ROWS), HALF * ROWS)], res_v)
     copies[0].wait()
@@ -524,7 +523,7 @@
         scratch_shapes=[
             pltpu.VMEM((4 * ROWS, LANES), jnp.int32),
             pltpu.VMEM((ROWS, LANES), jnp.int32),
-            pltpu.SemaphoreType.DMA((4 + 2 * (2 + FPLANES),)),
+            pltpu.SemaphoreType.DMA((10,)),
         ],
         compiler_params=params(4),
         name="prepare",

time: 71 us -> 70.6 us (level)
  no operation moved by 1% of the time
where the time goes in v11:
time: 70.6 us; the launch traced here: 70.3 us
  starting transfers between devices  34.9 us (49%)
  Pallas kernels  15.8 us (22%)
  waiting for transfers between devices  6.21 us (9%)
  blocking collectives  5.07 us (7%)
  other arithmetic  3.25 us (5%)
  local copies, waits for them, and re-layouts  2.77 us (4%)
  between operations  2.19 us (3%)
    ppermute x6, starting transfers between devices, shift(): return lax.ppermute(value, axis, [(i, (i + step) % n) for i in range(n)])  31.4 us
    pallas_call x1, Pallas kernels, per_device(): pl.pallas_call(adjoint_kernel, out_shape=(jax.ShapeDtypeStruct((2, 4, ROW...  6.96 us
    ppermute x6, waiting for transfers between devices, shift(): return lax.ppermute(value, axis, [(i, (i + step) % n) for i in range(n)])  6.2 us
    all_gather x1, blocking collectives, per_device(): grad = jnp.sum(lax.all_gather(grad, 'vec'), axis=0)  5.07 us
    pallas_call x1, Pallas kernels, per_device(): pl.pallas_call(weights_kernel, out_shape=jax.ShapeDtypeStruct((2, TERMS,...  3.85 us
    ppermute x1, starting transfers between devices, swap_cores(): return lax.ppermute(value, 'vec', [(0, 1), (1, 0), (2, 3), (3, 2)])  3.57 us
    pallas_call x1, Pallas kernels, per_device(): pl.pallas_call(forward_kernel, out_shape=jax.ShapeDtypeStruct((TERMS, 4,...  3.11 us
    mul x1, local copies, waits for them, and re-layouts, per_device(): coefs[:, None, :, None] * jnp.eye(8, dtype=F32)[None, :, None, :]  2.65 us
  transfers between devices with their start and end apart: 7, of which 2 were waited for; matrix products, arithmetic and copies ran while one was open for 8% of the time, Pallas kernels for 11%

profile of v11, /device:TPU:23, one launch (start us, length us, event | category | flops | bytes accessed | tf_op | source)
XLA Modules:
  0.0 70.3 jit_solution(15995456395789608702)
XLA Ops:
  1.3 1.5 %prepare.1 = (f32[928,128]{1,0:T(8,128)S(1)}, f32[928,128]{1,0:T(8,128)S(1)}, f32[512,128]{1,0:T(8,128)S(1)}, f32[256,128]{1,0:T(8,128)S(1)}) custom-call(s32[1]{0:T(128)} %bitcast.1.core, f32[1]{0:T(128)S(6)} %copy.17.scalar, f32[256,128]{1,0:T(8,128)} %bitcast.12, s32[128,128]{1,0:T(8,128)} %bitcast.13, s32[32,128]{1,0:T(8,128)} %pot.1, ...), custom_call_target="tpu_custom_call" | custom-call | tf_op jit(solution)/shard_map/prepare/pallas_call | solution.py:513
  2.8 2.0 %collective-permute-start.1 = (f32[928,128]{1,0:T(8,128)S(1)}, f32[928,128]{1,0:T(8,128)S(1)}, u32[]{:S(2)}, u32[]{:S(2)}) collective-permute-start(f32[928,128]{1,0:T(8,128)S(1)} %get-tuple-element.24), channel_id=1, source_target_pairs={{0,112},{16,0},{32,16},{48,32},{64,48},{80,64},{96,80},{112,96},{1... | collective-permute-start | bytes 1425416 | tf_op jit(solution)/shard_map/ppermute | solution.py:547
  4.7 6.9 %collective-permute-start = (f32[928,128]{1,0:T(8,128)S(1)}, f32[928,128]{1,0:T(8,128)S(1)}, u32[]{:S(2)}, u32[]{:S(2)}) collective-permute-start(f32[928,128]{1,0:T(8,128)S(1)} %get-tuple-element.25.own), channel_id=1, source_target_pairs={{0,16},{16,32},{32,48},{48,64},{64,80},{80,96},{96,112},{112,0},{1... | collective-permute-start | bytes 1425416 | tf_op jit(solution)/shard_map/ppermute | solution.py:547
  12.4 0.7 %sine_multiply_fusion = (f32[16]{0:T(128)S(1)}, f32[16]{0:T(128)S(1)}) fusion(f32[16]{0:T(128)} %param.13), kind=kLoop, calls=%fused_computation.18 | loop fusion | flops 64 | bytes 192 | tf_op jit(solution)/shard_map/mul | solution.py:62
  13.1 0.1 multiply_divide_fusion
  13.3 0.1 fusion.4
  13.4 0.1 maximum_select_fusion.coef
  13.5 1.5 %broadcast_multiply_fusion = f32[32,8,16,8]{3,2,1,0:T(8,128)} fusion(f32[8,8]{1,0:T(8,128)S(1)} %fusion.1, f32[32,16]{1,0:T(8,128)S(1)} %maximum_select_fusion.coef), kind=kLoop, calls=%fused_computation | loop fusion | flops 32768 | bytes 133376 | tf_op jit(solution)/shard_map/mul | solution.py:567
  15.0 2.6 %mul.107 = f32[256,128]{1,0:T(8,128)S(1)} reshape(f32[32,8,16,8]{3,2,1,0:T(8,128)} %broadcast_multiply_fusion) | data formatting | bytes 262144 | tf_op jit(solution)/shard_map/mul | solution.py:567
  17.7 0.2 pack_own.1
  17.9 11.1 %collective-permute-start.2 = (f32[232,128]{1,0:T(8,128)S(1)}, f32[232,128]{1,0:T(8,128)S(1)}, u32[]{:S(2)}, u32[]{:S(2)}) collective-permute-start(f32[232,128]{1,0:T(8,128)S(1)} %get-tuple-element.27), channel_id=1, source_target_pairs={{0,15},{1,0},{2,1},{3,2},{4,3},{5,4},{6,5},{7,6},{8,7},{9,8},{10,9... | collective-permute-start | bytes 356360 | tf_op jit(solution)/shard_map/ppermute | solution.py:547
  29.1 1.9 %collective-permute-start.3 = (f32[232,128]{1,0:T(8,128)S(1)}, f32[232,128]{1,0:T(8,128)S(1)}, u32[]{:S(2)}, u32[]{:S(2)}) collective-permute-start(f32[232,128]{1,0:T(8,128)S(1)} %get-tuple-element.28), channel_id=1, source_target_pairs={{0,1},{1,2},{2,3},{3,4},{4,5},{5,6},{6,7},{7,8},{8,9},{9,10},{10,1... | collective-permute-start | bytes 356360 | tf_op jit(solution)/shard_map/ppermute | solution.py:547
  31.0 3.9 %weights.1.own_weights = f32[2,32,32,128]{3,2,1,0:T(8,128)S(1)} custom-call(f32[32,16]{1,0:T(8,128)S(1)} %maximum_select_fusion.coef, f32[928,128]{1,0:T(8,128)S(1)} %get-tuple-element.25.own, f32[256,128]{1,0:T(8,128)S(1)} %get-tuple-element.30.res_other), custom_call_target="tpu_custom_call" | custom-call | flops 4000000 | bytes 1000000 | tf_op jit(solution)/shard_map/weights/pallas_call | solution.py:575
  34.8 0.0 collective-permute-done.1.below
  34.8 0.0 collective-permute-done.above
  34.8 0.3 pack_edge.1
  35.1 7.5 %collective-permute-start.4 = (f32[328,128]{1,0:T(8,128)S(1)}, f32[328,128]{1,0:T(8,128)S(1)}, u32[]{:S(2)}, u32[]{:S(2)}) collective-permute-start(f32[328,128]{1,0:T(8,128)S(1)} %get-tuple-element.31), channel_id=1, source_target_pairs={{0,15},{1,0},{2,1},{3,2},{4,3},{5,4},{6,5},{7,6},{8,7},{9,8},{10,9... | collective-permute-start | bytes 503816 | tf_op jit(solution)/shard_map/ppermute | solution.py:547
  42.7 1.9 %collective-permute-start.5 = (f32[328,128]{1,0:T(8,128)S(1)}, f32[328,128]{1,0:T(8,128)S(1)}, u32[]{:S(2)}, u32[]{:S(2)}) collective-permute-start(f32[328,128]{1,0:T(8,128)S(1)} %get-tuple-element.32), channel_id=1, source_target_pairs={{0,1},{1,2},{2,3},{3,4},{4,5},{5,6},{6,7},{7,8},{8,9},{9,10},{10,1... | collective-permute-start | bytes 503816 | tf_op jit(solution)/shard_map/ppermute | solution.py:547
  44.6 0.0 collective-permute-done.2.own_right
  44.6 1.2 %collective-permute-done.4.edge_right = f32[328,128]{1,0:T(8,128)S(1)} collective-permute-done((f32[328,128]{1,0:T(8,128)S(1)}, f32[328,128]{1,0:T(8,128)S(1)}, u32[]{:S(2)}, u32[]{:S(2)}) %collective-permute-start.4) | collective-permute-done | bytes 167968 | tf_op jit(solution)/shard_map/ppermute | solution.py:547
  45.8 5.0 %collective-permute-done.5.edge_left = f32[328,128]{1,0:T(8,128)S(1)} collective-permute-done((f32[328,128]{1,0:T(8,128)S(1)}, f32[328,128]{1,0:T(8,128)S(1)}, u32[]{:S(2)}, u32[]{:S(2)}) %collective-permute-start.5) | collective-permute-done | bytes 167968 | tf_op jit(solution)/shard_map/ppermute | solution.py:547
  50.8 0.0 collective-permute-done.3.own_left
  50.9 3.6 %collective-permute-start.6 = (f32[832,128]{1,0:T(8,128)S(1)}, f32[832,128]{1,0:T(8,128)S(1)}, u32[]{:S(2)}, u32[]{:S(2)}) collective-permute-start(f32[832,128]{1,0:T(8,128)S(1)} %slice_dynamic-update-slice_fusion), channel_id=1, source_target_pairs={{0,128},{128,0},{256,384},{384,256},{1,129},{129,1},{257,385},{385... | collective-permute-start | bytes 1277960 | tf_op jit(solution)/shard_map/ppermute | solution.py:550
  54.5 3.1 %forward.1.vs = f32[32,4,32,128]{3,2,1,0:T(8,128)S(1)} custom-call(f32[1]{0:T(128)S(6)} %div.18.scale, f32[928,128]{1,0:T(8,128)S(1)} %get-tuple-element.25.own, f32[512,128]{1,0:T(8,128)S(1)} %get-tuple-element.26.chk, f32[928,128]{1,0:T(8,128)S(1)} %collective-permute-done.above, f32[928,128]{1,0:T(8,128)S(1)} %collective-permute-done.1.below, ...), custom_call_target="tpu_custom_call" | custom-call | flops 20000000 | bytes 6000000 | tf_op jit(solution)/shard_map/forward/pallas_call | solution.py:596
  57.6 0.0 collective-permute-done.6.swapped
  57.6 7.0 %adjoint.1 = (f32[2,4,32,128]{3,2,1,0:T(8,128)}, f32[32,128]{1,0:T(8,128)S(1)}) custom-call(f32[1]{0:T(128)S(6)} %div.18.scale, bf16[256,128]{1,0:T(8,128)(2,1)S(1)} %get-tuple-element.22.high, bf16[256,128]{1,0:T(8,128)(2,1)S(1)} %get-tuple-element.23.low, f32[928,128]{1,0:T(8,128)S(1)} %get-tuple-element.25.own, ...), custom_call_target="tpu_custom_call" | custom-call | tf_op jit(solution)/shard_map/adjoint/pallas_call | solution.py:611
  64.6 5.1 %all-gather = f32[128,128]{1,0:T(8,128)S(1)} all-gather(f32[32,128]{1,0:T(8,128)S(1)} %get-tuple-element.36), channel_id=2, replica_groups=mesh['vec'=4,'row'=8,'col'=16] {'vec'}, dimensions={0}, use_global_device_ids=true | all-gather | bytes 81920 | tf_op jit(solution)/shard_map/all_gather | solution.py:631
  69.7 0.6 reduce_sum.9
  (12 shorter events, 0.1 us)
Async XLA Ops:
  2.8 32.1 %collective-permute-start.1 = (f32[928,128]{1,0:T(8,128)S(1)}, f32[928,128]{1,0:T(8,128)S(1)}, u32[]{:S(2)}, u32[]{:S(2)}) collective-permute-start(f32[928,128]{1,0:T(8,128)S(1)} %get-tuple-element.24), channel_id=1, source_target_pairs={{0,112},{16,0},{32,16},{48,32},{64,48},{80,64},{96,80},{112,96},{1... | collective-permute-start | bytes 1425416 | tf_op jit(solution)/shard_map/ppermute | solution.py:547
  4.7 30.1 %collective-permute-start = (f32[928,128]{1,0:T(8,128)S(1)}, f32[928,128]{1,0:T(8,128)S(1)}, u32[]{:S(2)}, u32[]{:S(2)}) collective-permute-start(f32[928,128]{1,0:T(8,128)S(1)} %get-tuple-element.25.own), channel_id=1, source_target_pairs={{0,16},{16,32},{32,48},{48,64},{64,80},{80,96},{96,112},{112,0},{1... | collective-permute-start | bytes 1425416 | tf_op jit(solution)/shard_map/ppermute | solution.py:547
  17.9 26.7 %collective-permute-start.2 = (f32[232,128]{1,0:T(8,128)S(1)}, f32[232,128]{1,0:T(8,128)S(1)}, u32[]{:S(2)}, u32[]{:S(2)}) collective-permute-start(f32[232,128]{1,0:T(8,128)S(1)} %get-tuple-element.27), channel_id=1, source_target_pairs={{0,15},{1,0},{2,1},{3,2},{4,3},{5,4},{6,5},{7,6},{8,7},{9,8},{10,9... | collective-permute-start | bytes 356360 | tf_op jit(solution)/shard_map/ppermute | solution.py:547
  29.1 21.7 %collective-permute-start.3 = (f32[232,128]{1,0:T(8,128)S(1)}, f32[232,128]{1,0:T(8,128)S(1)}, u32[]{:S(2)}, u32[]{:S(2)}) collective-permute-start(f32[232,128]{1,0:T(8,128)S(1)} %get-tuple-element.28), channel_id=1, source_target_pairs={{0,1},{1,2},{2,3},{3,4},{4,5},{5,6},{6,7},{7,8},{8,9},{9,10},{10,1... | collective-permute-start | bytes 356360 | tf_op jit(solution)/shard_map/ppermute | solution.py:547
  35.1 10.7 %collective-permute-start.4 = (f32[328,128]{1,0:T(8,128)S(1)}, f32[328,128]{1,0:T(8,128)S(1)}, u32[]{:S(2)}, u32[]{:S(2)}) collective-permute-start(f32[328,128]{1,0:T(8,128)S(1)} %get-tuple-element.31), channel_id=1, source_target_pairs={{0,15},{1,0},{2,1},{3,2},{4,3},{5,4},{6,5},{7,6},{8,7},{9,8},{10,9... | collective-permute-start | bytes 503816 | tf_op jit(solution)/shard_map/ppermute | solution.py:547
  42.7 8.1 %collective-permute-start.5 = (f32[328,128]{1,0:T(8,128)S(1)}, f32[328,128]{1,0:T(8,128)S(1)}, u32[]{:S(2)}, u32[]{:S(2)}) collective-permute-start(f32[328,128]{1,0:T(8,128)S(1)} %get-tuple-element.32), channel_id=1, source_target_pairs={{0,1},{1,2},{2,3},{3,4},{4,5},{5,6},{6,7},{7,8},{8,9},{9,10},{10,1... | collective-permute-start | bytes 503816 | tf_op jit(solution)/shard_map/ppermute | solution.py:547
  50.9 6.7 %collective-permute-start.6 = (f32[832,128]{1,0:T(8,128)S(1)}, f32[832,128]{1,0:T(8,128)S(1)}, u32[]{:S(2)}, u32[]{:S(2)}) collective-permute-start(f32[832,128]{1,0:T(8,128)S(1)} %slice_dynamic-update-slice_fusion), channel_id=1, source_target_pairs={{0,128},{128,0},{256,384},{384,256},{1,129},{129,1},{257,385},{385... | collective-permute-start | bytes 1277960 | tf_op jit(solution)/shard_map/ppermute | solution.py:550
